TPU v7x, 32 devices: a whole 2x2x4 slice. The times are simulated.
32 devices in a mesh: row: 16 (over z, y, x), col: 2 (over core).
Axes of the slice: x: 2, y: 2, z: 4, core: 2. Of those that a mesh axis runs over, the one named last changes fastest.
Arguments:
- object_field: float32 [2, 8192, 1024], P(None, 'row', 'col'), may hold values from -13 to 13
- probe_modes: float32 [2, 2, 256, 256], replicated, may hold values from -5 to 5
- scan_offsets: int32 [16, 2, 2, 6], P('row', 'col'), may hold values from 0 to 7936, as said below
- scan_counts: int32 [16, 2], P('row', 'col'), may hold values from 1 to 6, as said below
- amplitudes: bfloat16 [16, 2, 6, 256, 256], P('row', 'col'), may hold values from 0 to 2.5
Outputs:
- object_new: float32 [2, 8192, 1024], P(None, 'row', 'col')
- probe_new: float32 [2, 2, 256, 256], replicated
Inputs may be any that keep to these rules, and one draw needn't show every extreme that they name: `scan_counts`: some tile has exactly 6 live positions. `scan_offsets`: each patch of 256 x 256 pixels lies inside the object, and its centre (top-left plus 256 // 2 in each direction) lies in the slot's own tile.
All inputs are finite; a program needn't handle non-finite values.
Results may differ from a plain program's by a relative error of at most 0.0003.
Values sent between devices are 32-bit elements; how exact they have to be, the bound alone decides.
No kernel may reach another device: no remote copies, remote signals or barrier semaphores. Data moves between devices by JAX's collectives and lax.ppermute only.
A program may use at most 64 MiB of HBM per device.

v0:
```python
import math

import jax
import jax.numpy as jnp
from jax import lax
from jax.sharding import PartitionSpec as P

HIGHEST = lax.Precision.HIGHEST


def extended_2(cells, sides, width):
    for axis, dim in sides:
        count = lax.axis_size(axis)
        ends = count - 1
        head = lax.slice_in_dim(cells, 0, width, axis=dim)
        tail = lax.slice_in_dim(cells, cells.shape[dim] - width, cells.shape[dim], axis=dim)
        cells = jnp.concatenate(
            [
                lax.ppermute(tail, axis, [(i, (i + 1) % count) for i in range(ends)]),
                cells,
                lax.ppermute(head, axis, [((i + 1) % count, i) for i in range(ends)]),
            ],
            axis=dim,
        )
    return cells


def dft_tables(edge_size):
    counter = jnp.arange(edge_size, dtype=jnp.int32)
    phases = counter[:, None] * counter[None, :] % edge_size
    angles = phases.astype(jnp.float32) * (2.0 * math.pi / edge_size)
    return jnp.concatenate([jnp.cos(angles), jnp.sin(angles)], axis=1)


def combine_parts(cosine_real, cosine_imag, sine_real, sine_imag, inverse):
    if inverse:
        return (cosine_real - sine_imag, cosine_imag + sine_real)
    return (cosine_real + sine_imag, cosine_imag - sine_real)


def transform(real_part, imag_part, table_pair, inverse):
    mode_count = real_part.shape[0]
    edge_size = real_part.shape[-1]
    stacked = jnp.concatenate([real_part, imag_part], axis=0)
    right_pass = jnp.einsum("bij,jk->bik", stacked, table_pair, precision=HIGHEST)
    first_real, first_imag = combine_parts(
        right_pass[:mode_count, :, :edge_size],
        right_pass[mode_count:, :, :edge_size],
        right_pass[:mode_count, :, edge_size:],
        right_pass[mode_count:, :, edge_size:],
        inverse,
    )
    stacked = jnp.concatenate([first_real, first_imag], axis=0)
    left_pass = jnp.einsum("jk,bji->bki", table_pair, stacked, precision=HIGHEST)
    second_real, second_imag = combine_parts(
        left_pass[:mode_count, :edge_size],
        left_pass[mode_count:, :edge_size],
        left_pass[:mode_count, edge_size:],
        left_pass[mode_count:, edge_size:],
        inverse,
    )
    return (second_real / edge_size, second_imag / edge_size)


def fold_rims(padded, tile_rows, tile_cols, margin):
    low = 2 * margin
    row_end = tile_rows + 3 * margin
    col_end = tile_cols + 3 * margin
    inner = padded[:, low : low + tile_rows, low : low + tile_cols]
    inner = inner.at[:, :margin, :].add(padded[:, :margin, low : low + tile_cols])
    inner = inner.at[:, tile_rows - margin :, :].add(padded[:, row_end:, low : low + tile_cols])
    inner = inner.at[:, :, :margin].add(padded[:, low : low + tile_rows, :margin])
    inner = inner.at[:, :, tile_cols - margin :].add(padded[:, low : low + tile_rows, col_end:])
    inner = inner.at[:, :margin, :margin].add(padded[:, :margin, :margin])
    inner = inner.at[:, :margin, tile_cols - margin :].add(padded[:, :margin, col_end:])
    inner = inner.at[:, tile_rows - margin :, :margin].add(padded[:, row_end:, :margin])
    inner = inner.at[:, tile_rows - margin :, tile_cols - margin :].add(
        padded[:, row_end:, col_end:]
    )
    return inner


def on_device(object_field, probe_modes, scan_offsets, scan_counts, amplitudes):
    tile_rows = object_field.shape[1]
    tile_cols = object_field.shape[2]
    mode_count = probe_modes.shape[1]
    edge_size = probe_modes.shape[-1]
    margin = edge_size // 2
    anchor_row = lax.axis_index("row") * tile_rows
    anchor_col = lax.axis_index("col") * tile_cols
    extended = extended_2(object_field, (("row", 1), ("col", 2)), margin)
    table_pair = dft_tables(edge_size)
    probe_real = probe_modes[0]
    probe_imag = probe_modes[1]
    probe_power = jnp.sum(probe_real * probe_real + probe_imag * probe_imag, axis=0)
    live_count = scan_counts[0, 0]

    def slot_terms(position):
        row_start = scan_offsets[0, 0, 0, position] - anchor_row + margin
        col_start = scan_offsets[0, 0, 1, position] - anchor_col + margin
        patch_field = lax.dynamic_slice(
            extended, (0, row_start, col_start), (2, edge_size, edge_size)
        )
        patch_real = patch_field[0]
        patch_imag = patch_field[1]
        wave_real = probe_real * patch_real - probe_imag * patch_imag
        wave_imag = probe_real * patch_imag + probe_imag * patch_real
        far_real, far_imag = transform(wave_real, wave_imag, table_pair, False)
        intensity = jnp.sum(far_real * far_real + far_imag * far_imag, axis=0)
        factor = (
            amplitudes[0, 0, position].astype(jnp.float32) / jnp.sqrt(jnp.maximum(intensity, 0.25))
            - 1.0
        )
        back_real, back_imag = transform(far_real * factor, far_imag * factor, table_pair, True)
        update = jnp.stack(
            [
                jnp.sum(probe_real * back_real + probe_imag * back_imag, axis=0),
                jnp.sum(probe_real * back_imag - probe_imag * back_real, axis=0),
            ]
        )
        probe_term = jnp.stack(
            [
                patch_real * back_real + patch_imag * back_imag,
                patch_real * back_imag - patch_imag * back_real,
            ]
        )
        power_term = patch_real * patch_real + patch_imag * patch_imag
        return (row_start, col_start, update, probe_term, power_term)

    def add_window(canvas, values, row_start, col_start):
        window = lax.dynamic_slice(canvas, (0, row_start, col_start), values.shape)
        return lax.dynamic_update_slice(canvas, window + values, (0, row_start, col_start))

    gradient = jnp.zeros((2, tile_rows + edge_size, tile_cols + edge_size), jnp.float32)
    probe_grad = jnp.zeros((2, mode_count, edge_size, edge_size), jnp.float32)
    probe_norm = jnp.zeros((edge_size, edge_size), jnp.float32)

    def visit_lit(position, state_tuple):
        gradient_now, lighting_now, grad_now, norm_now = state_tuple
        row_start, col_start, update, probe_term, power_term = slot_terms(position)
        gradient_now = add_window(gradient_now, update, row_start, col_start)
        lighting_now = add_window(lighting_now, probe_power[None], row_start, col_start)
        return (gradient_now, lighting_now, grad_now + probe_term, norm_now + power_term)

    lighting = jnp.zeros((1, tile_rows + edge_size, tile_cols + edge_size), jnp.float32)
    gradient, lighting, probe_grad, probe_norm = lax.fori_loop(
        0, live_count, visit_lit, (gradient, lighting, probe_grad, probe_norm)
    )
    stacked = jnp.concatenate([gradient, lighting], axis=0)
    padded = extended_2(stacked, (("row", 1), ("col", 2)), margin)
    folded = fold_rims(padded, tile_rows, tile_cols, margin)
    object_grad = folded[:2]
    lighting_sum = folded[2]
    object_new = object_field + object_grad / (lighting_sum + 1.0)[None]
    total_grad, total_norm = lax.psum((probe_grad, probe_norm), ("row", "col"))
    probe_new = probe_modes + total_grad / (total_norm + 1.0)
    return (object_new, probe_new)


def solution(mesh):
    in_specs = (
        P(None, "row", "col"),
        P(),
        P("row", "col", None, None),
        P("row", "col"),
        P("row", "col", None, None, None),
    )
    out_specs = (P(None, "row", "col"), P())
    return jax.shard_map(
        on_device, mesh=mesh, in_specs=in_specs, out_specs=out_specs, check_vma=False
    )
```

profile of v0, /device:TPU:0, one launch (start us, length us, event | category | flops | bytes accessed | tf_op | source)
XLA Modules:
  0.0 479.1 jit_solution(10610719921189110495)
XLA Ops:
  9.2 4.9 %collective-permute-start = (f32[2,128,512]{1,2,0:T(8,128)S(1)}, f32[2,128,512]{1,2,0:T(8,128)S(1)}, u32[]{:S(2)}, u32[]{:S(2)}) collective-permute-start(f32[2,128,512]{1,2,0:T(8,128)S(1)} %get-tuple-element.468), channel_id=1, source_target_pairs={{0,2},{2,4},{4,6},{6,8},{8,10},{10,12},{12,14},{14,16},{16,18},{18... | collective-permute-start | bytes 1572872 | tf_op jit(solution)/shard_map/ppermute | solution.py:19
  15.4 21.1 %collective-permute-done = f32[2,128,512]{1,2,0:T(8,128)S(1)} collective-permute-done((f32[2,128,512]{1,2,0:T(8,128)S(1)}, f32[2,128,512]{1,2,0:T(8,128)S(1)}, u32[]{:S(2)}, u32[]{:S(2)}) %collective-permute-start) | collective-permute-done | bytes 524320 | tf_op jit(solution)/shard_map/ppermute | solution.py:19
  39.8 2.3 collective-permute-start.2
  46.9 3.5 pad_maximum_fusion
  50.3 2.5 broadcast_in_dim.25.clone
  56.1 211.3 %while.27 = (s32[]{:T(128)}, f32[2,768,768]{2,1,0:T(8,128)}, f32[1,768,768]{2,1,0:T(8,128)}, f32[2,2,256,256]{3,2,1,0:T(8,128)}, f32[256,256]{0,1:T(8,128)}, /*i...) while((s32[]{:T(128)}, f32[2,768,768]{2,1,0:T(8,128)}, ...), condition=%wide.region_5.6_spmd, body=%wide.region_1.5_spmd.sunk | while | flops 6450118656 | bytes 70124120 | solution.py:146
  62.0 2.3 multiply_subtract_fusion.2
  78.3 3.0 add_reduce_fusion.6
  87.0 6.8 %dynamic_update_slice.16 = f32[2,768,768]{2,1,0:T(8,128)} dynamic-update-slice(f32[2,768,768]{2,1,0:T(8,128)} %get-tuple-element.634, f32[2,256,256]{2,1,0:T(8,128)S(1)} %copy.76, s32[]{:T(128)} %constant.306.clone.1..sunk, s32[]{:T(128)S(6)} %select_n.54, s32[]{:T(128)S(6)} %select_n.55) | dynamic-update-slice | bytes 1048580 | tf_op jit(solution)/shard_map/while/body/dynamic_update_slice | solution.py:132
  94.9 3.9 dynamic_update_slice.17
  104.6 2.3 multiply_subtract_fusion.2
  120.8 3.0 add_reduce_fusion.6
  129.5 6.0 %dynamic_update_slice.16 = f32[2,768,768]{2,1,0:T(8,128)} dynamic-update-slice(f32[2,768,768]{2,1,0:T(8,128)} %get-tuple-element.634, f32[2,256,256]{2,1,0:T(8,128)S(1)} %copy.76, s32[]{:T(128)} %constant.306.clone.1..sunk, s32[]{:T(128)S(6)} %select_n.54, s32[]{:T(128)S(6)} %select_n.55) | dynamic-update-slice | bytes 1048580 | tf_op jit(solution)/shard_map/while/body/dynamic_update_slice | solution.py:132
  136.6 3.5 dynamic_update_slice.17
  162.2 3.0 add_reduce_fusion.6
  170.9 6.8 %dynamic_update_slice.16 = f32[2,768,768]{2,1,0:T(8,128)} dynamic-update-slice(f32[2,768,768]{2,1,0:T(8,128)} %get-tuple-element.634, f32[2,256,256]{2,1,0:T(8,128)S(1)} %copy.76, s32[]{:T(128)} %constant.306.clone.1..sunk, s32[]{:T(128)S(6)} %select_n.54, s32[]{:T(128)S(6)} %select_n.55) | dynamic-update-slice | bytes 1048580 | tf_op jit(solution)/shard_map/while/body/dynamic_update_slice | solution.py:132
  178.8 3.9 dynamic_update_slice.17
  204.7 3.0 add_reduce_fusion.6
  213.4 6.8 %dynamic_update_slice.16 = f32[2,768,768]{2,1,0:T(8,128)} dynamic-update-slice(f32[2,768,768]{2,1,0:T(8,128)} %get-tuple-element.634, f32[2,256,256]{2,1,0:T(8,128)S(1)} %copy.76, s32[]{:T(128)} %constant.306.clone.1..sunk, s32[]{:T(128)S(6)} %select_n.54, s32[]{:T(128)S(6)} %select_n.55) | dynamic-update-slice | bytes 1048580 | tf_op jit(solution)/shard_map/while/body/dynamic_update_slice | solution.py:132
  221.3 3.9 dynamic_update_slice.17
  247.3 3.0 add_reduce_fusion.6
  255.9 5.9 %dynamic_update_slice.16 = f32[2,768,768]{2,1,0:T(8,128)} dynamic-update-slice(f32[2,768,768]{2,1,0:T(8,128)} %get-tuple-element.634, f32[2,256,256]{2,1,0:T(8,128)S(1)} %copy.76, s32[]{:T(128)} %constant.306.clone.1..sunk, s32[]{:T(128)S(6)} %select_n.54, s32[]{:T(128)S(6)} %select_n.55) | dynamic-update-slice | bytes 1048580 | tf_op jit(solution)/shard_map/while/body/dynamic_update_slice | solution.py:132
  263.0 3.6 dynamic_update_slice.17
  267.5 2.8 constant_dynamic-update-slice_fusion.1
  270.7 2.9 copy-done.6
  277.5 37.5 %collective-permute-done.4 = f32[3,128,768]{2,1,0:T(8,128)S(1)} collective-permute-done((f32[3,128,768]{2,1,0:T(8,128)}, f32[3,128,768]{2,1,0:T(8,128)S(1)}, u32[]{:S(2)}, u32[]{:S(2)}) %collective-permute-start.4) | collective-permute-done | bytes 1179680 | tf_op jit(solution)/shard_map/ppermute | solution.py:19
  315.1 4.4 pad_maximum_fusion.1
  319.4 37.9 %collective-permute-start.6 = (f32[3,1024,128]{2,1,0:T(8,128)}, f32[3,1024,128]{2,1,0:T(8,128)}, u32[]{:S(2)}, u32[]{:S(2)}) collective-permute-start(f32[3,1024,128]{2,1,0:T(8,128)} %get-tuple-element.463), channel_id=1, source_target_pairs={{0,1},{2,3},{4,5},{6,7},{8,9},{10,11},{12,13},{14,15},{16,17},{18,... | collective-permute-start | bytes 4718600 | tf_op jit(solution)/shard_map/ppermute | solution.py:19
  362.2 90.4 %all-reduce.3.cloned.1.call-done = (f32[2,2,256,256]{3,2,1,0:T(8,128)}, f32[256,256]{0,1:T(8,128)}) async-done(((f32[2,2,256,256]{3,2,1,0:T(8,128)}, f32[256,256]{0,1:T(8,128)}), (f32[2,2,256,256]{3,2,1,0:T(8,128)}, f32[256,256]{0,1:T(8,128)})) %all-reduce.3.cloned.1.call-update) | async-done | bytes 1310736 | tf_op jit(solution)/shard_map/psum | solution.py:155
  454.4 2.9 divide_add_fusion
  462.4 3.0 add_select_fusion.1
  465.4 2.6 scatter-add.35
  (274 shorter events, 164.0 us)
Async XLA Ops:
  7.2 445.5 %all-reduce.3.cloned.1.call-start = ((), (), s32[]{:S(2)}) async-start(), calls=%async_computation | async-start | bytes 2621440 | tf_op jit(solution)/shard_map/psum | solution.py:155
  9.1 30.6 %copy-start.7 = (f32[2,512,512]{1,2,0:T(8,128)}, f32[2,512,512]{1,2,0:T(8,128)S(1)}, u32[]{:S(2)}) copy-start(f32[2,512,512]{1,2,0:T(8,128)S(1)} %copy.47) | copy-start | bytes 6291460
  9.2 27.3 %collective-permute-start = (f32[2,128,512]{1,2,0:T(8,128)S(1)}, f32[2,128,512]{1,2,0:T(8,128)S(1)}, u32[]{:S(2)}, u32[]{:S(2)}) collective-permute-start(f32[2,128,512]{1,2,0:T(8,128)S(1)} %get-tuple-element.468), channel_id=1, source_target_pairs={{0,2},{2,4},{4,6},{6,8},{8,10},{10,12},{12,14},{14,16},{16,18},{18... | collective-permute-start | bytes 1572872 | tf_op jit(solution)/shard_map/ppermute | solution.py:19
  14.1 24.3 %collective-permute-start.1 = (f32[2,128,512]{1,2,0:T(8,128)S(1)}, f32[2,128,512]{1,2,0:T(8,128)S(1)}, u32[]{:S(2)}, u32[]{:S(2)}) collective-permute-start(f32[2,128,512]{1,2,0:T(8,128)S(1)} %get-tuple-element.469), channel_id=1, source_target_pairs={{2,0},{4,2},{6,4},{8,6},{10,8},{12,10},{14,12},{16,14},{18,16},{20... | collective-permute-start | bytes 1572872 | tf_op jit(solution)/shard_map/ppermute | solution.py:21
  36.5 3.3 copy-start.17
  39.8 6.9 %copy-start.10 = (f32[2,2,256,256]{3,2,1,0:T(8,128)S(1)}, f32[2,2,256,256]{3,2,1,0:T(8,128)}, u32[]{:S(2)}) copy-start(f32[2,2,256,256]{3,2,1,0:T(8,128)} %param.24) | copy-start | bytes 3145732
  39.8 7.0 %collective-permute-start.2 = (f32[2,768,128]{1,2,0:T(8,128)}, f32[2,768,128]{1,2,0:T(8,128)}, u32[]{:S(2)}, u32[]{:S(2)}) collective-permute-start(f32[2,768,128]{1,2,0:T(8,128)} %get-tuple-element.466), channel_id=1, source_target_pairs={{0,1},{2,3},{4,5},{6,7},{8,9},{10,11},{12,13},{14,15},{16,17},{18,... | collective-permute-start | bytes 2359304 | tf_op jit(solution)/shard_map/ppermute | solution.py:19
  42.1 4.7 collective-permute-start.3
  52.8 3.3 copy-start.21
  57.0 7.3 %copy-start = (f32[2,256,256]{2,1,0:T(8,128)}, f32[2,256,256]{2,1,0:T(8,128)S(1)}, u32[]{:S(2)}) copy-start(f32[2,256,256]{2,1,0:T(8,128)S(1)} %get-tuple-element.664) | copy-start | bytes 1572868 | tf_op jit(solution)/shard_map/while
  85.5 8.3 %copy-start.11 = (f32[256,256]{1,0:T(8,128)S(1)}, f32[256,256]{1,0:T(8,128)}, u32[]{:S(2)}) copy-start(f32[256,256]{1,0:T(8,128)} %get-tuple-element.668) | copy-start | bytes 786436 | tf_op jit(solution)/shard_map/while
  85.7 13.1 %copy-start.2 = (f32[2,256,256]{2,1,0:T(8,128)S(1)}, f32[2,256,256]{2,1,0:T(8,128)}, u32[]{:S(2)}) copy-start(f32[2,256,256]{2,1,0:T(8,128)} %copy-done) | copy-start | bytes 1572868 | tf_op jit(solution)/shard_map/while
  99.5 7.3 %copy-start = (f32[2,256,256]{2,1,0:T(8,128)}, f32[2,256,256]{2,1,0:T(8,128)S(1)}, u32[]{:S(2)}) copy-start(f32[2,256,256]{2,1,0:T(8,128)S(1)} %get-tuple-element.664) | copy-start | bytes 1572868 | tf_op jit(solution)/shard_map/while
  128.0 7.5 %copy-start.11 = (f32[256,256]{1,0:T(8,128)S(1)}, f32[256,256]{1,0:T(8,128)}, u32[]{:S(2)}) copy-start(f32[256,256]{1,0:T(8,128)} %get-tuple-element.668) | copy-start | bytes 786436 | tf_op jit(solution)/shard_map/while
  128.2 11.9 %copy-start.2 = (f32[2,256,256]{2,1,0:T(8,128)S(1)}, f32[2,256,256]{2,1,0:T(8,128)}, u32[]{:S(2)}) copy-start(f32[2,256,256]{2,1,0:T(8,128)} %copy-done) | copy-start | bytes 1572868 | tf_op jit(solution)/shard_map/while
  140.8 7.3 %copy-start = (f32[2,256,256]{2,1,0:T(8,128)}, f32[2,256,256]{2,1,0:T(8,128)S(1)}, u32[]{:S(2)}) copy-start(f32[2,256,256]{2,1,0:T(8,128)S(1)} %get-tuple-element.664) | copy-start | bytes 1572868 | tf_op jit(solution)/shard_map/while
  169.4 8.3 %copy-start.11 = (f32[256,256]{1,0:T(8,128)S(1)}, f32[256,256]{1,0:T(8,128)}, u32[]{:S(2)}) copy-start(f32[256,256]{1,0:T(8,128)} %get-tuple-element.668) | copy-start | bytes 786436 | tf_op jit(solution)/shard_map/while
  169.6 13.1 %copy-start.2 = (f32[2,256,256]{2,1,0:T(8,128)S(1)}, f32[2,256,256]{2,1,0:T(8,128)}, u32[]{:S(2)}) copy-start(f32[2,256,256]{2,1,0:T(8,128)} %copy-done) | copy-start | bytes 1572868 | tf_op jit(solution)/shard_map/while
  183.3 7.3 %copy-start = (f32[2,256,256]{2,1,0:T(8,128)}, f32[2,256,256]{2,1,0:T(8,128)S(1)}, u32[]{:S(2)}) copy-start(f32[2,256,256]{2,1,0:T(8,128)S(1)} %get-tuple-element.664) | copy-start | bytes 1572868 | tf_op jit(solution)/shard_map/while
  211.9 8.3 %copy-start.11 = (f32[256,256]{1,0:T(8,128)S(1)}, f32[256,256]{1,0:T(8,128)}, u32[]{:S(2)}) copy-start(f32[256,256]{1,0:T(8,128)} %get-tuple-element.668) | copy-start | bytes 786436 | tf_op jit(solution)/shard_map/while
  212.1 13.1 %copy-start.2 = (f32[2,256,256]{2,1,0:T(8,128)S(1)}, f32[2,256,256]{2,1,0:T(8,128)}, u32[]{:S(2)}) copy-start(f32[2,256,256]{2,1,0:T(8,128)} %copy-done) | copy-start | bytes 1572868 | tf_op jit(solution)/shard_map/while
  225.9 7.3 %copy-start = (f32[2,256,256]{2,1,0:T(8,128)}, f32[2,256,256]{2,1,0:T(8,128)S(1)}, u32[]{:S(2)}) copy-start(f32[2,256,256]{2,1,0:T(8,128)S(1)} %get-tuple-element.664) | copy-start | bytes 1572868 | tf_op jit(solution)/shard_map/while
  254.4 7.4 %copy-start.11 = (f32[256,256]{1,0:T(8,128)S(1)}, f32[256,256]{1,0:T(8,128)}, u32[]{:S(2)}) copy-start(f32[256,256]{1,0:T(8,128)} %get-tuple-element.668) | copy-start | bytes 786436 | tf_op jit(solution)/shard_map/while
  254.6 11.9 %copy-start.2 = (f32[2,256,256]{2,1,0:T(8,128)S(1)}, f32[2,256,256]{2,1,0:T(8,128)}, u32[]{:S(2)}) copy-start(f32[2,256,256]{2,1,0:T(8,128)} %copy-done) | copy-start | bytes 1572868 | tf_op jit(solution)/shard_map/while
  274.8 40.2 %collective-permute-start.4 = (f32[3,128,768]{2,1,0:T(8,128)}, f32[3,128,768]{2,1,0:T(8,128)S(1)}, u32[]{:S(2)}, u32[]{:S(2)}) collective-permute-start(f32[3,128,768]{2,1,0:T(8,128)} %get-tuple-element.465), channel_id=1, source_target_pairs={{0,2},{2,4},{4,6},{6,8},{8,10},{10,12},{12,14},{14,16},{16,18},{18... | collective-permute-start | bytes 3538952 | tf_op jit(solution)/shard_map/ppermute | solution.py:19
  276.2 38.9 %collective-permute-start.5 = (f32[3,128,768]{2,1,0:T(8,128)S(1)}, f32[3,128,768]{2,1,0:T(8,128)S(1)}, u32[]{:S(2)}, u32[]{:S(2)}) collective-permute-start(f32[3,128,768]{2,1,0:T(8,128)S(1)} %get-tuple-element.464), channel_id=1, source_target_pairs={{2,0},{4,2},{6,4},{8,6},{10,8},{12,10},{14,12},{16,14},{18,16},{20... | collective-permute-start | bytes 3538952 | tf_op jit(solution)/shard_map/ppermute | solution.py:21
  277.5 81.7 %copy-start.22 = (s32[3]{0:T(128)S(1)}, s32[3]{0:T(128)}, u32[]{:S(2)}) copy-start(s32[3]{0:T(128)} %constant.316.clone.1) | copy-start | bytes 40
  315.0 4.4 copy-start.13
  315.1 4.4 copy-start.15
  319.4 139.3 %collective-permute-start.6 = (f32[3,1024,128]{2,1,0:T(8,128)}, f32[3,1024,128]{2,1,0:T(8,128)}, u32[]{:S(2)}, u32[]{:S(2)}) collective-permute-start(f32[3,1024,128]{2,1,0:T(8,128)} %get-tuple-element.463), channel_id=1, source_target_pairs={{0,1},{2,3},{4,5},{6,7},{8,9},{10,11},{12,13},{14,15},{16,17},{18,... | collective-permute-start | bytes 4718600 | tf_op jit(solution)/shard_map/ppermute | solution.py:19
  357.3 102.8 %collective-permute-start.7 = (f32[3,1024,128]{2,1,0:T(8,128)}, f32[3,1024,128]{2,1,0:T(8,128)}, u32[]{:S(2)}, u32[]{:S(2)}) collective-permute-start(f32[3,1024,128]{2,1,0:T(8,128)} %get-tuple-element.462), channel_id=1, source_target_pairs={{1,0},{3,2},{5,4},{7,6},{9,8},{11,10},{13,12},{15,14},{17,16},{19,... | collective-permute-start | bytes 4718600 | tf_op jit(solution)/shard_map/ppermute | solution.py:21
  454.4 4.1 copy-start.16
  (28 other events, 59.1 us)
Sparse Core Ops, SparseCore 0:
  277.6 174.9 all-reduce.2
where the time goes:
time: 484 us; the launch traced here: 479 us
  waiting for transfers between devices  151 us (31%)
  local copies, waits for them, and re-layouts  112 us (23%)
  other arithmetic  102 us (21%)
  starting transfers between devices  51.7 us (11%)
  matrix products  36.7 us (8%)
  between operations  14.3 us (3%)
  loops' own time  11.8 us (2%)
    psum x1, waiting for transfers between devices, on_device(): total_grad, total_norm = lax.psum((probe_grad, probe_norm), ('row', 'col'))  90.4 us
    ppermute x4, waiting for transfers between devices, extended_2(): lax.ppermute(tail, axis, [(i, (i + 1) % count) for i in range(ends)])  58.6 us
    dynamic_update_slice x15, local copies, waits for them, and re-layouts, add_window(): lax.dynamic_update_slice(canvas, window + values, (0, row_start, col_start))  52 us
    ppermute x4, starting transfers between devices, extended_2(): lax.ppermute(tail, axis, [(i, (i + 1) % count) for i in range(ends)])  46.5 us
    dot_general x10, matrix products, transform(): jnp.einsum('jk,bji->bki', table_pair, stacked, precision=HIGHEST)  18.4 us
    dot_general x10, matrix products, transform(): jnp.einsum('bij,jk->bik', stacked, table_pair, precision=HIGHEST)  18.3 us
    another operation x21, local copies, waits for them, and re-layouts  16.9 us
    reduce_sum x5, other arithmetic, slot_terms(): jnp.sum(probe_real * back_real + probe_imag * back_imag, axis=0)  14.8 us
  transfers between devices with their start and end apart: 9, of which 4 were waited for; matrix products, arithmetic and copies ran while one was open for 4% of the time, Pallas kernels for 0%

commit v1 on v0

v1 whole, which is shorter than its diff:
```python
import functools
import math

import jax
import jax.numpy as jnp
import numpy as np
from jax import lax
from jax.experimental import pallas as pl
from jax.experimental.pallas import tpu as pltpu
from jax.sharding import PartitionSpec as P

F32 = jnp.float32
BF16 = jnp.bfloat16
LANES = 128


def split_host(table):
    high = table.astype(BF16)
    low = (table - high.astype(np.float64)).astype(BF16)
    return high, low


def dft_tables(edge):
    half = edge // 2
    scale = 1.0 / math.sqrt(edge)
    n = np.arange(half)[:, None]
    k = np.arange(half)[None, :]
    right, left = [], []
    for parity in (0, 1):
        angle = (n * (2 * k + parity) % edge) * (2.0 * np.pi / edge)
        cosine, sine = np.cos(angle) * scale, np.sin(angle) * scale
        w = np.block([[cosine, -sine], [sine, cosine]])
        right.append(w)
        left.append(w.T)
    mats = [right[0], right[1], left[0], left[1]]
    as_right = []
    as_left = []
    for m in mats:
        high, low = split_host(m)
        as_right.append(np.concatenate([high, high, low], axis=0))
        as_left.append(np.concatenate([high, high, low], axis=1))
    return (
        np.stack([as_right[0], as_right[1], as_right[2], as_right[3]]),
        np.stack([as_left[2], as_left[3], as_left[0], as_left[1]]),
    )


def split_parts(x):
    high = x.astype(BF16)
    low = (x - high.astype(F32)).astype(BF16)
    return high, low


def right_dot(x, table):
    high, low = split_parts(x)
    return jnp.dot(jnp.concatenate([high, low, high], axis=1), table, preferred_element_type=F32)


def left_dot(table, x):
    high, low = split_parts(x)
    return jnp.dot(table, jnp.concatenate([high, low, high], axis=0), preferred_element_type=F32)


def slots_kernel(
    phase,
    geometry,
    meta,
    tile,
    left,
    right,
    top,
    bottom,
    probe,
    amps,
    rights,
    lefts,
    probe_in,
    *refs,
):
    tile_rows, tile_cols, margin, edge, modes = geometry
    tiles = tile_cols // LANES
    side = margin // LANES
    half = edge // 2
    outs, scratch = refs[:-4], refs[-4:]
    ext, acc, amp_buf, sems = scratch
    if phase == 0:
        mid_out, left_out, right_out, lit_mid, lit_top, lit_bottom, lit_left, lit_right, probe_out = outs
    else:
        mid_out, top_out, bottom_out, left_out, right_out, probe_out = outs
    count = meta[2, 0]

    loads = []

    def load(src, dst):
        copy = pltpu.make_async_copy(src, dst, sems.at[len(loads)])
        copy.start()
        loads.append(copy)

    body = pl.ds(margin, tile_rows)
    for t in range(tiles):
        load(tile.at[:, :, pl.ds(t * LANES, LANES)], ext.at[side + t, :, body, :])
    if phase == 0:
        load(left, ext.at[0, :, body, :])
        load(right, ext.at[side + tiles, :, body, :])
    else:
        load(left, ext.at[0])
        load(right, ext.at[side + tiles])
        for t in range(tiles):
            load(top.at[:, :, pl.ds(t * LANES, LANES)], ext.at[side + t, :, pl.ds(0, margin), :])
            load(
                bottom.at[:, :, pl.ds(t * LANES, LANES)],
                ext.at[side + t, :, pl.ds(margin + tile_rows, margin), :],
            )
    acc[...] = jnp.zeros_like(acc)
    probe_out[...] = probe_in[...]
    for copy in loads:
        copy.wait()

    lane = lax.broadcasted_iota(jnp.int32, (edge, LANES), 1)
    power = [
        sum(
            probe[c, k, :, pl.ds(t * LANES, LANES)] * probe[c, k, :, pl.ds(t * LANES, LANES)]
            for c in range(2)
            for k in range(modes)
        )
        for t in range(2)
    ] if phase == 0 else None

    def add_window(channel, parts, row, block, shift):
        keep = lane >= shift
        first = pltpu.roll(parts[0], shift, 1)
        second = pltpu.roll(parts[1], shift, 1)
        rows = pl.ds(row, edge)
        zero = jnp.zeros_like(first)
        acc[block, channel, rows, :] += jnp.where(keep, first, zero)
        acc[block + 1, channel, rows, :] += jnp.where(keep, second, first)
        acc[block + 2, channel, rows, :] += jnp.where(keep, zero, second)

    def visit(slot, carry):
        row = meta[0, slot]
        col = meta[1, slot]
        block = col // LANES
        shift = col - block * LANES
        interior = jnp.logical_and(row >= margin, row + edge <= margin + tile_rows)
        chosen = interior if phase == 0 else jnp.logical_not(interior)

        if phase == 0:
            add_window(2, power, row, block, shift)

        @pl.when(chosen)
        def _():
            fetch = pltpu.make_async_copy(amps.at[slot], amp_buf, sems.at[len(loads)])
            fetch.start()
            back_shift = lax.rem(LANES - shift, LANES)
            keep = lane < LANES - shift
            patch = []
            for c in range(2):
                rolled = [
                    pltpu.roll(ext[block + t, c, pl.ds(row, edge), :], back_shift, 1)
                    for t in range(3)
                ]
                patch.append([jnp.where(keep, rolled[t], rolled[t + 1]) for t in range(2)])

            def probe_at(c, k, t):
                return probe[c, k, :, pl.ds(t * LANES, LANES)]

            evens, odds = [], []
            for k in range(modes):
                re = [probe_at(0, k, t) * patch[0][t] - probe_at(1, k, t) * patch[1][t] for t in range(2)]
                im = [probe_at(0, k, t) * patch[1][t] + probe_at(1, k, t) * patch[0][t] for t in range(2)]
                even = right_dot(jnp.concatenate([re[0] + re[1], im[0] + im[1]], axis=1), rights[0])
                odd = right_dot(jnp.concatenate([re[0] - re[1], im[0] - im[1]], axis=1), rights[1])
                evens.append(even)
                odds.append(odd)
            far = []
            for k in range(modes):
                re = jnp.concatenate([evens[k][:, :half], odds[k][:, :half]], axis=1)
                im = jnp.concatenate([evens[k][:, half:], odds[k][:, half:]], axis=1)
                far.append(
                    [
                        left_dot(
                            lefts[0],
                            jnp.concatenate([re[:half] + re[half:], im[:half] + im[half:]], axis=0),
                        ),
                        left_dot(
                            lefts[1],
                            jnp.concatenate([re[:half] - re[half:], im[:half] - im[half:]], axis=0),
                        ),
                    ]
                )
            fetch.wait()
            factor = []
            for p in range(2):
                total = sum(
                    far[k][p][:half] * far[k][p][:half] + far[k][p][half:] * far[k][p][half:]
                    for k in range(modes)
                )
                amp = amp_buf[pl.ds(p * half, half), :].astype(F32)
                one = amp / jnp.sqrt(jnp.maximum(total, 0.25)) - 1.0
                factor.append(jnp.concatenate([one, one], axis=0))
            update = [[None, None], [None, None]]
            for k in range(modes):
                even = left_dot(lefts[2], far[k][0] * factor[0])
                odd = left_dot(lefts[3], far[k][1] * factor[1])
                plus, minus = even + odd, even - odd
                re = jnp.concatenate([plus[:half], minus[:half]], axis=0)
                im = jnp.concatenate([plus[half:], minus[half:]], axis=0)
                even = right_dot(jnp.concatenate([re[:, :half], im[:, :half]], axis=1), rights[2])
                odd = right_dot(jnp.concatenate([re[:, half:], im[:, half:]], axis=1), rights[3])
                plus, minus = even + odd, even - odd
                back_re = [plus[:, :half], minus[:, :half]]
                back_im = [plus[:, half:], minus[:, half:]]
                for t in range(2):
                    pr, pi = probe_at(0, k, t), probe_at(1, k, t)
                    u_re = pr * back_re[t] + pi * back_im[t]
                    u_im = pr * back_im[t] - pi * back_re[t]
                    update[0][t] = u_re if k == 0 else update[0][t] + u_re
                    update[1][t] = u_im if k == 0 else update[1][t] + u_im
                    lanes = pl.ds(t * LANES, LANES)
                    xr, xi = patch[0][t], patch[1][t]
                    probe_out[k, :, lanes] += xr * back_re[t] + xi * back_im[t]
                    probe_out[modes + k, :, lanes] += xr * back_im[t] - xi * back_re[t]
            for t in range(2):
                lanes = pl.ds(t * LANES, LANES)
                probe_out[2 * modes, :, lanes] += patch[0][t] * patch[0][t] + patch[1][t] * patch[1][t]
            for c in range(2):
                add_window(c, update[c], row, block, shift)

        return carry

    lax.fori_loop(0, count, visit, 0)

    stores = []

    def store(src, dst):
        copy = pltpu.make_async_copy(src, dst, sems.at[len(stores)])
        copy.start()
        stores.append(copy)

    def store_all(chan, mid, above, below, west, east):
        for t in range(tiles):
            cols = pl.ds(t * LANES, LANES)
            store(acc.at[side + t, chan, body, :], mid.at[:, :, cols])
            if above is not None:
                store(acc.at[side + t, chan, pl.ds(0, margin), :], above.at[:, :, cols])
                store(acc.at[side + t, chan, pl.ds(margin + tile_rows, margin), :], below.at[:, :, cols])
        if above is not None:
            store(acc.at[0, chan], west)
            store(acc.at[side + tiles, chan], east)
        else:
            store(acc.at[0, chan, body, :], west)
            store(acc.at[side + tiles, chan, body, :], east)

    grads = pl.ds(0, 2)
    if phase == 0:
        store_all(grads, mid_out, None, None, left_out, right_out)
        store_all(pl.ds(2, 1), lit_mid, lit_top, lit_bottom, lit_left, lit_right)
    else:
        store_all(grads, mid_out, top_out, bottom_out, left_out, right_out)
    for copy in stores:
        copy.wait()


def run_slots(phase, geometry, meta, tile, left, right, top, bottom, probe, amps, tables, probe_in):
    tile_rows, tile_cols, margin, edge, modes = geometry
    rows_all = tile_rows + 2 * margin
    tiles = tile_cols // LANES
    anywhere = pl.BlockSpec(memory_space=pl.ANY)
    vmem = pl.BlockSpec(memory_space=pltpu.VMEM)
    smem = pl.BlockSpec(memory_space=pltpu.SMEM)

    def shape(*dims):
        return jax.ShapeDtypeStruct(dims, F32)

    probe_shape = shape(2 * modes + 1, edge, edge)
    if phase == 0:
        outs = [shape(2, tile_rows, tile_cols), shape(2, tile_rows, margin), shape(2, tile_rows, margin)]
        lead = 1
        outs += [
            shape(lead, tile_rows, tile_cols),
            shape(lead, margin, tile_cols),
            shape(lead, margin, tile_cols),
            shape(lead, rows_all, margin),
            shape(lead, rows_all, margin),
        ]
    else:
        lead = 2
        outs = [
            shape(lead, tile_rows, tile_cols),
            shape(lead, margin, tile_cols),
            shape(lead, margin, tile_cols),
            shape(lead, rows_all, margin),
            shape(lead, rows_all, margin),
        ]
    out_specs = [anywhere] * len(outs) + [vmem]
    outs.append(probe_shape)
    channels = 3 if phase == 0 else 2
    blocks = tiles + 3
    kernel = functools.partial(slots_kernel, phase, geometry)
    return pl.pallas_call(
        kernel,
        out_shape=outs,
        in_specs=[smem, anywhere, anywhere, anywhere, anywhere, anywhere, vmem, anywhere, vmem, vmem, vmem],
        out_specs=out_specs,
        scratch_shapes=[
            pltpu.VMEM((blocks, 2, rows_all, LANES), F32),
            pltpu.VMEM((blocks, channels, rows_all, LANES), F32),
            pltpu.VMEM((edge, edge), BF16),
            pltpu.SemaphoreType.DMA((40,)),
        ],
        compiler_params=pltpu.CompilerParams(vmem_limit_bytes=48 * 1024 * 1024),
        cost_estimate=pl.CostEstimate(flops=int(1e10), bytes_accessed=20_000_000, transcendentals=0),
        name=f"slots_{phase}",
    )(meta, tile, left, right, top, bottom, probe, amps, tables[0], tables[1], probe_in)


def shift_both(low, high, axis):
    count = lax.axis_size(axis)
    up = [(i, i + 1) for i in range(count - 1)]
    down = [(i + 1, i) for i in range(count - 1)]
    return lax.ppermute(high, axis, up), lax.ppermute(low, axis, down)


def bits_of(count):
    return count.bit_length() - 1


def all_reduce_finish(stack, finish, stages):
    def index_of(axis, bits):
        place = lax.axis_index(axis)
        index = jnp.int32(0)
        for position, bit in enumerate(bits):
            index = index + (((place >> bit) & 1) << position)
        return index

    def partner_perm(axis, bits, member):
        mask = sum(((member >> position) & 1) << bit for position, bit in enumerate(bits))
        return [(i, i ^ mask) for i in range(lax.axis_size(axis))]

    start = jnp.int32(0)
    for axis, bits in stages:
        group = 1 << len(bits)
        rows = stack.shape[1] // group
        index = index_of(axis, bits)
        total = lax.dynamic_slice_in_dim(stack, index * rows, rows, axis=1)
        pieces = []
        for member in range(1, group):
            piece = lax.dynamic_slice_in_dim(stack, (index ^ member) * rows, rows, axis=1)
            pieces.append(lax.ppermute(piece, axis, partner_perm(axis, bits, member)))
        for piece in pieces:
            total = total + piece
        start = start + index * rows
        stack = total
    shard = finish(stack, start)
    for axis, bits in reversed(stages):
        group = 1 << len(bits)
        rows = shard.shape[1]
        index = index_of(axis, bits)
        pieces = [shard]
        for member in range(1, group):
            pieces.append(lax.ppermute(shard, axis, partner_perm(axis, bits, member)))
        if group == 2:
            shard = jnp.where(
                index == 0,
                jnp.concatenate(pieces, axis=1),
                jnp.concatenate(pieces[::-1], axis=1),
            )
        else:
            whole = jnp.zeros((shard.shape[0], rows * group, shard.shape[2]), F32)
            for member in range(group):
                whole = lax.dynamic_update_slice_in_dim(
                    whole, pieces[member], (index ^ member) * rows, axis=1
                )
            shard = whole
    return shard


def stages_of(rows, cols):
    stages = [("col", (bit,)) for bit in range(bits_of(cols))]
    row_bits = list(range(1, bits_of(rows))) + [0]
    while row_bits:
        take, row_bits = row_bits[:1], row_bits[1:]
        stages.append(("row", tuple(take)))
    return stages


def on_device(object_field, probe_modes, scan_offsets, scan_counts, amplitudes):
    tile_rows = object_field.shape[1]
    tile_cols = object_field.shape[2]
    modes = probe_modes.shape[1]
    edge = probe_modes.shape[-1]
    margin = edge // 2
    slots = amplitudes.shape[2]
    geometry = (tile_rows, tile_cols, margin, edge, modes)
    anchor = jnp.stack(
        [lax.axis_index("row") * tile_rows - margin, lax.axis_index("col") * tile_cols - margin]
    )
    places = scan_offsets[0, 0] - anchor[:, None].astype(jnp.int32)
    meta = jnp.concatenate([places, jnp.broadcast_to(scan_counts[0, 0], (1, slots))], axis=0)

    top, bottom = shift_both(object_field[:, :margin], object_field[:, tile_rows - margin :], "row")
    left, right = shift_both(
        object_field[:, :, :margin], object_field[:, :, tile_cols - margin :], "col"
    )
    tables = tuple(jnp.asarray(t) for t in dft_tables(edge))
    order = np.concatenate([np.arange(0, edge, 2), np.arange(1, edge, 2)])
    select = jnp.asarray(np.eye(edge)[order].astype(BF16))
    amps = jnp.einsum("ui,sij->suj", select, amplitudes[0, 0], preferred_element_type=BF16)
    amps = jnp.einsum("suj,vj->suv", amps, select, preferred_element_type=BF16)

    none = jnp.zeros((2 * modes + 1, edge, edge), F32)
    first = run_slots(
        0, geometry, meta, object_field, left, right, top[:1, :8, :128], bottom[:1, :8, :128], probe_modes, amps, tables, none
    ) if False else run_slots(
        0, geometry, meta, object_field, left, right, left, right, probe_modes, amps, tables, none
    )
    grad_a, left_a, right_a, lit_mid, lit_top, lit_bottom, lit_left, lit_right, probe_a = first

    corner = jnp.concatenate([top, bottom], axis=1)
    corner_left, corner_right = shift_both(
        corner[:, :, :margin], corner[:, :, tile_cols - margin :], "col"
    )

    def tall(corners, mid):
        return jnp.concatenate([corners[:, :margin], mid, corners[:, margin:]], axis=1)

    second = run_slots(
        1,
        geometry,
        meta,
        object_field,
        tall(corner_left, left),
        tall(corner_right, right),
        top,
        bottom,
        probe_modes,
        amps,
        tables,
        probe_a,
    )
    grad_b, top_b, bottom_b, left_b, right_b, probe_sum = second

    pad = ((0, 0), (margin, margin), (0, 0))
    west = jnp.concatenate([left_b + jnp.pad(left_a, pad), lit_left], axis=0)
    east = jnp.concatenate([right_b + jnp.pad(right_a, pad), lit_right], axis=0)
    from_west, from_east = shift_both(west, east, "col")
    add_cols = jnp.concatenate(
        [from_west, jnp.zeros((3, tile_rows + 2 * margin, tile_cols - 2 * margin), F32), from_east],
        axis=2,
    )
    above = jnp.concatenate([top_b, lit_top], axis=0) + add_cols[:, :margin]
    below = jnp.concatenate([bottom_b, lit_bottom], axis=0) + add_cols[:, margin + tile_rows :]
    from_above, from_below = shift_both(above, below, "row")

    def finish(stack, start):
        rows = stack.shape[1]
        old = lax.dynamic_slice_in_dim(
            probe_modes.reshape(2 * modes, edge, edge), start, rows, axis=1
        )
        return old + stack[: 2 * modes] / (stack[2 * modes :] + 1.0)

    stages = stages_of(lax.axis_size("row"), lax.axis_size("col"))
    probe_new = all_reduce_finish(probe_sum, finish, stages).reshape(probe_modes.shape)

    mid = jnp.concatenate([grad_a + grad_b, lit_mid], axis=0) + add_cols[:, margin : margin + tile_rows]
    add_rows = jnp.concatenate(
        [from_above, jnp.zeros((3, tile_rows - 2 * margin, tile_cols), F32), from_below], axis=1
    )
    mid = mid + add_rows
    object_new = object_field + mid[:2] / (mid[2:] + 1.0)
    return object_new, probe_new


def solution(mesh):
    in_specs = (
        P(None, "row", "col"),
        P(),
        P("row", "col", None, None),
        P("row", "col"),
        P("row", "col", None, None, None),
    )
    out_specs = (P(None, "row", "col"), P())
    return jax.shard_map(
        on_device, mesh=mesh, in_specs=in_specs, out_specs=out_specs, check_vma=False
    )
```

time: 484 us -> 168 us (0.35)
  local copies, waits for them, and re-layouts: 112 us -> 15.9 us
  waiting for transfers between devices: 151 us -> 63.1 us
  other arithmetic: 102 us -> 15.4 us
  matrix products: 36.7 us -> 0.58 us
  Pallas kernels: 0 us -> 17.4 us
  between operations: 14.3 us -> 1.91 us
  loops' own time: 11.8 us -> 0 us
    psum x1 -> x0, waiting for transfers between devices: 90.4 us -> none  [on_device(): total_grad, total_norm = lax.psum((probe_grad, probe_norm), ('row', 'col'))]
    dynamic_update_slice x15 -> x0, local copies, waits for them, and re-layouts: 52 us -> none  [add_window(): lax.dynamic_update_slice(canvas, window + values, (0, row_start, col_start))]
    dot_general x20 -> x1, matrix products: 36.7 us -> 0.58 us  [on_device(): amps = jnp.einsum('suj,vj->suv', amps, select, preferred_element_type=BF16)]
    add x28 -> x12, other arithmetic: 34.8 us -> 10.4 us  [the longest x1 2.87 us: on_device(): grad_a + grad_b]
    reduce_sum x11 -> x0, other arithmetic: 21.2 us -> none  [the longest x5 14.8 us: slot_terms(): jnp.sum(probe_real * back_real + probe_imag * back_imag, axis=0)]
    pallas_call x0 -> x2, Pallas kernels: none -> 17.4 us  [run_slots(): pl.pallas_call(kernel, out_shape=outs, in_specs=[smem, anywhere, anywhere...]
    another operation x21 -> x0, local copies, waits for them, and re-layouts: 16.9 us -> none
    dynamic_slice x20 -> x5, local copies, waits for them, and re-layouts: 17.2 us -> 2.15 us  [all_reduce_finish(): lax.dynamic_slice_in_dim(stack, (index ^ member) * rows, rows, axis=1)]
  transfers between devices with their start and end apart: 9 -> 20, of which waited for: 4 -> 11; matrix products, arithmetic and copies ran while one was open for 4% -> 10% of each run, Pallas kernels for 0% -> 4%
where the time goes in v1:
time: 168 us; the launch traced here: 166 us
  waiting for transfers between devices  63.1 us (38%)
  starting transfers between devices  51.2 us (30%)
  Pallas kernels  17.4 us (10%)
  local copies, waits for them, and re-layouts  15.9 us (9%)
  other arithmetic  15.4 us (9%)
  between operations  1.91 us (1%)
    ppermute x10, waiting for transfers between devices, shift_both(): return (lax.ppermute(high, axis, up), lax.ppermute(low, axis, down))  27.5 us
    ppermute x10, starting transfers between devices, shift_both(): return (lax.ppermute(high, axis, up), lax.ppermute(low, axis, down))  22.3 us
    ppermute x5, starting transfers between devices, all_reduce_finish(): pieces.append(lax.ppermute(piece, axis, partner_perm(axis, bits, member)))  20.6 us
    ppermute x5, waiting for transfers between devices, all_reduce_finish(): pieces.append(lax.ppermute(shard, axis, partner_perm(axis, bits, member)))  19.6 us
    pallas_call x2, Pallas kernels, run_slots(): pl.pallas_call(kernel, out_shape=outs, in_specs=[smem, anywhere, anywhere...  17.4 us
    ppermute x5, waiting for transfers between devices, all_reduce_finish(): pieces.append(lax.ppermute(piece, axis, partner_perm(axis, bits, member)))  16 us
    ppermute x5, starting transfers between devices, all_reduce_finish(): pieces.append(lax.ppermute(shard, axis, partner_perm(axis, bits, member)))  8.37 us
    unnamed x61, local copies, waits for them, and re-layouts  7.97 us
  transfers between devices with their start and end apart: 20, of which 11 were waited for; matrix products, arithmetic and copies ran while one was open for 10% of the time, Pallas kernels for 4%

profile of v1, /device:TPU:0, one launch (start us, length us, event | category | flops | bytes accessed | tf_op | source)
XLA Modules:
  0.0 165.5 jit_solution(5606969436044340101)
XLA Ops:
  0.7 2.4 %fusion.9 = (f32[2,512,128]{2,1,0:T(8,128)}, f32[2,512,128]{2,1,0:T(8,128)}) fusion(f32[2,512,512]{2,1,0:T(8,128)} %tile.3), kind=kLoop, calls=%fused_computation.45 | loop fusion | bytes 2097152 | tf_op jit(solution)/shard_map/slice | solution.py:403
  3.1 2.5 %collective-permute-start = (f32[2,512,128]{2,1,0:T(8,128)}, f32[2,512,128]{2,1,0:T(8,128)S(1)}, u32[]{:S(2)}, u32[]{:S(2)}) collective-permute-start(f32[2,512,128]{2,1,0:T(8,128)} %get-tuple-element.37), channel_id=1, source_target_pairs={{0,1},{2,3},{4,5},{6,7},{8,9},{10,11},{12,13},{14,15},{16,17},{18,... | collective-permute-start | bytes 1572872 | tf_op jit(solution)/shard_map/ppermute | solution.py:321
  8.0 4.2 %collective-permute-start.2 = (f32[2,128,512]{2,1,0:T(8,128)}, f32[2,128,512]{2,1,0:T(8,128)S(1)}, u32[]{:S(2)}, u32[]{:S(2)}) collective-permute-start(f32[2,128,512]{2,1,0:T(8,128)} %get-tuple-element.35), channel_id=1, source_target_pairs={{0,2},{2,4},{4,6},{6,8},{8,10},{10,12},{12,14},{14,16},{16,18},{18... | collective-permute-start | bytes 1572872 | tf_op jit(solution)/shard_map/ppermute | solution.py:321
  15.0 20.9 %collective-permute-done.2.top = f32[2,128,512]{2,1,0:T(8,128)S(1)} collective-permute-done((f32[2,128,512]{2,1,0:T(8,128)}, f32[2,128,512]{2,1,0:T(8,128)S(1)}, u32[]{:S(2)}, u32[]{:S(2)}) %collective-permute-start.2) | collective-permute-done | bytes 524320 | tf_op jit(solution)/shard_map/ppermute | solution.py:321
  35.9 1.9 %collective-permute-done.3.bottom = f32[2,128,512]{2,1,0:T(8,128)} collective-permute-done((f32[2,128,512]{2,1,0:T(8,128)}, f32[2,128,512]{2,1,0:T(8,128)}, u32[]{:S(2)}, u32[]{:S(2)}) %collective-permute-start.3) | collective-permute-done | bytes 524320 | tf_op jit(solution)/shard_map/ppermute | solution.py:321
  38.9 2.0 %collective-permute-start.4 = (f32[2,256,128]{2,1,0:T(8,128)S(1)}, f32[2,256,128]{2,1,0:T(8,128)S(1)}, u32[]{:S(2)}, u32[]{:S(2)}) collective-permute-start(f32[2,256,128]{2,1,0:T(8,128)S(1)} %get-tuple-element.39), channel_id=1, source_target_pairs={{0,1},{2,3},{4,5},{6,7},{8,9},{10,11},{12,13},{14,15},{16,17},{18,... | collective-permute-start | bytes 786440 | tf_op jit(solution)/shard_map/ppermute | solution.py:321
  45.3 7.2 %slots_0.1 = (f32[2,512,512]{2,1,0:T(8,128)}, f32[2,512,128]{2,1,0:T(8,128)S(1)}, f32[2,512,128]{2,1,0:T(8,128)S(1)}, f32[1,512,512]{2,1,0:T(8,128)S(1)}, f32[1,...) custom-call(s32[3,6]{1,0:T(4,128)S(1)} %concatenate.93.meta, ...), custom_call_target="tpu_custom_call" | custom-call | flops 10000000000 | bytes 20000000 | tf_op jit(solution)/shard_map/slots_0/pallas_call | solution.py:300
  54.7 10.2 %slots_1.1 = (f32[2,512,512]{2,1,0:T(8,128)}, f32[2,128,512]{2,1,0:T(8,128)S(1)}, f32[2,128,512]{2,1,0:T(8,128)S(1)}, f32[2,768,128]{2,1,0:T(8,128)S(1)}, f32[2,...) custom-call(s32[3,6]{1,0:T(4,128)S(1)} %concatenate.93.meta, f32[2,512,512]{2,1,0:T(8,128)} %tile.3, ...), custom_call_target="tpu_custom_call" | custom-call | flops 10000000000 | bytes 20000000 | tf_op jit(solution)/shard_map/slots_1/pallas_call | solution.py:300
  67.5 2.1 %constant_dynamic-slice_fusion.4 = f32[5,128,256]{2,1,0:T(8,128)} fusion(f32[5,256,256]{2,1,0:T(8,128)} %get-tuple-element.31, s32[]{:T(128)S(6)} %select_n.96), kind=kLoop, calls=%fused_computation.41 | loop fusion | bytes 1310724 | tf_op jit(solution)/shard_map/dynamic_slice | solution.py:348
  70.8 2.1 %collective-permute-done.10 = f32[5,128,256]{2,1,0:T(8,128)} collective-permute-done((f32[5,128,256]{2,1,0:T(8,128)}, f32[5,128,256]{2,1,0:T(8,128)}, u32[]{:S(2)}, u32[]{:S(2)}) %collective-permute-start.10) | collective-permute-done | bytes 655392 | tf_op jit(solution)/shard_map/ppermute | solution.py:349
  72.8 1.4 dynamic-slice_add_fusion
  75.6 3.4 %collective-permute-start.6 = (f32[3,768,128]{2,1,0:T(8,128)}, f32[3,768,128]{2,1,0:T(8,128)}, u32[]{:S(2)}, u32[]{:S(2)}) collective-permute-start(f32[3,768,128]{2,1,0:T(8,128)} %pad_maximum_fusion.1), channel_id=1, source_target_pairs={{0,1},{2,3},{4,5},{6,7},{8,9},{10,11},{12,13},{14,15},{16,17},{18,... | collective-permute-start | bytes 3538952 | tf_op jit(solution)/shard_map/ppermute | solution.py:321
  79.0 5.3 %collective-permute-done.11 = f32[5,64,256]{2,1,0:T(8,128)S(1)} collective-permute-done((f32[5,64,256]{2,1,0:T(8,128)S(1)}, f32[5,64,256]{2,1,0:T(8,128)S(1)}, u32[]{:S(2)}, u32[]{:S(2)}) %collective-permute-start.11) | collective-permute-done | bytes 327712 | tf_op jit(solution)/shard_map/ppermute | solution.py:349
  84.4 3.8 %collective-permute-start.12 = (f32[5,32,256]{2,1,0:T(8,128)S(1)}, f32[5,32,256]{2,1,0:T(8,128)S(1)}, u32[]{:S(2)}, u32[]{:S(2)}) collective-permute-start(f32[5,32,256]{2,1,0:T(8,128)S(1)} %constant_dynamic-slice_fusion.2), channel_id=1, source_target_pairs={{0,8},{2,10},{4,12},{6,14},{8,0},{10,2},{12,4},{14,6},{16,24},{18,... | collective-permute-start | bytes 491528 | tf_op jit(solution)/shard_map/ppermute | solution.py:349
  89.7 2.2 %collective-permute-done.12 = f32[5,32,256]{2,1,0:T(8,128)S(1)} collective-permute-done((f32[5,32,256]{2,1,0:T(8,128)S(1)}, f32[5,32,256]{2,1,0:T(8,128)S(1)}, u32[]{:S(2)}, u32[]{:S(2)}) %collective-permute-start.12) | collective-permute-done | bytes 163872 | tf_op jit(solution)/shard_map/ppermute | solution.py:349
  91.9 13.7 %collective-permute-start.13 = (f32[5,16,256]{2,1,0:T(8,128)S(1)}, f32[5,16,256]{2,1,0:T(8,128)S(1)}, u32[]{:S(2)}, u32[]{:S(2)}) collective-permute-start(f32[5,16,256]{2,1,0:T(8,128)S(1)} %constant_dynamic-slice_fusion.1), channel_id=1, source_target_pairs={{0,16},{2,18},{4,20},{6,22},{8,24},{10,26},{12,28},{14,30},{16,0},... | collective-permute-start | bytes 245768 | tf_op jit(solution)/shard_map/ppermute | solution.py:349
  105.6 4.1 %collective-permute-done.13 = f32[5,16,256]{2,1,0:T(8,128)S(1)} collective-permute-done((f32[5,16,256]{2,1,0:T(8,128)S(1)}, f32[5,16,256]{2,1,0:T(8,128)S(1)}, u32[]{:S(2)}, u32[]{:S(2)}) %collective-permute-start.13) | collective-permute-done | bytes 81952 | tf_op jit(solution)/shard_map/ppermute | solution.py:349
  109.8 1.7 %collective-permute-start.14 = (f32[5,8,256]{2,1,0:T(8,128)S(1)}, f32[5,8,256]{2,1,0:T(8,128)S(1)}, u32[]{:S(2)}, u32[]{:S(2)}) collective-permute-start(f32[5,8,256]{2,1,0:T(8,128)S(1)} %constant_dynamic-slice_fusion), channel_id=1, source_target_pairs={{0,2},{2,0},{4,6},{6,4},{8,10},{10,8},{12,14},{14,12},{16,18},{18,... | collective-permute-start | bytes 122888 | tf_op jit(solution)/shard_map/ppermute | solution.py:349
  111.5 2.3 %collective-permute-done.14 = f32[5,8,256]{2,1,0:T(8,128)S(1)} collective-permute-done((f32[5,8,256]{2,1,0:T(8,128)S(1)}, f32[5,8,256]{2,1,0:T(8,128)S(1)}, u32[]{:S(2)}, u32[]{:S(2)}) %collective-permute-start.14) | collective-permute-done | bytes 40992 | tf_op jit(solution)/shard_map/ppermute | solution.py:349
  114.7 1.7 %collective-permute-start.15 = (f32[4,8,256]{2,1,0:T(8,128)S(1)}, f32[4,8,256]{2,1,0:T(8,128)S(1)}, u32[]{:S(2)}, u32[]{:S(2)}) collective-permute-start(f32[4,8,256]{2,1,0:T(8,128)S(1)} %fusion.6), channel_id=1, source_target_pairs={{0,2},{2,0},{4,6},{6,4},{8,10},{10,8},{12,14},{14,12},{16,18},{18,... | collective-permute-start | bytes 98312 | tf_op jit(solution)/shard_map/ppermute | solution.py:361
  116.4 2.2 %pad_maximum_fusion = f32[3,768,512]{2,1,0:T(8,128)S(1)} fusion(f32[3,768,128]{2,1,0:T(8,128)} %collective-permute-done.7, f32[3,768,128]{2,1,0:T(8,128)} %collective-permute-done.6, f32[512]{0:T(512)S(1)} %pad.50.clone), kind=kLoop, calls=%fused_computation | loop fusion | flops 2359296 | bytes 7079936 | tf_op jit(solution)/shard_map/concatenate | solution.py:447
  120.0 1.6 slice_add_fusion.3
  121.6 3.6 %collective-permute-start.8 = (f32[3,128,512]{2,1,0:T(8,128)}, f32[3,128,512]{2,1,0:T(8,128)S(1)}, u32[]{:S(2)}, u32[]{:S(2)}) collective-permute-start(f32[3,128,512]{2,1,0:T(8,128)} %get-tuple-element.32), channel_id=1, source_target_pairs={{0,2},{2,4},{4,6},{6,8},{8,10},{10,12},{12,14},{14,16},{16,18},{18... | collective-permute-start | bytes 2359304 | tf_op jit(solution)/shard_map/ppermute | solution.py:321
  126.5 5.2 %collective-permute-start.17 = (f32[4,32,256]{2,1,0:T(8,128)S(1)}, f32[4,32,256]{2,1,0:T(8,128)S(1)}, u32[]{:S(2)}, u32[]{:S(2)}) collective-permute-start(f32[4,32,256]{2,1,0:T(8,128)S(1)} %maximum_select_fusion.6), channel_id=1, source_target_pairs={{0,8},{2,10},{4,12},{6,14},{8,0},{10,2},{12,4},{14,6},{16,24},{18,... | collective-permute-start | bytes 393224 | tf_op jit(solution)/shard_map/ppermute | solution.py:361
  131.7 16.2 %collective-permute-done.17 = f32[4,32,256]{2,1,0:T(8,128)S(1)} collective-permute-done((f32[4,32,256]{2,1,0:T(8,128)S(1)}, f32[4,32,256]{2,1,0:T(8,128)S(1)}, u32[]{:S(2)}, u32[]{:S(2)}) %collective-permute-start.17) | collective-permute-done | bytes 131104 | tf_op jit(solution)/shard_map/ppermute | solution.py:361
  148.0 2.9 %add.107 = f32[2,512,512]{2,1,0:T(8,128)S(1)} add(f32[2,512,512]{2,1,0:T(8,128)} %get-tuple-element.17, f32[2,512,512]{2,1,0:T(8,128)} %get-tuple-element.19) | non-fusion elementwise | flops 524288 | bytes 6291456 | tf_op jit(solution)/shard_map/add | solution.py:465
  151.0 3.4 %collective-permute-done.18 = f32[4,64,256]{2,1,0:T(8,128)S(1)} collective-permute-done((f32[4,64,256]{2,1,0:T(8,128)S(1)}, f32[4,64,256]{2,1,0:T(8,128)S(1)}, u32[]{:S(2)}, u32[]{:S(2)}) %collective-permute-start.18) | collective-permute-done | bytes 262176 | tf_op jit(solution)/shard_map/ppermute | solution.py:361
  154.5 2.0 %collective-permute-done.8 = f32[3,128,512]{2,1,0:T(8,128)S(1)} collective-permute-done((f32[3,128,512]{2,1,0:T(8,128)}, f32[3,128,512]{2,1,0:T(8,128)S(1)}, u32[]{:S(2)}, u32[]{:S(2)}) %collective-permute-start.8) | collective-permute-done | bytes 786464 | tf_op jit(solution)/shard_map/ppermute | solution.py:321
  156.5 2.7 %collective-permute-done.9 = f32[3,128,512]{2,1,0:T(8,128)} collective-permute-done((f32[3,128,512]{2,1,0:T(8,128)}, f32[3,128,512]{2,1,0:T(8,128)}, u32[]{:S(2)}, u32[]{:S(2)}) %collective-permute-start.9) | collective-permute-done | bytes 786464 | tf_op jit(solution)/shard_map/ppermute | solution.py:321
  159.2 1.7 %fusion = f32[3,512,512]{2,1,0:T(8,128)S(1)} fusion(f32[3,768,512]{2,1,0:T(8,128)S(1)} %bitcast.28, f32[1,512,512]{2,1,0:T(8,128)S(1)} %get-tuple-element.20, f32[2,512,512]{2,1,0:T(8,128)S(1)} %add.107, f32[3,128,512]{2,1,0:T(8,128)} %collective-permute-done.9, f32[3,128,512]{2,1,0:T(8,128)S(1)} %collective-permute-done.8, f32[512]{0:T(512)S(1)} %pad.50.clone), kind=kLoop, calls=%fused_computation.2 | loop fusion | flops 3932160 | bytes 11012096 | tf_op jit(solution)/shard_map/add | solution.py:469
  161.0 1.5 copy-done.25
  162.5 2.0 %fusion.1 = f32[2,512,512]{2,1,0:T(8,128)} fusion(f32[2,512,512]{2,1,0:T(8,128)S(1)} %copy-done.25, f32[3,512,512]{2,1,0:T(8,128)S(1)} %fusion, f32[512,512]{1,0:T(8,128)S(1)} %fusion.3), kind=kLoop, calls=%fused_computation.4 | loop fusion | flops 1048576 | bytes 7340032 | tf_op jit(solution)/shard_map/add | solution.py:470
  (117 shorter events, 23.5 us)
Async XLA Ops:
  0.6 12.9 %copy-start = (bf16[1,1,6,256,256]{4,3,2,1,0:T(8,128)(2,1)S(1)}, bf16[1,1,6,256,256]{4,3,2,1,0:T(8,128)(2,1)}, u32[]{:S(2)}) copy-start(bf16[1,1,6,256,256]{4,3,2,1,0:T(8,128)(2,1)} %param.12) | copy-start | bytes 2359300
  0.6 6.3 %copy-start.24 = (f32[2,512,512]{2,1,0:T(8,128)S(1)}, f32[2,512,512]{2,1,0:T(8,128)}, u32[]{:S(2)}) copy-start(f32[2,512,512]{2,1,0:T(8,128)} %tile.3) | copy-start | bytes 6291460
  0.7 12.9 %copy-start.26 = (bf16[256,256,1]{1,0,2:T(8,128)(2,1)S(1)}, bf16[256,256,1]{1,0,2:T(8,128)(2,1)}, u32[]{:S(2)}) copy-start(bf16[256,256,1]{1,0,2:T(8,128)(2,1)} %constant.59) | copy-start | bytes 393220
  3.1 11.1 %copy-start.27 = (s32[1,1,2,6]{3,2,1,0:T(2,128)S(1)}, s32[1,1,2,6]{3,2,1,0:T(2,128)}, u32[]{:S(2)}) copy-start(s32[1,1,2,6]{3,2,1,0:T(2,128)} %param.10) | copy-start | bytes 148
  3.1 39.2 %collective-permute-start = (f32[2,512,128]{2,1,0:T(8,128)}, f32[2,512,128]{2,1,0:T(8,128)S(1)}, u32[]{:S(2)}, u32[]{:S(2)}) collective-permute-start(f32[2,512,128]{2,1,0:T(8,128)} %get-tuple-element.37), channel_id=1, source_target_pairs={{0,1},{2,3},{4,5},{6,7},{8,9},{10,11},{12,13},{14,15},{16,17},{18,... | collective-permute-start | bytes 1572872 | tf_op jit(solution)/shard_map/ppermute | solution.py:321
  5.6 36.7 %collective-permute-start.1 = (f32[2,512,128]{2,1,0:T(8,128)}, f32[2,512,128]{2,1,0:T(8,128)S(1)}, u32[]{:S(2)}, u32[]{:S(2)}) collective-permute-start(f32[2,512,128]{2,1,0:T(8,128)} %get-tuple-element.36), channel_id=1, source_target_pairs={{1,0},{3,2},{5,4},{7,6},{9,8},{11,10},{13,12},{15,14},{17,16},{19,... | collective-permute-start | bytes 1572872 | tf_op jit(solution)/shard_map/ppermute | solution.py:321
  8.0 27.9 %collective-permute-start.2 = (f32[2,128,512]{2,1,0:T(8,128)}, f32[2,128,512]{2,1,0:T(8,128)S(1)}, u32[]{:S(2)}, u32[]{:S(2)}) collective-permute-start(f32[2,128,512]{2,1,0:T(8,128)} %get-tuple-element.35), channel_id=1, source_target_pairs={{0,2},{2,4},{4,6},{6,8},{8,10},{10,12},{12,14},{14,16},{16,18},{18... | collective-permute-start | bytes 1572872 | tf_op jit(solution)/shard_map/ppermute | solution.py:321
  12.2 25.6 %collective-permute-start.3 = (f32[2,128,512]{2,1,0:T(8,128)}, f32[2,128,512]{2,1,0:T(8,128)}, u32[]{:S(2)}, u32[]{:S(2)}) collective-permute-start(f32[2,128,512]{2,1,0:T(8,128)} %get-tuple-element.34), channel_id=1, source_target_pairs={{2,0},{4,2},{6,4},{8,6},{10,8},{12,10},{14,12},{16,14},{18,16},{20... | collective-permute-start | bytes 1572872 | tf_op jit(solution)/shard_map/ppermute | solution.py:321
  35.9 6.4 %copy-start.9 = (f32[2,128,512]{2,1,0:T(8,128)}, f32[2,128,512]{2,1,0:T(8,128)S(1)}, u32[]{:S(2)}) copy-start(f32[2,128,512]{2,1,0:T(8,128)S(1)} %collective-permute-done.2.top) | copy-start | bytes 1572868
  38.9 14.4 %collective-permute-start.4 = (f32[2,256,128]{2,1,0:T(8,128)S(1)}, f32[2,256,128]{2,1,0:T(8,128)S(1)}, u32[]{:S(2)}, u32[]{:S(2)}) collective-permute-start(f32[2,256,128]{2,1,0:T(8,128)S(1)} %get-tuple-element.39), channel_id=1, source_target_pairs={{0,1},{2,3},{4,5},{6,7},{8,9},{10,11},{12,13},{14,15},{16,17},{18,... | collective-permute-start | bytes 786440 | tf_op jit(solution)/shard_map/ppermute | solution.py:321
  41.0 12.4 %collective-permute-start.5 = (f32[2,256,128]{2,1,0:T(8,128)S(1)}, f32[2,256,128]{2,1,0:T(8,128)S(1)}, u32[]{:S(2)}, u32[]{:S(2)}) collective-permute-start(f32[2,256,128]{2,1,0:T(8,128)S(1)} %get-tuple-element.38), channel_id=1, source_target_pairs={{1,0},{3,2},{5,4},{7,6},{9,8},{11,10},{13,12},{15,14},{17,16},{19,... | collective-permute-start | bytes 786440 | tf_op jit(solution)/shard_map/ppermute | solution.py:321
  67.5 6.8 %copy-start.2 = (f32[2,768,128]{2,1,0:T(8,128)S(1)}, f32[2,768,128]{2,1,0:T(8,128)}, u32[]{:S(2)}) copy-start(f32[2,768,128]{2,1,0:T(8,128)} %copy-done.1) | copy-start | bytes 2359300
  69.6 3.3 %collective-permute-start.10 = (f32[5,128,256]{2,1,0:T(8,128)}, f32[5,128,256]{2,1,0:T(8,128)}, u32[]{:S(2)}, u32[]{:S(2)}) collective-permute-start(f32[5,128,256]{2,1,0:T(8,128)} %constant_dynamic-slice_fusion.4), channel_id=1, source_target_pairs={{0,1},{1,0},{2,3},{3,2},{4,5},{5,4},{6,7},{7,6},{8,9},{9,8},{10,11... | collective-permute-start | bytes 1966088 | tf_op jit(solution)/shard_map/ppermute | solution.py:349
  74.2 10.1 %collective-permute-start.11 = (f32[5,64,256]{2,1,0:T(8,128)S(1)}, f32[5,64,256]{2,1,0:T(8,128)S(1)}, u32[]{:S(2)}, u32[]{:S(2)}) collective-permute-start(f32[5,64,256]{2,1,0:T(8,128)S(1)} %constant_dynamic-slice_fusion.3), channel_id=1, source_target_pairs={{0,4},{2,6},{4,0},{6,2},{8,12},{10,14},{12,8},{14,10},{16,20},{18,... | collective-permute-start | bytes 983048 | tf_op jit(solution)/shard_map/ppermute | solution.py:349
  74.4 13.8 %copy-start.12 = (f32[2,512,128]{2,1,0:T(8,128)S(1)}, f32[2,512,128]{2,1,0:T(8,128)}, u32[]{:S(2)}) copy-start(f32[2,512,128]{2,1,0:T(8,128)} %copy-done.11) | copy-start | bytes 1572868
  75.6 12.7 %copy-start.16 = (f32[1,768,128]{2,1,0:T(8,128)S(1)}, f32[1,768,128]{2,1,0:T(8,128)}, u32[]{:S(2)}) copy-start(f32[1,768,128]{2,1,0:T(8,128)} %copy-done.15) | copy-start | bytes 1179652
  75.6 40.8 %collective-permute-start.6 = (f32[3,768,128]{2,1,0:T(8,128)}, f32[3,768,128]{2,1,0:T(8,128)}, u32[]{:S(2)}, u32[]{:S(2)}) collective-permute-start(f32[3,768,128]{2,1,0:T(8,128)} %pad_maximum_fusion.1), channel_id=1, source_target_pairs={{0,1},{2,3},{4,5},{6,7},{8,9},{10,11},{12,13},{14,15},{16,17},{18,... | collective-permute-start | bytes 3538952 | tf_op jit(solution)/shard_map/ppermute | solution.py:321
  84.4 7.5 %collective-permute-start.12 = (f32[5,32,256]{2,1,0:T(8,128)S(1)}, f32[5,32,256]{2,1,0:T(8,128)S(1)}, u32[]{:S(2)}, u32[]{:S(2)}) collective-permute-start(f32[5,32,256]{2,1,0:T(8,128)S(1)} %constant_dynamic-slice_fusion.2), channel_id=1, source_target_pairs={{0,8},{2,10},{4,12},{6,14},{8,0},{10,2},{12,4},{14,6},{16,24},{18,... | collective-permute-start | bytes 491528 | tf_op jit(solution)/shard_map/ppermute | solution.py:349
  88.4 28.0 %collective-permute-start.7 = (f32[3,768,128]{2,1,0:T(8,128)S(1)}, f32[3,768,128]{2,1,0:T(8,128)}, u32[]{:S(2)}, u32[]{:S(2)}) collective-permute-start(f32[3,768,128]{2,1,0:T(8,128)S(1)} %pad_maximum_fusion.2), channel_id=1, source_target_pairs={{1,0},{3,2},{5,4},{7,6},{9,8},{11,10},{13,12},{15,14},{17,16},{19,... | collective-permute-start | bytes 3538952 | tf_op jit(solution)/shard_map/ppermute | solution.py:321
  91.9 17.9 %collective-permute-start.13 = (f32[5,16,256]{2,1,0:T(8,128)S(1)}, f32[5,16,256]{2,1,0:T(8,128)S(1)}, u32[]{:S(2)}, u32[]{:S(2)}) collective-permute-start(f32[5,16,256]{2,1,0:T(8,128)S(1)} %constant_dynamic-slice_fusion.1), channel_id=1, source_target_pairs={{0,16},{2,18},{4,20},{6,22},{8,24},{10,26},{12,28},{14,30},{16,0},... | collective-permute-start | bytes 245768 | tf_op jit(solution)/shard_map/ppermute | solution.py:349
  109.8 4.1 %collective-permute-start.14 = (f32[5,8,256]{2,1,0:T(8,128)S(1)}, f32[5,8,256]{2,1,0:T(8,128)S(1)}, u32[]{:S(2)}, u32[]{:S(2)}) collective-permute-start(f32[5,8,256]{2,1,0:T(8,128)S(1)} %constant_dynamic-slice_fusion), channel_id=1, source_target_pairs={{0,2},{2,0},{4,6},{6,4},{8,10},{10,8},{12,14},{14,12},{16,18},{18,... | collective-permute-start | bytes 122888 | tf_op jit(solution)/shard_map/ppermute | solution.py:349
  114.6 5.4 %copy-start.4 = (f32[2,128,512]{2,1,0:T(8,128)S(1)}, f32[2,128,512]{2,1,0:T(8,128)}, u32[]{:S(2)}) copy-start(f32[2,128,512]{2,1,0:T(8,128)} %copy-done.3) | copy-start | bytes 1572868
  114.7 5.4 %copy-start.6 = (f32[2,128,512]{2,1,0:T(8,128)S(1)}, f32[2,128,512]{2,1,0:T(8,128)}, u32[]{:S(2)}) copy-start(f32[2,128,512]{2,1,0:T(8,128)} %copy-done.5) | copy-start | bytes 1572868
  114.7 4.0 %collective-permute-start.15 = (f32[4,8,256]{2,1,0:T(8,128)S(1)}, f32[4,8,256]{2,1,0:T(8,128)S(1)}, u32[]{:S(2)}, u32[]{:S(2)}) collective-permute-start(f32[4,8,256]{2,1,0:T(8,128)S(1)} %fusion.6), channel_id=1, source_target_pairs={{0,2},{2,0},{4,6},{6,4},{8,10},{10,8},{12,14},{14,12},{16,18},{18,... | collective-permute-start | bytes 98312 | tf_op jit(solution)/shard_map/ppermute | solution.py:361
  118.7 7.8 %collective-permute-start.16 = (f32[4,16,256]{2,1,0:T(8,128)S(1)}, f32[4,16,256]{2,1,0:T(8,128)S(1)}, u32[]{:S(2)}, u32[]{:S(2)}) collective-permute-start(f32[4,16,256]{2,1,0:T(8,128)S(1)} %maximum_select_fusion.7), channel_id=1, source_target_pairs={{0,16},{2,18},{4,20},{6,22},{8,24},{10,26},{12,28},{14,30},{16,0},... | collective-permute-start | bytes 196616 | tf_op jit(solution)/shard_map/ppermute | solution.py:361
  121.6 34.9 %collective-permute-start.8 = (f32[3,128,512]{2,1,0:T(8,128)}, f32[3,128,512]{2,1,0:T(8,128)S(1)}, u32[]{:S(2)}, u32[]{:S(2)}) collective-permute-start(f32[3,128,512]{2,1,0:T(8,128)} %get-tuple-element.32), channel_id=1, source_target_pairs={{0,2},{2,4},{4,6},{6,8},{8,10},{10,12},{12,14},{14,16},{16,18},{18... | collective-permute-start | bytes 2359304 | tf_op jit(solution)/shard_map/ppermute | solution.py:321
  125.2 34.0 %collective-permute-start.9 = (f32[3,128,512]{2,1,0:T(8,128)}, f32[3,128,512]{2,1,0:T(8,128)}, u32[]{:S(2)}, u32[]{:S(2)}) collective-permute-start(f32[3,128,512]{2,1,0:T(8,128)} %get-tuple-element.33), channel_id=1, source_target_pairs={{2,0},{4,2},{6,4},{8,6},{10,8},{12,10},{14,12},{16,14},{18,16},{20... | collective-permute-start | bytes 2359304 | tf_op jit(solution)/shard_map/ppermute | solution.py:321
  126.5 21.4 %collective-permute-start.17 = (f32[4,32,256]{2,1,0:T(8,128)S(1)}, f32[4,32,256]{2,1,0:T(8,128)S(1)}, u32[]{:S(2)}, u32[]{:S(2)}) collective-permute-start(f32[4,32,256]{2,1,0:T(8,128)S(1)} %maximum_select_fusion.6), channel_id=1, source_target_pairs={{0,8},{2,10},{4,12},{6,14},{8,0},{10,2},{12,4},{14,6},{16,24},{18,... | collective-permute-start | bytes 393224 | tf_op jit(solution)/shard_map/ppermute | solution.py:361
  147.9 6.4 %collective-permute-start.18 = (f32[4,64,256]{2,1,0:T(8,128)S(1)}, f32[4,64,256]{2,1,0:T(8,128)S(1)}, u32[]{:S(2)}, u32[]{:S(2)}) collective-permute-start(f32[4,64,256]{2,1,0:T(8,128)S(1)} %maximum_select_fusion.4), channel_id=1, source_target_pairs={{0,4},{2,6},{4,0},{6,2},{8,12},{10,14},{12,8},{14,10},{16,20},{18,... | collective-permute-start | bytes 786440 | tf_op jit(solution)/shard_map/ppermute | solution.py:361
  148.0 11.2 %slice-start = ((s8[4718592]{0:T(1024)(128)(4,1)}), s8[4194304]{0:T(1024)(128)(4,1)S(1)}, s32[]{:S(2)}) async-start(s8[4718592]{0:T(1024)(128)(4,1)} %bitcast.27), calls=%async_computation | async-start | bytes 8388608
  148.0 11.2 %slice-start.1 = ((s8[4718592]{0:T(1024)(128)(4,1)}), s8[524288]{0:T(1024)(128)(4,1)S(1)}, s32[]{:S(2)}) async-start(s8[4718592]{0:T(1024)(128)(4,1)} %bitcast.27), calls=%async_computation.1 | async-start | bytes 1048576
  154.4 10.0 %collective-permute-start.19 = (f32[4,128,256]{2,1,0:T(8,128)S(1)}, f32[4,128,256]{2,1,0:T(8,128)S(1)}, u32[]{:S(2)}, u32[]{:S(2)}) collective-permute-start(f32[4,128,256]{2,1,0:T(8,128)S(1)} %maximum_select_fusion.2), channel_id=1, source_target_pairs={{0,1},{1,0},{2,3},{3,2},{4,5},{5,4},{6,7},{7,6},{8,9},{9,8},{10,11... | collective-permute-start | bytes 1572872 | tf_op jit(solution)/shard_map/ppermute | solution.py:361
  (18 other events, 34.5 us)

commit v2 on v0

v2 whole, which is shorter than its diff:
```python
import functools
import math

import jax
import jax.numpy as jnp
import numpy as np
from jax import lax
from jax.experimental import pallas as pl
from jax.experimental.pallas import tpu as pltpu
from jax.sharding import PartitionSpec as P


F32 = jnp.float32
BF16 = jnp.bfloat16
LANES = 128


def split_host(table):
    high = table.astype(BF16)
    low = (table - high.astype(np.float64)).astype(BF16)
    return high, low


def dft_tables(edge):
    half = edge // 2
    scale = 1.0 / math.sqrt(edge)
    n = np.arange(half)[:, None]
    k = np.arange(half)[None, :]
    right, left = [], []
    for parity in (0, 1):
        angle = (n * (2 * k + parity) % edge) * (2.0 * np.pi / edge)
        cosine, sine = np.cos(angle) * scale, np.sin(angle) * scale
        w = np.block([[cosine, -sine], [sine, cosine]])
        right.append(w)
        left.append(w.T)
    mats = [right[0], right[1], left[0], left[1]]
    as_right = []
    as_left = []
    for m in mats:
        high, low = split_host(m)
        as_right.append(np.concatenate([high, high, low], axis=0))
        as_left.append(np.concatenate([high, high, low], axis=1))
    return (
        np.stack([as_right[0], as_right[1], as_right[2], as_right[3]]),
        np.stack([as_left[2], as_left[3], as_left[0], as_left[1]]),
    )


def split_parts(x):
    high = x.astype(BF16)
    low = (x - high.astype(F32)).astype(BF16)
    return high, low


def right_dot(x, table):
    high, low = split_parts(x)
    return jnp.dot(jnp.concatenate([high, low, high], axis=1), table, preferred_element_type=F32)


def left_dot(table, x):
    high, low = split_parts(x)
    return jnp.dot(table, jnp.concatenate([high, low, high], axis=0), preferred_element_type=F32)


VMEM = pltpu.VMEM
ANYWHERE = pl.BlockSpec(memory_space=pl.ANY)
IN_VMEM = pl.BlockSpec(memory_space=pltpu.VMEM)
IN_SMEM = pl.BlockSpec(memory_space=pltpu.SMEM)
MIB = 1024 * 1024


def shape(*dims):
    return jax.ShapeDtypeStruct(dims, F32)


def aligned(start, size):
    return pl.ds(pl.multiple_of(start, size) if size % 8 == 0 else start, size)


def copy_all(pairs, sems):
    copies = []
    for number, (src, dst) in enumerate(pairs):
        copy = pltpu.make_async_copy(src, dst, sems.at[number])
        copy.start()
        copies.append(copy)
    return copies


def pack_kernel(margin, tile, top, bottom, left, right, sems):
    rows, cols = tile.shape[1:]
    copies = copy_all(
        [
            (tile.at[:, pl.ds(0, margin), :], top),
            (tile.at[:, pl.ds(rows - margin, margin), :], bottom),
            (tile.at[:, :, pl.ds(0, margin)], left),
            (tile.at[:, :, pl.ds(cols - margin, margin)], right),
        ],
        sems,
    )
    for copy in copies:
        copy.wait()


def pack_edges(tile, margin):
    rows, cols = tile.shape[1:]
    return pl.pallas_call(
        functools.partial(pack_kernel, margin),
        out_shape=[shape(2, margin, cols)] * 2 + [shape(2, rows, margin)] * 2,
        in_specs=[ANYWHERE],
        out_specs=[IN_VMEM] * 4,
        scratch_shapes=[pltpu.SemaphoreType.DMA((4,))],
        compiler_params=pltpu.CompilerParams(vmem_limit_bytes=8 * MIB),
        name="pack_edges",
    )(tile)


def add_window(acc, channel, parts, row, block, shift, edge):
    lane = lax.broadcasted_iota(jnp.int32, (edge, LANES), 1)
    keep = lane >= shift
    first = pltpu.roll(parts[0], shift, 1)
    second = pltpu.roll(parts[1], shift, 1)
    rows = pl.ds(row, edge)
    zero = jnp.zeros_like(first)
    last = jnp.minimum(block + 2, acc.shape[0] - 1)
    acc[block, channel, rows, :] += jnp.where(keep, first, zero)
    acc[block + 1, channel, rows, :] += jnp.where(keep, second, first)
    acc[last, channel, rows, :] += jnp.where(keep, zero, second)


def slot_body(slot, row, col, ext, acc, sums, probe, amps, rights, lefts):
    edge = probe.shape[-1]
    modes = probe.shape[1]
    half = edge // 2
    block = col // LANES
    shift = col - block * LANES
    lane = lax.broadcasted_iota(jnp.int32, (edge, LANES), 1)
    back_shift = lax.rem(LANES - shift, LANES)
    keep = lane < LANES - shift
    last = jnp.minimum(block + 2, ext.shape[0] - 1)
    patch = []
    for c in range(2):
        rolled = [
            pltpu.roll(ext[b, c, pl.ds(row, edge), :], back_shift, 1) for b in (block, block + 1, last)
        ]
        patch.append([jnp.where(keep, rolled[t], rolled[t + 1]) for t in range(2)])

    def probe_at(c, k, t):
        return probe[c, k, :, pl.ds(t * LANES, LANES)]

    evens, odds = [], []
    for k in range(modes):
        re = [probe_at(0, k, t) * patch[0][t] - probe_at(1, k, t) * patch[1][t] for t in range(2)]
        im = [probe_at(0, k, t) * patch[1][t] + probe_at(1, k, t) * patch[0][t] for t in range(2)]
        evens.append(right_dot(jnp.concatenate([re[0] + re[1], im[0] + im[1]], axis=1), rights[0]))
        odds.append(right_dot(jnp.concatenate([re[0] - re[1], im[0] - im[1]], axis=1), rights[1]))
    far = []
    for k in range(modes):
        re = jnp.concatenate([evens[k][:, :half], odds[k][:, :half]], axis=1)
        im = jnp.concatenate([evens[k][:, half:], odds[k][:, half:]], axis=1)
        plus = jnp.concatenate([re[:half] + re[half:], im[:half] + im[half:]], axis=0)
        minus = jnp.concatenate([re[:half] - re[half:], im[:half] - im[half:]], axis=0)
        far.append([left_dot(lefts[0], plus), left_dot(lefts[1], minus)])
    factor = []
    for p in range(2):
        total = sum(
            far[k][p][:half] * far[k][p][:half] + far[k][p][half:] * far[k][p][half:]
            for k in range(modes)
        )
        amp = amps[slot, pl.ds(p * half, half), :].astype(F32)
        one = amp / jnp.sqrt(jnp.maximum(total, 0.25)) - 1.0
        factor.append(jnp.concatenate([one, one], axis=0))
    update = [[None, None], [None, None]]
    for k in range(modes):
        even = left_dot(lefts[2], far[k][0] * factor[0])
        odd = left_dot(lefts[3], far[k][1] * factor[1])
        plus, minus = even + odd, even - odd
        re = jnp.concatenate([plus[:half], minus[:half]], axis=0)
        im = jnp.concatenate([plus[half:], minus[half:]], axis=0)
        even = right_dot(jnp.concatenate([re[:, :half], im[:, :half]], axis=1), rights[2])
        odd = right_dot(jnp.concatenate([re[:, half:], im[:, half:]], axis=1), rights[3])
        plus, minus = even + odd, even - odd
        back_re = [plus[:, :half], minus[:, :half]]
        back_im = [plus[:, half:], minus[:, half:]]
        for t in range(2):
            pr, pi = probe_at(0, k, t), probe_at(1, k, t)
            u_re = pr * back_re[t] + pi * back_im[t]
            u_im = pr * back_im[t] - pi * back_re[t]
            update[0][t] = u_re if k == 0 else update[0][t] + u_re
            update[1][t] = u_im if k == 0 else update[1][t] + u_im
            lanes = pl.ds(t * LANES, LANES)
            xr, xi = patch[0][t], patch[1][t]
            sums[k, :, lanes] += xr * back_re[t] + xi * back_im[t]
            sums[modes + k, :, lanes] += xr * back_im[t] - xi * back_re[t]
    for t in range(2):
        lanes = pl.ds(t * LANES, LANES)
        sums[2 * modes, :, lanes] += patch[0][t] * patch[0][t] + patch[1][t] * patch[1][t]
    for c in range(2):
        add_window(acc, c, update[c], row, block, shift, edge)


def interior_kernel(margin, meta, tile, left, right, probe, amps, rights, lefts, ext, acc, sums, sems):
    tile_rows, tile_cols = tile.shape[1:]
    tiles = tile_cols // LANES
    edge = probe.shape[-1]
    modes = probe.shape[1]
    body = pl.ds(margin, tile_rows)
    pairs = [(left, ext.at[0, :, body, :]), (right, ext.at[tiles + 1, :, body, :])]
    for t in range(tiles):
        pairs.append((tile.at[:, :, pl.ds(t * LANES, LANES)], ext.at[1 + t, :, body, :]))
    copies = copy_all(pairs, sems)
    acc[...] = jnp.zeros_like(acc)
    sums[...] = jnp.zeros_like(sums)
    for copy in copies:
        copy.wait()

    def visit(slot, carry):
        row, col = meta[0, slot], meta[1, slot]
        block = col // LANES
        power = [
            sum(
                probe[c, k, :, pl.ds(t * LANES, LANES)] * probe[c, k, :, pl.ds(t * LANES, LANES)]
                for c in range(2)
                for k in range(modes)
            )
            for t in range(2)
        ]
        add_window(acc, 2, power, row, block, col - block * LANES, edge)

        @pl.when(jnp.logical_and(row >= margin, row + edge <= margin + tile_rows))
        def _():
            slot_body(slot, row, col, ext, acc, sums, probe, amps, rights, lefts)

        return carry

    lax.fori_loop(0, meta[2, 0], visit, 0)


def boundary_kernel(
    margin,
    meta,
    top,
    bottom,
    corner_left,
    corner_right,
    probe,
    amps,
    rights,
    lefts,
    ext_in,
    acc_in,
    sums_in,
    ext,
    acc,
    west,
    east,
    keep,
    send,
    sums,
    sems,
):
    tiles = acc.shape[0] - 2
    tile_rows = acc.shape[2] - 2 * margin
    edge = probe.shape[-1]
    above, below = pl.ds(0, margin), pl.ds(margin + tile_rows, margin)
    pairs = []
    for t in range(tiles):
        cols = pl.ds(t * LANES, LANES)
        pairs.append((top.at[:, :, cols], ext.at[1 + t, :, above, :]))
        pairs.append((bottom.at[:, :, cols], ext.at[1 + t, :, below, :]))
    for side, corner in ((0, corner_left), (tiles + 1, corner_right)):
        pairs.append((corner.at[0], ext.at[side, :, above, :]))
        pairs.append((corner.at[1], ext.at[side, :, below, :]))
    copies = copy_all(pairs, sems)
    sums[...] = sums_in[...]
    for copy in copies:
        copy.wait()

    def visit(slot, carry):
        row, col = meta[0, slot], meta[1, slot]

        @pl.when(jnp.logical_or(row < margin, row + edge > margin + tile_rows))
        def _():
            slot_body(slot, row, col, ext, acc, sums, probe, amps, rights, lefts)

        return carry

    lax.fori_loop(0, meta[2, 0], visit, 0)
    west[...] = acc[0]
    east[...] = acc[tiles + 1]
    rows = keep.shape[1]
    index = meta[2, 1]
    keep[...] = sums[:, aligned(index * rows, rows), :]
    send[...] = sums[:, aligned((1 - index) * rows, rows), :]


def run_interior(meta, tile, left, right, probe, amps, tables, margin):
    tile_rows, tile_cols = tile.shape[1:]
    edge = probe.shape[-1]
    modes = probe.shape[1]
    blocks, rows = tile_cols // LANES + 2, tile_rows + 2 * margin
    return pl.pallas_call(
        functools.partial(interior_kernel, margin),
        out_shape=[
            shape(blocks, 2, rows, LANES),
            shape(blocks, 3, rows, LANES),
            shape(2 * modes + 1, edge, edge),
        ],
        in_specs=[IN_SMEM, ANYWHERE, ANYWHERE, ANYWHERE] + [IN_VMEM] * 4,
        out_specs=[IN_VMEM] * 3,
        scratch_shapes=[pltpu.SemaphoreType.DMA((blocks,))],
        compiler_params=pltpu.CompilerParams(vmem_limit_bytes=KERNEL_VMEM),
        cost_estimate=pl.CostEstimate(flops=int(1e10), bytes_accessed=20_000_000, transcendentals=0),
        name="slots_interior",
    )(meta, tile, left, right, probe, amps, tables[0], tables[1])


KERNEL_VMEM = 10 * MIB


def run_boundary(meta, top, bottom, corner_left, corner_right, probe, amps, tables, ext, acc, sums, margin):
    edge = probe.shape[-1]
    modes = probe.shape[1]
    part = shape(2 * modes + 1, edge // 2, edge)
    return pl.pallas_call(
        functools.partial(boundary_kernel, margin),
        out_shape=[
            shape(*ext.shape),
            shape(*acc.shape),
            shape(*acc.shape[1:]),
            shape(*acc.shape[1:]),
            part,
            part,
        ],
        in_specs=[IN_SMEM] + [ANYWHERE] * 4 + [IN_VMEM] * 7,
        out_specs=[IN_VMEM] * 6,
        scratch_shapes=[VMEM(sums.shape, F32), pltpu.SemaphoreType.DMA((2 * ext.shape[0],))],
        input_output_aliases={9: 0, 10: 1},
        compiler_params=pltpu.CompilerParams(vmem_limit_bytes=KERNEL_VMEM),
        cost_estimate=pl.CostEstimate(flops=int(1e10), bytes_accessed=20_000_000, transcendentals=0),
        name="slots_boundary",
    )(meta, top, bottom, corner_left, corner_right, probe, amps, tables[0], tables[1], ext, acc, sums)


def small_call(kernel, outs, in_specs, limit=4 * MIB, scratch=(), out_specs=None):
    return pl.pallas_call(
        kernel,
        out_shape=outs,
        in_specs=in_specs,
        out_specs=out_specs if out_specs is not None else [IN_VMEM] * len(outs),
        scratch_shapes=list(scratch),
        compiler_params=pltpu.CompilerParams(vmem_limit_bytes=limit),
    )


def fold_kernel(margin, acc, from_west, from_east, above, below):
    tiles = acc.shape[0] - 2
    rows = acc.shape[2]
    for out, part in ((above, pl.ds(0, margin)), (below, pl.ds(rows - margin, margin))):
        for t in range(tiles):
            value = acc[1 + t, :, part, :]
            if t == 0:
                value = value + from_west[:, part, :]
            if t == tiles - 1:
                value = value + from_east[:, part, :]
            out[t] = value


def object_kernel(margin, ext, acc, from_west, from_east, from_above, from_below, out, stage, sems):
    tiles = acc.shape[0] - 2
    tile_rows = acc.shape[2] - 2 * margin
    copies = []
    for t in range(tiles):
        for start in range(0, tile_rows, margin):
            rows = pl.ds(margin + start, margin)
            total = acc[1 + t, :, rows, :]
            if t == 0:
                total = total + from_west[:, rows, :]
            if t == tiles - 1:
                total = total + from_east[:, rows, :]
            if start == 0:
                total = total + from_above[t]
            if start == tile_rows - margin:
                total = total + from_below[t]
            scale = 1.0 / (total[2] + 1.0)
            for c in range(2):
                stage[t, c, pl.ds(start, margin), :] = ext[1 + t, c, rows, :] + total[c] * scale
        copy = pltpu.make_async_copy(stage.at[t], out.at[:, :, pl.ds(t * LANES, LANES)], sems.at[t])
        copy.start()
        copies.append(copy)
    for copy in copies:
        copy.wait()


def combine_kernel(inputs, stage, meta, *refs):
    ins, outs = refs[:inputs], refs[inputs:]
    index = meta[0, stage]
    rows = outs[0].shape[1]
    for member, out in enumerate(outs):
        part = aligned(jnp.bitwise_xor(index, member) * rows, rows)
        if len(outs) == 1:
            part = slice(None)
        value = ins[0][:, part, :]
        for other in ins[1:]:
            value = value + other[:, part, :]
        out[...] = value


def combine(places, stage, parts, group):
    planes, rows, cols = parts[0].shape
    if (rows // group) % 8:
        total = sum(parts[1:], parts[0])
        if group == 1:
            return [total]
        rows = rows // group
        return [
            lax.dynamic_slice_in_dim(total, jnp.bitwise_xor(places[0, stage], m) * rows, rows, axis=1)
            for m in range(group)
        ]
    return small_call(
        functools.partial(combine_kernel, len(parts), stage),
        [shape(planes, rows // group, cols)] * group,
        [IN_SMEM] + [IN_VMEM] * len(parts),
    )(places, *parts)


def place_kernel(group, stage, meta, *refs):
    ins, out = refs[:group], refs[group]
    index = meta[0, stage]
    rows = ins[0].shape[1]
    for member, piece in enumerate(ins):
        out[:, aligned(jnp.bitwise_xor(index, member) * rows, rows), :] = piece[...]


def place(places, stage, parts):
    planes, rows, cols = parts[0].shape
    if rows % 8:
        whole = jnp.zeros((planes, rows * len(parts), cols), F32)
        for m, piece in enumerate(parts):
            at = jnp.bitwise_xor(places[0, stage], m) * rows
            whole = lax.dynamic_update_slice_in_dim(whole, piece, at, axis=1)
        return whole
    return small_call(
        functools.partial(place_kernel, len(parts), stage),
        [shape(planes, rows * len(parts), cols)],
        [IN_SMEM] + [IN_VMEM] * len(parts),
    )(places, *parts)[0]


def finish_kernel(inputs, meta, probe, *refs):
    ins, out = refs[:inputs], refs[inputs]
    total = ins[0][...]
    for other in ins[1:]:
        total = total + other[...]
    planes, rows = out.shape[:2]
    old = probe[:, aligned(meta[1, 0], rows), :]
    out[...] = old + total[:planes] / (total[planes:] + 1.0)


def finish(places, probe, parts):
    planes, rows, cols = parts[0].shape
    if rows % 8:
        total = sum(parts[1:], parts[0])
        old = lax.dynamic_slice_in_dim(probe, places[1, 0], rows, axis=1)
        return old + total[:-1] / (total[-1:] + 1.0)
    return small_call(
        functools.partial(finish_kernel, len(parts)),
        [shape(planes - 1, rows, cols)],
        [IN_SMEM] + [IN_VMEM] * (1 + len(parts)),
    )(places, probe, *parts)[0]


def shift_both(low, high, axis):
    count = lax.axis_size(axis)
    up = [(i, i + 1) for i in range(count - 1)]
    down = [(i + 1, i) for i in range(count - 1)]
    from_low = lax.ppermute(high, axis, up)
    from_high = lax.ppermute(low, axis, down)
    return from_low, from_high


def member_perm(axis, bits, member):
    mask = sum(((member >> position) & 1) << bit for position, bit in enumerate(bits))
    return [(i, i ^ mask) for i in range(lax.axis_size(axis))]


def member_index(axis, bits):
    where = lax.axis_index(axis)
    return sum(((where >> bit) & 1) << position for position, bit in enumerate(bits))


def stages_of(rows, cols):
    stages = [("col", (bit,)) for bit in range(cols.bit_length() - 1)]
    bits = list(range(1, rows.bit_length() - 1))
    if len(bits) > 1:
        stages.append(("row", (bits[0], bits[1])))
        bits = bits[2:]
    stages += [("row", (bit,)) for bit in bits]
    return stages, ("row", (0,))


def step(object_field, probe_modes, scan_offsets, scan_counts, amplitudes):
    tile_rows, tile_cols = object_field.shape[1:]
    modes = probe_modes.shape[1]
    edge = probe_modes.shape[-1]
    margin = edge // 2
    slots = amplitudes.shape[2]
    stages, last = stages_of(lax.axis_size("row"), lax.axis_size("col"))

    top, bottom, left, right = pack_edges(object_field, margin)
    above, below = shift_both(top, bottom, "row")
    west, east = shift_both(left, right, "col")

    anchor = [
        lax.axis_index("row") * tile_rows - margin,
        lax.axis_index("col") * tile_cols - margin,
    ]
    indices = [member_index(axis, bits) for axis, bits in stages]
    offsets = scan_offsets[0, 0]
    row_of = offsets[0] - anchor[0]
    col_of = offsets[1] - anchor[1]
    counts = jnp.stack([scan_counts[0, 0], indices[0]] + [jnp.int32(0)] * (slots - 2))
    meta = jnp.stack([row_of, col_of, counts]).astype(jnp.int32)
    start, rows = jnp.int32(0), edge
    for index, (axis, bits) in zip(indices, stages):
        rows = rows >> len(bits)
        start = start + index * rows
    places = jnp.stack(
        [jnp.stack(indices), jnp.stack([start] + [jnp.int32(0)] * (len(stages) - 1))]
    ).astype(jnp.int32)

    tables = tuple(jnp.asarray(t) for t in dft_tables(edge))
    order = np.concatenate([np.arange(0, edge, 2), np.arange(1, edge, 2)])
    select = jnp.asarray(np.eye(edge)[order].astype(BF16))
    amps = jnp.einsum("ui,sij->suj", select, amplitudes[0, 0], preferred_element_type=BF16)
    amps = jnp.einsum("suj,vj->suv", amps, select, preferred_element_type=BF16)

    ext, acc, sums = run_interior(meta, object_field, west, east, probe_modes, amps, tables, margin)

    corners = jnp.stack([above, below])
    corner_west, corner_east = shift_both(
        corners[..., :margin], corners[..., tile_cols - margin :], "col"
    )

    ext, acc, fold_west, fold_east, keep, send = run_boundary(
        meta, above, below, corner_west, corner_east, probe_modes, amps, tables, ext, acc, sums, margin
    )

    parts = [keep]
    for number, (axis, bits) in enumerate(stages):
        if number:
            parts = combine(places, number, parts, 1 << len(bits))
            mine, pieces = parts[0], parts[1:]
        else:
            mine, pieces = keep, [send]
        parts = [mine] + [
            lax.ppermute(piece, axis, member_perm(axis, bits, member + 1))
            for member, piece in enumerate(pieces)
        ]
    total = combine(places, 0, parts, 1)[0] if len(parts) > 1 else parts[0]
    parts = [total, lax.ppermute(total, last[0], member_perm(*last, 1))]
    flat = probe_modes.reshape(2 * modes, edge, edge)
    shard = finish(places, flat, parts)
    for number, (axis, bits) in reversed(list(enumerate(stages))):
        pieces = [shard] + [
            lax.ppermute(shard, axis, member_perm(axis, bits, member))
            for member in range(1, 1 << len(bits))
        ]
        shard = place(places, number, pieces)
    probe_new = shard.reshape(probe_modes.shape)

    from_west, from_east = shift_both(fold_west, fold_east, "col")
    strip = shape(tile_cols // LANES, 3, margin, LANES)
    out_above, out_below = small_call(
        functools.partial(fold_kernel, margin), [strip, strip], [IN_VMEM] * 3
    )(acc, from_west, from_east)
    from_above, from_below = shift_both(out_above, out_below, "row")
    object_new = small_call(
        functools.partial(object_kernel, margin),
        [shape(2, tile_rows, tile_cols)],
        [IN_VMEM] * 6,
        limit=8 * MIB,
        scratch=(
            VMEM((tile_cols // LANES, 2, tile_rows, LANES), F32),
            pltpu.SemaphoreType.DMA((tile_cols // LANES,)),
        ),
        out_specs=[ANYWHERE],
    )(ext, acc, from_west, from_east, from_above, from_below)[0]
    return object_new, probe_new


def solution(mesh):
    in_specs = (
        P(None, "row", "col"),
        P(),
        P("row", "col", None, None),
        P("row", "col"),
        P("row", "col", None, None, None),
    )
    out_specs = (P(None, "row", "col"), P())
    return jax.shard_map(step, mesh=mesh, in_specs=in_specs, out_specs=out_specs, check_vma=False)
```

time: 484 us -> 152 us (0.31)
  the two profiles are of different devices: /device:TPU:0 before, /device:TPU:27 now
where the time goes in v2:
time: 152 us; the launch traced here: 151 us
  waiting for transfers between devices  57.4 us (38%)
  starting transfers between devices  49.9 us (33%)
  Pallas kernels  24.1 us (16%)
  local copies, waits for them, and re-layouts  15.6 us (10%)
  between operations  1.67 us (1%)
    ppermute x5, waiting for transfers between devices, step(): lax.ppermute(shard, axis, member_perm(axis, bits, member))  28.1 us
    ppermute x5, starting transfers between devices, shift_both(): from_high = lax.ppermute(low, axis, down)  22.6 us
    ppermute x5, waiting for transfers between devices, step(): lax.ppermute(piece, axis, member_perm(axis, bits, member + 1))  15.7 us
    unnamed x38, local copies, waits for them, and re-layouts  15.6 us
    ppermute x5, waiting for transfers between devices, shift_both(): from_high = lax.ppermute(low, axis, down)  12.3 us
    ppermute x5, starting transfers between devices, step(): lax.ppermute(shard, axis, member_perm(axis, bits, member))  11.5 us
    ppermute x5, starting transfers between devices, shift_both(): from_low = lax.ppermute(high, axis, up)  9.85 us
    pallas_call x1, Pallas kernels, run_boundary(): pl.pallas_call(functools.partial(boundary_kernel, margin), out_shape=[sha...  9.77 us
  transfers between devices with their start and end apart: 21, of which 11 were waited for; matrix products, arithmetic and copies ran while one was open for 2% of the time, Pallas kernels for 7%

profile of v2, /device:TPU:27, one launch (start us, length us, event | category | flops | bytes accessed | tf_op | source)
XLA Modules:
  0.0 151.4 jit_solution(7415119627369197160)
XLA Ops:
  0.7 1.7 %copy-done.6 = f32[2,512,512]{2,1,0:T(8,128)S(1)} copy-done((f32[2,512,512]{2,1,0:T(8,128)S(1)}, f32[2,512,512]{2,1,0:T(8,128)}, u32[]{:S(2)}) %copy-start.6) | copy-done | bytes 2097176
  2.3 1.6 %pack_edges.1 = (f32[2,128,512]{2,1,0:T(8,128)}, f32[2,128,512]{2,1,0:T(8,128)}, f32[2,512,128]{2,1,0:T(8,128)}, f32[2,512,128]{2,1,0:T(8,128)}) custom-call(f32[2,512,512]{2,1,0:T(8,128)S(1)} %copy-done.6), custom_call_target="tpu_custom_call" | custom-call | tf_op jit(solution)/shard_map/pack_edges/pallas_call | solution.py:106
  3.9 3.1 %collective-permute-start = (f32[2,128,512]{2,1,0:T(8,128)}, f32[2,128,512]{2,1,0:T(8,128)S(1)}, u32[]{:S(2)}, u32[]{:S(2)}) collective-permute-start(f32[2,128,512]{2,1,0:T(8,128)} %get-tuple-element.23), channel_id=1, source_target_pairs={{0,2},{2,4},{4,6},{6,8},{8,10},{10,12},{12,14},{14,16},{16,18},{18... | collective-permute-start | bytes 1572872 | tf_op jit(solution)/shard_map/ppermute | solution.py:476
  7.0 2.2 %collective-permute-start.1 = (f32[2,128,512]{2,1,0:T(8,128)}, f32[2,128,512]{2,1,0:T(8,128)}, u32[]{:S(2)}, u32[]{:S(2)}) collective-permute-start(f32[2,128,512]{2,1,0:T(8,128)} %get-tuple-element.24), channel_id=1, source_target_pairs={{2,0},{4,2},{6,4},{8,6},{10,8},{12,10},{14,12},{16,14},{18,16},{20... | collective-permute-start | bytes 1572872 | tf_op jit(solution)/shard_map/ppermute | solution.py:477
  10.5 4.7 %collective-permute-start.5 = (f32[2,512,128]{2,1,0:T(8,128)}, f32[2,512,128]{2,1,0:T(8,128)}, u32[]{:S(2)}, u32[]{:S(2)}) collective-permute-start(f32[2,512,128]{2,1,0:T(8,128)} %get-tuple-element.26), channel_id=1, source_target_pairs={{1,0},{3,2},{5,4},{7,6},{9,8},{11,10},{13,12},{15,14},{17,16},{19,... | collective-permute-start | bytes 1572872 | tf_op jit(solution)/shard_map/ppermute | solution.py:477
  16.0 1.5 fusion.amps
  17.5 1.3 collective-permute-done.top
  18.8 12.3 %collective-permute-done.1.bottom = f32[2,128,512]{2,1,0:T(8,128)} collective-permute-done((f32[2,128,512]{2,1,0:T(8,128)}, f32[2,128,512]{2,1,0:T(8,128)}, u32[]{:S(2)}, u32[]{:S(2)}) %collective-permute-start.1) | collective-permute-done | bytes 524320 | tf_op jit(solution)/shard_map/ppermute | solution.py:477
  32.1 3.5 %collective-permute-start.3 = (f32[2,2,128,128]{3,2,1,0:T(8,128)S(1)}, f32[2,2,128,128]{3,2,1,0:T(8,128)S(1)}, u32[]{:S(2)}, u32[]{:S(2)}) collective-permute-start(f32[2,2,128,128]{3,2,1,0:T(8,128)S(1)} %get-tuple-element.44), channel_id=1, source_target_pairs={{1,0},{3,2},{5,4},{7,6},{9,8},{11,10},{13,12},{15,14},{17,16},{19,... | collective-permute-start | bytes 786440 | tf_op jit(solution)/shard_map/ppermute | solution.py:477
  38.1 1.4 copy-done.14
  39.5 1.4 copy-done.15
  40.9 5.4 %slots_interior.1 = (f32[6,2,768,128]{3,2,1,0:T(8,128)S(1)}, f32[6,3,768,128]{3,2,1,0:T(8,128)S(1)}, f32[5,256,256]{2,1,0:T(8,128)S(1)}) custom-call(s32[3,6]{1,0:T(4,128)S(1)} %pad_add_fusion.meta, f32[2,512,512]{2,1,0:T(8,128)S(1)} %copy-done.7, f32[2,512,128]{2,1,0:T(8,128)} %collective-permute-done.4.left, f32[2,512,128]{2,1,0:T(8,128)} %collective-permute-done.5.right, ...), custom_call_target="tpu_custom_call" | custom-call | flops 10000000000 | bytes 20000000 | tf_op jit(solution)/shard_map/slots_interior/pallas_call | solution.py:301
  46.4 9.8 %slots_boundary.1 = (f32[6,2,768,128]{3,2,1,0:T(8,128)S(1)}, f32[6,3,768,128]{3,2,1,0:T(8,128)S(1)}, f32[3,768,128]{2,1,0:T(8,128)}, f32[3,768,128]{2,1,0:T(8,12...) custom-call(s32[3,6]{1,0:T(4,128)S(1)} %pad_add_fusion.meta, ...), custom_call_target="tpu_custom_call", output_to_operand_aliasing={{0}: (9, {}), {1}: (10, {})} | custom-call | flops 10000000000 | bytes 20000000 | tf_op jit(solution)/shard_map/slots_boundary/pallas_call | solution.py:324
  56.2 2.8 %copy-done.1 = f32[6,3,768,128]{3,2,1,0:T(8,128)} copy-done((f32[6,3,768,128]{3,2,1,0:T(8,128)}, f32[6,3,768,128]{3,2,1,0:T(8,128)S(1)}, u32[]{:S(2)}) %copy-start.1) | copy-done | bytes 7077912
  59.0 2.1 %copy-done.4 = f32[6,2,768,128]{3,2,1,0:T(8,128)} copy-done((f32[6,2,768,128]{3,2,1,0:T(8,128)}, f32[6,2,768,128]{3,2,1,0:T(8,128)S(1)}, u32[]{:S(2)}) %copy-start.4) | copy-done | bytes 4718616
  63.3 9.4 %collective-permute-start.7 = (f32[3,768,128]{2,1,0:T(8,128)}, f32[3,768,128]{2,1,0:T(8,128)S(1)}, u32[]{:S(2)}, u32[]{:S(2)}) collective-permute-start(f32[3,768,128]{2,1,0:T(8,128)} %get-tuple-element.33), channel_id=1, source_target_pairs={{1,0},{3,2},{5,4},{7,6},{9,8},{11,10},{13,12},{15,14},{17,16},{19,... | collective-permute-start | bytes 3538952 | tf_op jit(solution)/shard_map/ppermute | solution.py:477
  72.9 3.5 %collective-permute-done.10.refs_1_ = f32[5,128,256]{2,1,0:T(8,128)} collective-permute-done((f32[5,128,256]{2,1,0:T(8,128)}, f32[5,128,256]{2,1,0:T(8,128)}, u32[]{:S(2)}, u32[]{:S(2)}) %collective-permute-start.10) | collective-permute-done | bytes 655392 | tf_op jit(solution)/shard_map/ppermute | solution.py:556
  78.9 2.6 %collective-permute-start.13 = (f32[5,32,256]{2,1,0:T(8,128)S(1)}, f32[5,32,256]{2,1,0:T(8,128)S(1)}, u32[]{:S(2)}, u32[]{:S(2)}) collective-permute-start(f32[5,32,256]{2,1,0:T(8,128)S(1)} %get-tuple-element.41), channel_id=1, source_target_pairs={{0,12},{2,14},{4,8},{6,10},{8,4},{10,6},{12,0},{14,2},{16,28},{18,... | collective-permute-start | bytes 491528 | tf_op jit(solution)/shard_map/ppermute | solution.py:556
  81.4 2.7 %collective-permute-done.11.refs_1_ = f32[5,32,256]{2,1,0:T(8,128)S(1)} collective-permute-done((f32[5,32,256]{2,1,0:T(8,128)S(1)}, f32[5,32,256]{2,1,0:T(8,128)S(1)}, u32[]{:S(2)}, u32[]{:S(2)}) %collective-permute-start.11) | collective-permute-done | bytes 163872 | tf_op jit(solution)/shard_map/ppermute | solution.py:556
  84.2 4.3 %collective-permute-done.13.refs_3_ = f32[5,32,256]{2,1,0:T(8,128)S(1)} collective-permute-done((f32[5,32,256]{2,1,0:T(8,128)S(1)}, f32[5,32,256]{2,1,0:T(8,128)S(1)}, u32[]{:S(2)}, u32[]{:S(2)}) %collective-permute-start.13) | collective-permute-done | bytes 163872 | tf_op jit(solution)/shard_map/ppermute | solution.py:556
  89.2 5.1 %collective-permute-done.14.refs_1_ = f32[5,16,256]{2,1,0:T(8,128)S(1)} collective-permute-done((f32[5,16,256]{2,1,0:T(8,128)S(1)}, f32[5,16,256]{2,1,0:T(8,128)S(1)}, u32[]{:S(2)}, u32[]{:S(2)}) %collective-permute-start.14) | collective-permute-done | bytes 81952 | tf_op jit(solution)/shard_map/ppermute | solution.py:556
  94.9 3.2 %collective-permute-start.15 = (f32[5,16,256]{2,1,0:T(8,128)S(1)}, f32[5,16,256]{2,1,0:T(8,128)S(1)}, u32[]{:S(2)}, u32[]{:S(2)}) collective-permute-start(f32[5,16,256]{2,1,0:T(8,128)S(1)} %shard_map.99.refs_0_), channel_id=1, source_target_pairs={{0,2},{2,0},{4,6},{6,4},{8,10},{10,8},{12,14},{14,12},{16,18},{18,... | collective-permute-start | bytes 245768 | tf_op jit(solution)/shard_map/ppermute | solution.py:560
  98.1 3.0 %copy-done.2 = f32[6,3,768,128]{3,2,1,0:T(8,128)S(1)} copy-done((f32[6,3,768,128]{3,2,1,0:T(8,128)S(1)}, f32[6,3,768,128]{3,2,1,0:T(8,128)}, u32[]{:S(2)}) %copy-start.2) | copy-done | bytes 7077912
  101.2 2.9 %collective-permute-start.8 = (f32[4,3,128,128]{3,2,1,0:T(8,128)S(1)}, f32[4,3,128,128]{3,2,1,0:T(8,128)S(1)}, u32[]{:S(2)}, u32[]{:S(2)}) collective-permute-start(f32[4,3,128,128]{3,2,1,0:T(8,128)S(1)} %get-tuple-element.34), channel_id=1, source_target_pairs={{0,2},{2,4},{4,6},{6,8},{8,10},{10,12},{12,14},{14,16},{16,18},{18... | collective-permute-start | bytes 2359304 | tf_op jit(solution)/shard_map/ppermute | solution.py:476
  104.1 2.8 %collective-permute-start.9 = (f32[4,3,128,128]{3,2,1,0:T(8,128)S(1)}, f32[4,3,128,128]{3,2,1,0:T(8,128)S(1)}, u32[]{:S(2)}, u32[]{:S(2)}) collective-permute-start(f32[4,3,128,128]{3,2,1,0:T(8,128)S(1)} %get-tuple-element.35), channel_id=1, source_target_pairs={{2,0},{4,2},{6,4},{8,6},{10,8},{12,10},{14,12},{16,14},{18,16},{20... | collective-permute-start | bytes 2359304 | tf_op jit(solution)/shard_map/ppermute | solution.py:477
  107.6 4.0 %collective-permute-done.16.refs_1_ = f32[4,16,256]{2,1,0:T(8,128)S(1)} collective-permute-done((f32[4,16,256]{2,1,0:T(8,128)S(1)}, f32[4,16,256]{2,1,0:T(8,128)S(1)}, u32[]{:S(2)}, u32[]{:S(2)}) %collective-permute-start.16) | collective-permute-done | bytes 65568 | tf_op jit(solution)/shard_map/ppermute | solution.py:565
  112.2 10.5 %collective-permute-start.19 = (f32[4,32,256]{2,1,0:T(8,128)S(1)}, f32[4,32,256]{2,1,0:T(8,128)S(1)}, u32[]{:S(2)}, u32[]{:S(2)}) collective-permute-start(f32[4,32,256]{2,1,0:T(8,128)S(1)} %shard_map.101.refs_0_), channel_id=1, source_target_pairs={{0,12},{2,14},{4,8},{6,10},{8,4},{10,6},{12,0},{14,2},{16,28},{18,... | collective-permute-start | bytes 393224 | tf_op jit(solution)/shard_map/ppermute | solution.py:565
  123.0 4.2 %collective-permute-done.19.refs_3_ = f32[4,32,256]{2,1,0:T(8,128)S(1)} collective-permute-done((f32[4,32,256]{2,1,0:T(8,128)S(1)}, f32[4,32,256]{2,1,0:T(8,128)S(1)}, u32[]{:S(2)}, u32[]{:S(2)}) %collective-permute-start.19) | collective-permute-done | bytes 131104 | tf_op jit(solution)/shard_map/ppermute | solution.py:565
  127.2 18.4 %collective-permute-done.17.refs_1_ = f32[4,32,256]{2,1,0:T(8,128)S(1)} collective-permute-done((f32[4,32,256]{2,1,0:T(8,128)S(1)}, f32[4,32,256]{2,1,0:T(8,128)S(1)}, u32[]{:S(2)}, u32[]{:S(2)}) %collective-permute-start.17) | collective-permute-done | bytes 131104 | tf_op jit(solution)/shard_map/ppermute | solution.py:565
  146.7 1.5 %collective-permute-done.20.refs_1_ = f32[4,128,256]{2,1,0:T(8,128)S(1)} collective-permute-done((f32[4,128,256]{2,1,0:T(8,128)S(1)}, f32[4,128,256]{2,1,0:T(8,128)S(1)}, u32[]{:S(2)}, u32[]{:S(2)}) %collective-permute-start.20) | collective-permute-done | bytes 524320 | tf_op jit(solution)/shard_map/ppermute | solution.py:565
  148.3 1.6 %shard_map.103 = f32[4,256,256]{2,1,0:T(8,128)} custom-call(s32[2,3]{1,0:T(2,128)S(1)} %pad_add_fusion.1.meta, f32[4,128,256]{2,1,0:T(8,128)S(1)} %shard_map.102.refs_0_, f32[4,128,256]{2,1,0:T(8,128)S(1)} %collective-permute-done.20.refs_1_), custom_call_target="tpu_custom_call" | custom-call | tf_op jit(solution)/shard_map/pallas_call | solution.py:442
  149.9 1.5 shard_map.96
  (68 shorter events, 13.8 us)
Async XLA Ops:
  0.6 15.4 %copy-start = (bf16[1,1,6,256,256]{4,3,2,1,0:T(8,128)(2,1)S(1)}, bf16[1,1,6,256,256]{4,3,2,1,0:T(8,128)(2,1)}, u32[]{:S(2)}) copy-start(bf16[1,1,6,256,256]{4,3,2,1,0:T(8,128)(2,1)} %param.12) | copy-start | bytes 2359300
  2.3 12.9 %copy-start.18 = (s32[1,1,2,6]{3,2,1,0:T(2,128)S(1)}, s32[1,1,2,6]{3,2,1,0:T(2,128)}, u32[]{:S(2)}) copy-start(s32[1,1,2,6]{3,2,1,0:T(2,128)} %param.10) | copy-start | bytes 148
  2.3 13.7 %copy-start.17 = (bf16[256,256,1]{1,0,2:T(8,128)(2,1)S(1)}, bf16[256,256,1]{1,0,2:T(8,128)(2,1)}, u32[]{:S(2)}) copy-start(bf16[256,256,1]{1,0,2:T(8,128)(2,1)} %constant.43) | copy-start | bytes 393220
  3.9 14.9 %collective-permute-start = (f32[2,128,512]{2,1,0:T(8,128)}, f32[2,128,512]{2,1,0:T(8,128)S(1)}, u32[]{:S(2)}, u32[]{:S(2)}) collective-permute-start(f32[2,128,512]{2,1,0:T(8,128)} %get-tuple-element.23), channel_id=1, source_target_pairs={{0,2},{2,4},{4,6},{6,8},{8,10},{10,12},{12,14},{14,16},{16,18},{18... | collective-permute-start | bytes 1572872 | tf_op jit(solution)/shard_map/ppermute | solution.py:476
  7.0 24.1 %collective-permute-start.1 = (f32[2,128,512]{2,1,0:T(8,128)}, f32[2,128,512]{2,1,0:T(8,128)}, u32[]{:S(2)}, u32[]{:S(2)}) collective-permute-start(f32[2,128,512]{2,1,0:T(8,128)} %get-tuple-element.24), channel_id=1, source_target_pairs={{2,0},{4,2},{6,4},{8,6},{10,8},{12,10},{14,12},{16,14},{18,16},{20... | collective-permute-start | bytes 1572872 | tf_op jit(solution)/shard_map/ppermute | solution.py:477
  9.2 27.7 %collective-permute-start.4 = (f32[2,512,128]{2,1,0:T(8,128)}, f32[2,512,128]{2,1,0:T(8,128)}, u32[]{:S(2)}, u32[]{:S(2)}) collective-permute-start(f32[2,512,128]{2,1,0:T(8,128)} %get-tuple-element.25), channel_id=1, source_target_pairs={{0,1},{2,3},{4,5},{6,7},{8,9},{10,11},{12,13},{14,15},{16,17},{18,... | collective-permute-start | bytes 1572872 | tf_op jit(solution)/shard_map/ppermute | solution.py:476
  10.5 26.4 %collective-permute-start.5 = (f32[2,512,128]{2,1,0:T(8,128)}, f32[2,512,128]{2,1,0:T(8,128)}, u32[]{:S(2)}, u32[]{:S(2)}) collective-permute-start(f32[2,512,128]{2,1,0:T(8,128)} %get-tuple-element.26), channel_id=1, source_target_pairs={{1,0},{3,2},{5,4},{7,6},{9,8},{11,10},{13,12},{15,14},{17,16},{19,... | collective-permute-start | bytes 1572872 | tf_op jit(solution)/shard_map/ppermute | solution.py:477
  16.0 20.9 %copy-start.7 = (f32[2,512,512]{2,1,0:T(8,128)S(1)}, f32[2,512,512]{2,1,0:T(8,128)}, u32[]{:S(2)}) copy-start(f32[2,512,512]{2,1,0:T(8,128)} %tile.3) | copy-start | bytes 6291460
  17.5 19.4 %copy-start.8 = (f32[2,2,256,256]{3,2,1,0:T(8,128)S(1)}, f32[2,2,256,256]{3,2,1,0:T(8,128)}, u32[]{:S(2)}) copy-start(f32[2,2,256,256]{3,2,1,0:T(8,128)} %probe.3) | copy-start | bytes 3145732
  32.1 14.2 %collective-permute-start.3 = (f32[2,2,128,128]{3,2,1,0:T(8,128)S(1)}, f32[2,2,128,128]{3,2,1,0:T(8,128)S(1)}, u32[]{:S(2)}, u32[]{:S(2)}) collective-permute-start(f32[2,2,128,128]{3,2,1,0:T(8,128)S(1)} %get-tuple-element.44), channel_id=1, source_target_pairs={{1,0},{3,2},{5,4},{7,6},{9,8},{11,10},{13,12},{15,14},{17,16},{19,... | collective-permute-start | bytes 786440 | tf_op jit(solution)/shard_map/ppermute | solution.py:477
  35.6 10.8 %collective-permute-start.2 = (f32[2,2,128,128]{3,2,1,0:T(8,128)S(1)}, f32[2,2,128,128]{3,2,1,0:T(8,128)S(1)}, u32[]{:S(2)}, u32[]{:S(2)}) collective-permute-start(f32[2,2,128,128]{3,2,1,0:T(8,128)S(1)} %get-tuple-element.45), channel_id=1, source_target_pairs={{0,1},{2,3},{4,5},{6,7},{8,9},{10,11},{12,13},{14,15},{16,17},{18,... | collective-permute-start | bytes 786440 | tf_op jit(solution)/shard_map/ppermute | solution.py:476
  40.9 5.5 %copy-start.11 = (bf16[6,256,256]{2,1,0:T(8,128)(2,1)S(1)}, bf16[6,256,256]{2,1,0:T(8,128)(2,1)}, u32[]{:S(2)}) copy-start(bf16[6,256,256]{2,1,0:T(8,128)(2,1)} %fusion.amps) | copy-start | bytes 2359300
  40.9 5.5 %copy-start.16 = (bf16[4,768,256]{2,1,0:T(8,128)(2,1)S(1)}, bf16[4,768,256]{2,1,0:T(8,128)(2,1)}, u32[]{:S(2)}) copy-start(bf16[4,768,256]{2,1,0:T(8,128)(2,1)} %constant.35.clone.rights) | copy-start | bytes 4718596
  62.0 36.1 %collective-permute-start.6 = (f32[3,768,128]{2,1,0:T(8,128)}, f32[3,768,128]{2,1,0:T(8,128)S(1)}, u32[]{:S(2)}, u32[]{:S(2)}) collective-permute-start(f32[3,768,128]{2,1,0:T(8,128)} %get-tuple-element.32), channel_id=1, source_target_pairs={{0,1},{2,3},{4,5},{6,7},{8,9},{10,11},{12,13},{14,15},{16,17},{18,... | collective-permute-start | bytes 3538952 | tf_op jit(solution)/shard_map/ppermute | solution.py:476
  63.3 34.8 %collective-permute-start.7 = (f32[3,768,128]{2,1,0:T(8,128)}, f32[3,768,128]{2,1,0:T(8,128)S(1)}, u32[]{:S(2)}, u32[]{:S(2)}) collective-permute-start(f32[3,768,128]{2,1,0:T(8,128)} %get-tuple-element.33), channel_id=1, source_target_pairs={{1,0},{3,2},{5,4},{7,6},{9,8},{11,10},{13,12},{15,14},{17,16},{19,... | collective-permute-start | bytes 3538952 | tf_op jit(solution)/shard_map/ppermute | solution.py:477
  72.7 3.7 %collective-permute-start.10 = (f32[5,128,256]{2,1,0:T(8,128)}, f32[5,128,256]{2,1,0:T(8,128)}, u32[]{:S(2)}, u32[]{:S(2)}) collective-permute-start(f32[5,128,256]{2,1,0:T(8,128)} %get-tuple-element.37), channel_id=1, source_target_pairs={{0,1},{1,0},{2,3},{3,2},{4,5},{5,4},{6,7},{7,6},{8,9},{9,8},{10,11... | collective-permute-start | bytes 1966088 | tf_op jit(solution)/shard_map/ppermute | solution.py:556
  77.4 29.5 %copy-start.9 = (f32[2,2,256,256]{3,2,1,0:T(8,128)S(1)}, f32[2,2,256,256]{3,2,1,0:T(8,128)}, u32[]{:S(2)}) copy-start(f32[2,2,256,256]{3,2,1,0:T(8,128)} %probe.3) | copy-start | bytes 3145732
  78.7 5.5 %collective-permute-start.11 = (f32[5,32,256]{2,1,0:T(8,128)S(1)}, f32[5,32,256]{2,1,0:T(8,128)S(1)}, u32[]{:S(2)}, u32[]{:S(2)}) collective-permute-start(f32[5,32,256]{2,1,0:T(8,128)S(1)} %get-tuple-element.39), channel_id=1, source_target_pairs={{0,4},{2,6},{4,0},{6,2},{8,12},{10,14},{12,8},{14,10},{16,20},{18,... | collective-permute-start | bytes 491528 | tf_op jit(solution)/shard_map/ppermute | solution.py:556
  78.8 5.5 %collective-permute-start.12 = (f32[5,32,256]{2,1,0:T(8,128)S(1)}, f32[5,32,256]{2,1,0:T(8,128)S(1)}, u32[]{:S(2)}, u32[]{:S(2)}) collective-permute-start(f32[5,32,256]{2,1,0:T(8,128)S(1)} %get-tuple-element.40), channel_id=1, source_target_pairs={{0,8},{2,10},{4,12},{6,14},{8,0},{10,2},{12,4},{14,6},{16,24},{18,... | collective-permute-start | bytes 491528 | tf_op jit(solution)/shard_map/ppermute | solution.py:556
  78.9 9.7 %collective-permute-start.13 = (f32[5,32,256]{2,1,0:T(8,128)S(1)}, f32[5,32,256]{2,1,0:T(8,128)S(1)}, u32[]{:S(2)}, u32[]{:S(2)}) collective-permute-start(f32[5,32,256]{2,1,0:T(8,128)S(1)} %get-tuple-element.41), channel_id=1, source_target_pairs={{0,12},{2,14},{4,8},{6,10},{8,4},{10,6},{12,0},{14,2},{16,28},{18,... | collective-permute-start | bytes 491528 | tf_op jit(solution)/shard_map/ppermute | solution.py:556
  89.2 5.1 %collective-permute-start.14 = (f32[5,16,256]{2,1,0:T(8,128)S(1)}, f32[5,16,256]{2,1,0:T(8,128)S(1)}, u32[]{:S(2)}, u32[]{:S(2)}) collective-permute-start(f32[5,16,256]{2,1,0:T(8,128)S(1)} %get-tuple-element.43), channel_id=1, source_target_pairs={{0,16},{2,18},{4,20},{6,22},{8,24},{10,26},{12,28},{14,30},{16,0},... | collective-permute-start | bytes 245768 | tf_op jit(solution)/shard_map/ppermute | solution.py:556
  94.9 12.0 %collective-permute-start.15 = (f32[5,16,256]{2,1,0:T(8,128)S(1)}, f32[5,16,256]{2,1,0:T(8,128)S(1)}, u32[]{:S(2)}, u32[]{:S(2)}) collective-permute-start(f32[5,16,256]{2,1,0:T(8,128)S(1)} %shard_map.99.refs_0_), channel_id=1, source_target_pairs={{0,2},{2,0},{4,6},{6,4},{8,10},{10,8},{12,14},{14,12},{16,18},{18,... | collective-permute-start | bytes 245768 | tf_op jit(solution)/shard_map/ppermute | solution.py:560
  98.1 3.0 %copy-start.2 = (f32[6,3,768,128]{3,2,1,0:T(8,128)S(1)}, f32[6,3,768,128]{3,2,1,0:T(8,128)}, u32[]{:S(2)}) copy-start(f32[6,3,768,128]{3,2,1,0:T(8,128)} %copy-done.1) | copy-start | bytes 21233668
  101.1 48.8 %copy-start.3 = (f32[6,3,768,128]{3,2,1,0:T(8,128)S(1)}, f32[6,3,768,128]{3,2,1,0:T(8,128)}, u32[]{:S(2)}) copy-start(f32[6,3,768,128]{3,2,1,0:T(8,128)} %copy-done.1) | copy-start | bytes 21233668
  101.1 48.8 %copy-start.5 = (f32[6,2,768,128]{3,2,1,0:T(8,128)S(1)}, f32[6,2,768,128]{3,2,1,0:T(8,128)}, u32[]{:S(2)}) copy-start(f32[6,2,768,128]{3,2,1,0:T(8,128)} %copy-done.4) | copy-start | bytes 14155780
  101.2 48.7 %collective-permute-start.8 = (f32[4,3,128,128]{3,2,1,0:T(8,128)S(1)}, f32[4,3,128,128]{3,2,1,0:T(8,128)S(1)}, u32[]{:S(2)}, u32[]{:S(2)}) collective-permute-start(f32[4,3,128,128]{3,2,1,0:T(8,128)S(1)} %get-tuple-element.34), channel_id=1, source_target_pairs={{0,2},{2,4},{4,6},{6,8},{8,10},{10,12},{12,14},{14,16},{16,18},{18... | collective-permute-start | bytes 2359304 | tf_op jit(solution)/shard_map/ppermute | solution.py:476
  104.1 45.8 %collective-permute-start.9 = (f32[4,3,128,128]{3,2,1,0:T(8,128)S(1)}, f32[4,3,128,128]{3,2,1,0:T(8,128)S(1)}, u32[]{:S(2)}, u32[]{:S(2)}) collective-permute-start(f32[4,3,128,128]{3,2,1,0:T(8,128)S(1)} %get-tuple-element.35), channel_id=1, source_target_pairs={{2,0},{4,2},{6,4},{8,6},{10,8},{12,10},{14,12},{16,14},{18,16},{20... | collective-permute-start | bytes 2359304 | tf_op jit(solution)/shard_map/ppermute | solution.py:477
  107.5 4.1 %collective-permute-start.16 = (f32[4,16,256]{2,1,0:T(8,128)S(1)}, f32[4,16,256]{2,1,0:T(8,128)S(1)}, u32[]{:S(2)}, u32[]{:S(2)}) collective-permute-start(f32[4,16,256]{2,1,0:T(8,128)S(1)} %shard_map.100.refs_0_), channel_id=1, source_target_pairs={{0,16},{2,18},{4,20},{6,22},{8,24},{10,26},{12,28},{14,30},{16,0},... | collective-permute-start | bytes 196616 | tf_op jit(solution)/shard_map/ppermute | solution.py:565
  112.2 15.0 %collective-permute-start.19 = (f32[4,32,256]{2,1,0:T(8,128)S(1)}, f32[4,32,256]{2,1,0:T(8,128)S(1)}, u32[]{:S(2)}, u32[]{:S(2)}) collective-permute-start(f32[4,32,256]{2,1,0:T(8,128)S(1)} %shard_map.101.refs_0_), channel_id=1, source_target_pairs={{0,12},{2,14},{4,8},{6,10},{8,4},{10,6},{12,0},{14,2},{16,28},{18,... | collective-permute-start | bytes 393224 | tf_op jit(solution)/shard_map/ppermute | solution.py:565
  122.6 4.5 %collective-permute-start.18 = (f32[4,32,256]{2,1,0:T(8,128)S(1)}, f32[4,32,256]{2,1,0:T(8,128)S(1)}, u32[]{:S(2)}, u32[]{:S(2)}) collective-permute-start(f32[4,32,256]{2,1,0:T(8,128)S(1)} %shard_map.101.refs_0_), channel_id=1, source_target_pairs={{0,8},{2,10},{4,12},{6,14},{8,0},{10,2},{12,4},{14,6},{16,24},{18,... | collective-permute-start | bytes 393224 | tf_op jit(solution)/shard_map/ppermute | solution.py:565
  122.7 22.9 %collective-permute-start.17 = (f32[4,32,256]{2,1,0:T(8,128)S(1)}, f32[4,32,256]{2,1,0:T(8,128)S(1)}, u32[]{:S(2)}, u32[]{:S(2)}) collective-permute-start(f32[4,32,256]{2,1,0:T(8,128)S(1)} %shard_map.101.refs_0_), channel_id=1, source_target_pairs={{0,4},{2,6},{4,0},{6,2},{8,12},{10,14},{12,8},{14,10},{16,20},{18,... | collective-permute-start | bytes 393224 | tf_op jit(solution)/shard_map/ppermute | solution.py:565
  146.2 2.1 %collective-permute-start.20 = (f32[4,128,256]{2,1,0:T(8,128)S(1)}, f32[4,128,256]{2,1,0:T(8,128)S(1)}, u32[]{:S(2)}, u32[]{:S(2)}) collective-permute-start(f32[4,128,256]{2,1,0:T(8,128)S(1)} %shard_map.102.refs_0_), channel_id=1, source_target_pairs={{0,1},{1,0},{2,3},{3,2},{4,5},{5,4},{6,7},{7,6},{8,9},{9,8},{10,11... | collective-permute-start | bytes 1572872 | tf_op jit(solution)/shard_map/ppermute | solution.py:565
  (8 other events, 12.5 us)

commit v3 on v2

v3 whole, which is shorter than its diff:
```python
import functools
import math

import jax
import jax.numpy as jnp
import numpy as np
from jax import lax
from jax.experimental import pallas as pl
from jax.experimental.pallas import tpu as pltpu
from jax.sharding import PartitionSpec as P


F32 = jnp.float32
BF16 = jnp.bfloat16
LANES = 128


def split_host(table):
    high = table.astype(BF16)
    low = (table - high.astype(np.float64)).astype(BF16)
    return high, low


def dft_tables(edge):
    half = edge // 2
    scale = 1.0 / math.sqrt(edge)
    n = np.arange(half)[:, None]
    k = np.arange(half)[None, :]
    right, left = [], []
    for parity in (0, 1):
        angle = (n * (2 * k + parity) % edge) * (2.0 * np.pi / edge)
        cosine, sine = np.cos(angle) * scale, np.sin(angle) * scale
        w = np.block([[cosine, -sine], [sine, cosine]])
        right.append(w)
        left.append(w.T)
    mats = [right[0], right[1], left[0], left[1]]
    as_right = []
    as_left = []
    for m in mats:
        high, low = split_host(m)
        as_right.append(np.concatenate([high, high, low], axis=0))
        as_left.append(np.concatenate([high, high, low], axis=1))
    return (
        np.stack([as_right[0], as_right[1], as_right[2], as_right[3]]),
        np.stack([as_left[2], as_left[3], as_left[0], as_left[1]]),
    )


def split_parts(x):
    high = x.astype(BF16)
    low = (x - high.astype(F32)).astype(BF16)
    return high, low


def right_dot(x, table):
    high, low = split_parts(x)
    return jnp.dot(jnp.concatenate([high, low, high], axis=1), table, preferred_element_type=F32)


def left_dot(table, x):
    high, low = split_parts(x)
    return jnp.dot(table, jnp.concatenate([high, low, high], axis=0), preferred_element_type=F32)


VMEM = pltpu.VMEM
ANYWHERE = pl.BlockSpec(memory_space=pl.ANY)
IN_VMEM = pl.BlockSpec(memory_space=pltpu.VMEM)
IN_SMEM = pl.BlockSpec(memory_space=pltpu.SMEM)
MIB = 1024 * 1024
IN_HBM = pl.BlockSpec(memory_space=pltpu.HBM)


def in_hbm(x):
    return pltpu.with_memory_space_constraint(x, pltpu.HBM)


def shape(*dims):
    return jax.ShapeDtypeStruct(dims, F32)


def aligned(start, size):
    return pl.ds(pl.multiple_of(start, size) if size % 8 == 0 else start, size)


def copy_all(pairs, sems):
    copies = []
    for number, (src, dst) in enumerate(pairs):
        copy = pltpu.make_async_copy(src, dst, sems.at[number])
        copy.start()
        copies.append(copy)
    return copies


class Frame:
    def __init__(self, tile_rows, tile_cols, margin, sides):
        self.tile_rows, self.tile_cols, self.margin, self.sides = tile_rows, tile_cols, margin, sides
        self.tiles = tile_cols // LANES
        self.row = lax.axis_index("row")
        self.col = lax.axis_index("col")
        self.body = pl.ds(margin, tile_rows)

    def side_is_east(self, number):
        if self.sides == 2:
            return jnp.int32(number)
        return 1 - (self.col & 1)

    def side_block(self, number):
        return self.side_is_east(number) * (self.tiles + 1)

    def side_target(self, number):
        return 1 + self.side_is_east(number) * (self.tiles - 1)

    def side_cols(self, number):
        start = self.side_is_east(number) * (self.tile_cols - self.margin)
        return pl.ds(pl.multiple_of(start, LANES), self.margin)

    def is_below(self, number):
        return jnp.bitwise_xor(1 - (self.row & 1), number)

    def strip_rows(self, number):
        start = self.is_below(number) * (self.tile_rows - self.margin)
        return pl.ds(pl.multiple_of(start, self.margin), self.margin)

    def halo_rows(self, number):
        start = self.is_below(number) * (self.tile_rows + self.margin)
        return pl.ds(pl.multiple_of(start, self.margin), self.margin)

    def place_of(self, offsets, slot):
        return (
            offsets[0, 0, 0, slot] - self.row * self.tile_rows + self.margin,
            offsets[0, 0, 1, slot] - self.col * self.tile_cols + self.margin,
        )


def small_call(kernel, outs, in_specs, limit=4 * MIB, scratch=(), out_specs=None, aliases=None, cost=None):
    return pl.pallas_call(
        kernel,
        out_shape=outs,
        in_specs=in_specs,
        out_specs=out_specs if out_specs is not None else [IN_VMEM] * len(outs),
        scratch_shapes=list(scratch),
        input_output_aliases=aliases or {},
        compiler_params=pltpu.CompilerParams(vmem_limit_bytes=limit),
        cost_estimate=pl.CostEstimate(flops=cost, bytes_accessed=1_000_000, transcendentals=0) if cost else None,
    )


def pack_kernel(geometry, tile, straight, diagonal, *refs):
    sides, sems = refs[:-1], refs[-1]
    frame = Frame(*geometry)
    pairs = [
        (tile.at[:, frame.strip_rows(0), :], straight),
        (tile.at[:, frame.strip_rows(1), :], diagonal),
    ]
    for number, side in enumerate(sides):
        pairs.append((tile.at[:, :, frame.side_cols(number)], side))
    for copy in copy_all(pairs, sems):
        copy.wait()


def add_window(acc, channel, parts, row, block, shift):
    edge = parts[0].shape[0]
    lane = lax.broadcasted_iota(jnp.int32, (edge, LANES), 1)
    keep = lane >= shift
    first = pltpu.roll(parts[0], shift, 1)
    second = pltpu.roll(parts[1], shift, 1)
    rows = pl.ds(row, edge)
    zero = jnp.zeros_like(first)
    last = jnp.minimum(block + 2, acc.shape[0] - 1)
    acc[block, channel, rows, :] += jnp.where(keep, first, zero)
    acc[block + 1, channel, rows, :] += jnp.where(keep, second, first)
    acc[last, channel, rows, :] += jnp.where(keep, zero, second)


def slot_body(slot, row, col, ext, acc, sums, probe, amps, rights, lefts):
    edge = probe.shape[-1]
    modes = probe.shape[1]
    half = edge // 2
    block = col // LANES
    shift = col - block * LANES
    lane = lax.broadcasted_iota(jnp.int32, (edge, LANES), 1)
    back_shift = lax.rem(LANES - shift, LANES)
    keep = lane < LANES - shift
    last = jnp.minimum(block + 2, ext.shape[0] - 1)
    patch = []
    for c in range(2):
        rolled = [
            pltpu.roll(ext[b, c, pl.ds(row, edge), :], back_shift, 1) for b in (block, block + 1, last)
        ]
        patch.append([jnp.where(keep, rolled[t], rolled[t + 1]) for t in range(2)])

    def probe_at(c, k, t):
        return probe[c, k, :, pl.ds(t * LANES, LANES)]

    evens, odds = [], []
    for k in range(modes):
        re = [probe_at(0, k, t) * patch[0][t] - probe_at(1, k, t) * patch[1][t] for t in range(2)]
        im = [probe_at(0, k, t) * patch[1][t] + probe_at(1, k, t) * patch[0][t] for t in range(2)]
        evens.append(right_dot(jnp.concatenate([re[0] + re[1], im[0] + im[1]], axis=1), rights[0]))
        odds.append(right_dot(jnp.concatenate([re[0] - re[1], im[0] - im[1]], axis=1), rights[1]))
    far = []
    for k in range(modes):
        re = jnp.concatenate([evens[k][:, :half], odds[k][:, :half]], axis=1)
        im = jnp.concatenate([evens[k][:, half:], odds[k][:, half:]], axis=1)
        plus = jnp.concatenate([re[:half] + re[half:], im[:half] + im[half:]], axis=0)
        minus = jnp.concatenate([re[:half] - re[half:], im[:half] - im[half:]], axis=0)
        far.append([left_dot(lefts[0], plus), left_dot(lefts[1], minus)])
    factor = []
    for p in range(2):
        total = sum(
            far[k][p][:half] * far[k][p][:half] + far[k][p][half:] * far[k][p][half:]
            for k in range(modes)
        )
        amp = amps[slot, pl.ds(p * half, half), :].astype(F32)
        one = amp / jnp.sqrt(jnp.maximum(total, 0.25)) - 1.0
        factor.append(jnp.concatenate([one, one], axis=0))
    update = [[None, None], [None, None]]
    for k in range(modes):
        even = left_dot(lefts[2], far[k][0] * factor[0])
        odd = left_dot(lefts[3], far[k][1] * factor[1])
        plus, minus = even + odd, even - odd
        re = jnp.concatenate([plus[:half], minus[:half]], axis=0)
        im = jnp.concatenate([plus[half:], minus[half:]], axis=0)
        even = right_dot(jnp.concatenate([re[:, :half], im[:, :half]], axis=1), rights[2])
        odd = right_dot(jnp.concatenate([re[:, half:], im[:, half:]], axis=1), rights[3])
        plus, minus = even + odd, even - odd
        back_re = [plus[:, :half], minus[:, :half]]
        back_im = [plus[:, half:], minus[:, half:]]
        for t in range(2):
            pr, pi = probe_at(0, k, t), probe_at(1, k, t)
            u_re = pr * back_re[t] + pi * back_im[t]
            u_im = pr * back_im[t] - pi * back_re[t]
            update[0][t] = u_re if k == 0 else update[0][t] + u_re
            update[1][t] = u_im if k == 0 else update[1][t] + u_im
            lanes = pl.ds(t * LANES, LANES)
            xr, xi = patch[0][t], patch[1][t]
            sums[k, :, lanes] += xr * back_re[t] + xi * back_im[t]
            sums[modes + k, :, lanes] += xr * back_im[t] - xi * back_re[t]
    for t in range(2):
        lanes = pl.ds(t * LANES, LANES)
        sums[2 * modes, :, lanes] += patch[0][t] * patch[0][t] + patch[1][t] * patch[1][t]
    for c in range(2):
        add_window(acc, c, update[c], row, block, shift)


def interior_kernel(geometry, offsets, counts, tile, probe_in, amps_in, rights_in, lefts_in, *refs):
    frame = Frame(*geometry)
    halos = refs[: frame.sides]
    ext, acc, sums, probe, amps, rights, lefts, raw, sems = refs[frame.sides :]
    tiles, body, margin = frame.tiles, frame.body, frame.margin
    edge = probe.shape[-1]
    pairs = [(amps_in.at[0, 0], raw), (probe_in, probe), (rights_in, rights), (lefts_in, lefts)]
    for number, halo in enumerate(halos):
        pairs.append((halo, ext.at[frame.side_block(number), :, body, :]))
    for t in range(tiles):
        pairs.append((tile.at[:, :, pl.ds(t * LANES, LANES)], ext.at[1 + t, :, body, :]))
    copies = copy_all(pairs, sems)
    acc[...] = jnp.zeros_like(acc)
    sums[...] = jnp.zeros_like(sums)
    copies[0].wait()
    out_at = lax.broadcasted_iota(jnp.int32, (edge, edge), 0)
    in_at = lax.broadcasted_iota(jnp.int32, (edge, edge), 1)
    source = jnp.where(out_at < edge // 2, 2 * out_at, 2 * out_at - edge + 1)
    pick = jnp.where(in_at == source, 1.0, 0.0).astype(BF16)

    def reorder(slot, carry):
        half_way = jnp.dot(pick, raw[slot], preferred_element_type=F32).astype(BF16)
        amps[slot] = lax.dot_general(
            half_way, pick, (((1,), (1,)), ((), ())), preferred_element_type=F32
        ).astype(BF16)
        return carry

    lax.fori_loop(0, counts[0, 0], reorder, 0)
    for copy in copies[1:]:
        copy.wait()

    def visit(slot, carry):
        row, col = frame.place_of(offsets, slot)

        @pl.when(jnp.logical_and(row >= margin, row + edge <= margin + frame.tile_rows))
        def _():
            slot_body(slot, row, col, ext, acc, sums, probe, amps, rights, lefts)

        return carry

    lax.fori_loop(0, counts[0, 0], visit, 0)


def boundary_kernel(geometry, offsets, counts, straight, diagonal, *refs):
    frame = Frame(*geometry)
    sides = frame.sides
    corners, refs = refs[:sides], refs[sides:]
    probe, amps, rights, lefts = refs[:4]
    ext, acc, sums, mid, over_straight, over_diagonal = refs[7:13]
    side_outs, refs = refs[13 : 13 + sides], refs[13 + sides :]
    keep, send, sems = refs
    tiles, margin, body = frame.tiles, frame.margin, frame.body
    edge = probe.shape[-1]
    pairs = []
    for number, halo in enumerate((straight, diagonal)):
        for t in range(tiles):
            pairs.append(
                (halo.at[:, :, pl.ds(t * LANES, LANES)], ext.at[1 + t, :, frame.halo_rows(number), :])
            )
        for side, corner in enumerate(corners):
            pairs.append(
                (corner.at[number], ext.at[frame.side_block(side), :, frame.halo_rows(number), :])
            )
    for copy in copy_all(pairs, sems):
        copy.wait()

    def visit(slot, carry):
        row, col = frame.place_of(offsets, slot)

        @pl.when(jnp.logical_or(row < margin, row + edge > margin + frame.tile_rows))
        def _():
            slot_body(slot, row, col, ext, acc, sums, probe, amps, rights, lefts)

        return carry

    lax.fori_loop(0, counts[0, 0], visit, 0)
    out = [(acc.at[1 + t, :, body, :], mid.at[t]) for t in range(tiles)]
    copies = copy_all(out, sems)
    rows = keep.shape[1]
    index = frame.col & 1
    keep[...] = sums[:, aligned(index * rows, rows), :]
    send[...] = sums[:, aligned((1 - index) * rows, rows), :]
    for side, side_out in enumerate(side_outs):
        side_out[...] = acc[frame.side_block(side)]
    for number, over in enumerate((over_straight, over_diagonal)):
        for t in range(tiles):
            over[t] = acc[1 + t, :, frame.halo_rows(number), :]
    for copy in copies:
        copy.wait()


def corner_kernel(geometry, straight, diagonal, *outs):
    frame = Frame(*geometry)
    for side, out in enumerate(outs):
        out[0] = straight[:, :, frame.side_cols(side)]
        out[1] = diagonal[:, :, frame.side_cols(side)]


KERNEL_VMEM = 12 * MIB
SLOT_COST = dict(
    cost_estimate=pl.CostEstimate(flops=int(1e10), bytes_accessed=20_000_000, transcendentals=0),
)


def run_interior(geometry, offsets, counts, tile, probe, amps, tables, halos):
    tile_rows, tile_cols, margin, sides = geometry
    edge = probe.shape[-1]
    modes = probe.shape[1]
    window = shape(tile_cols // LANES + 2, 2, tile_rows + 2 * margin, LANES)
    amp_shape = jax.ShapeDtypeStruct(amps.shape[2:], BF16)
    outs = [window, window, shape(2 * modes + 1, edge, edge), shape(*probe.shape), amp_shape]
    outs += [jax.ShapeDtypeStruct(t.shape, t.dtype) for t in tables]
    return pl.pallas_call(
        functools.partial(interior_kernel, geometry),
        out_shape=outs,
        in_specs=[IN_SMEM] * 2 + [IN_HBM] * 5 + [ANYWHERE] * sides,
        out_specs=[IN_VMEM] * len(outs),
        scratch_shapes=[VMEM(amp_shape.shape, BF16), pltpu.SemaphoreType.DMA((16,))],
        compiler_params=pltpu.CompilerParams(vmem_limit_bytes=KERNEL_VMEM),
        name="slots_interior",
        **SLOT_COST,
    )(offsets, counts, tile, probe, amps, *tables, *halos)


def run_boundary(geometry, offsets, counts, straight, diagonal, corners, consts, ext, acc, sums):
    tile_rows, tile_cols, margin, sides = geometry
    planes, edge = sums.shape[:2]
    tiles = tile_cols // LANES
    part = shape(planes, edge // 2, edge)
    strip = shape(tiles, 2, margin, LANES)
    outs = [shape(*ext.shape), shape(*acc.shape), shape(*sums.shape)]
    outs += [shape(tiles, 2, tile_rows, LANES), strip, strip]
    outs += [shape(*acc.shape[1:])] * sides + [part, part]
    base = 4 + sides + 4
    return pl.pallas_call(
        functools.partial(boundary_kernel, geometry),
        out_shape=outs,
        in_specs=[IN_SMEM] * 2 + [ANYWHERE] * (2 + sides) + [IN_VMEM] * 7,
        out_specs=[IN_VMEM] * 3 + [IN_HBM] + [IN_VMEM] * (len(outs) - 4),
        scratch_shapes=[pltpu.SemaphoreType.DMA((16,))],
        input_output_aliases={base: 0, base + 1: 1, base + 2: 2},
        compiler_params=pltpu.CompilerParams(vmem_limit_bytes=KERNEL_VMEM),
        name="slots_boundary",
        **SLOT_COST,
    )(offsets, counts, straight, diagonal, *corners, *consts, ext, acc, sums)


def fold_kernel(geometry, over_straight, over_diagonal, *refs):
    frame = Frame(*geometry)
    received, outs = refs[: frame.sides], refs[frame.sides : frame.sides + 2]
    for number, (over, out) in enumerate(((over_straight, outs[0]), (over_diagonal, outs[1]))):
        out[...] = over[...]
        for side, value in enumerate(received):
            out[frame.side_target(side) - 1] += value[:, frame.halo_rows(number), :]


def light_kernel(geometry, own, *refs):
    frame = Frame(*geometry)
    others, (probe, out, canvas) = refs[:-3], refs[-3:]
    tiles = frame.tiles
    edge = probe.shape[-1]
    modes = probe.shape[1]
    canvas[...] = jnp.zeros_like(canvas)
    power = [
        sum(
            probe[c, k, :, pl.ds(t * LANES, LANES)] * probe[c, k, :, pl.ds(t * LANES, LANES)]
            for c in range(2)
            for k in range(modes)
        )
        for t in range(2)
    ]

    def add_from(read):
        def visit(slot, carry):
            row = read(0, slot) - frame.row * frame.tile_rows + edge
            col = read(1, slot) - frame.col * frame.tile_cols + edge
            meets = (row > 0) & (row < frame.tile_rows + edge) & (col > 0) & (col < frame.tile_cols + edge)

            @pl.when(meets)
            def _():
                block = col // LANES
                add_window(canvas, 0, power, row, block, col - block * LANES)

            return carry

        lax.fori_loop(0, read(2, 0), visit, 0)

    add_from(lambda plane, slot: own[plane, slot])
    for other in others:
        if len(other.shape) == 2:
            add_from(lambda plane, slot, other=other: other[plane, slot])
        else:
            for tile in range(other.shape[0]):
                add_from(lambda plane, slot, other=other, tile=tile: other[tile, plane, slot])
    for t in range(tiles):
        out[t] = canvas[edge // LANES + t, 0, pl.ds(edge, frame.tile_rows), :]


def object_kernel(geometry, tile, mid, light, from_straight, from_diagonal, *refs):
    frame = Frame(*geometry)
    received, (out, old, stage, sems_in, sems_out) = refs[: frame.sides], refs[frame.sides :]
    tiles = frame.tiles
    loads = []
    for t in range(tiles):
        loads.append(
            (
                pltpu.make_async_copy(
                    tile.at[:, :, pl.ds(t * LANES, LANES)], old.at[t], sems_in.at[2 * t]
                ),
                pltpu.make_async_copy(mid.at[t], stage.at[t], sems_in.at[2 * t + 1]),
            )
        )
        for copy in loads[-1]:
            copy.start()
    copies = []
    for t in range(tiles):
        for copy in loads[t]:
            copy.wait()
        for side, value in enumerate(received):

            @pl.when(frame.side_target(side) == 1 + t)
            def _(value=value, t=t):
                stage[t] += value[:, frame.body, :]

        for number, value in enumerate((from_straight, from_diagonal)):
            stage[t, :, frame.strip_rows(number), :] += value[t]
        scale = 1.0 / (light[t] + 1.0)
        for c in range(2):
            stage[t, c] = old[t, c] + stage[t, c] * scale
        copy = pltpu.make_async_copy(
            stage.at[t], out.at[:, :, pl.ds(t * LANES, LANES)], sems_out.at[t]
        )
        copy.start()
        copies.append(copy)
    for copy in copies:
        copy.wait()


def member_perm(axis, bits, member):
    mask = sum(((member >> position) & 1) << bit for position, bit in enumerate(bits))
    return [(i, i ^ mask) for i in range(lax.axis_size(axis))]


def member_index(axis, bits):
    where = lax.axis_index(axis)
    return sum(((where >> bit) & 1) << position for position, bit in enumerate(bits))


def combine_kernel(inputs, stage, *refs):
    ins, outs = refs[:inputs], refs[inputs:]
    rows = outs[0].shape[1]
    for member, out in enumerate(outs):
        part = slice(None)
        if len(outs) > 1:
            part = aligned(jnp.bitwise_xor(member_index(*stage), member) * rows, rows)
        value = ins[0][:, part, :]
        for other in ins[1:]:
            value = value + other[:, part, :]
        out[...] = value


def combine(stage, parts, group):
    planes, rows, cols = parts[0].shape
    if (rows // group) % 8:
        total = sum(parts[1:], parts[0])
        if group == 1:
            return [total]
        rows = rows // group
        return [
            lax.dynamic_slice_in_dim(
                total, jnp.bitwise_xor(member_index(*stage), m) * rows, rows, axis=1
            )
            for m in range(group)
        ]
    return small_call(
        functools.partial(combine_kernel, len(parts), stage),
        [shape(planes, rows // group, cols)] * group,
        [IN_VMEM] * len(parts),
    )(*parts)


def place_kernel(group, stage, *refs):
    ins, out = refs[:group], refs[group]
    rows = ins[0].shape[1]
    for member, piece in enumerate(ins):
        at = jnp.bitwise_xor(member_index(*stage), member) * rows
        out[:, aligned(at, rows), :] = piece[...]


def place(stage, parts):
    planes, rows, cols = parts[0].shape
    if rows % 8:
        whole = jnp.zeros((planes, rows * len(parts), cols), F32)
        for m, piece in enumerate(parts):
            at = jnp.bitwise_xor(member_index(*stage), m) * rows
            whole = lax.dynamic_update_slice_in_dim(whole, piece, at, axis=1)
        return whole
    return small_call(
        functools.partial(place_kernel, len(parts), stage),
        [shape(planes, rows * len(parts), cols)],
        [IN_VMEM] * len(parts),
    )(*parts)[0]


def shard_start(stages, edge):
    start, rows = jnp.int32(0), edge
    for axis, bits in stages:
        rows = rows >> len(bits)
        start = start + member_index(axis, bits) * rows
    return start


def finish_kernel(stages, edge, probe, *refs):
    ins, out = refs[:-1], refs[-1]
    total = ins[0][...]
    for other in ins[1:]:
        total = total + other[...]
    planes, rows = out.shape[:2]
    old = probe[:, aligned(shard_start(stages, edge), rows), :]
    out[...] = old + total[:planes] / (total[planes:] + 1.0)


def finish(stages, probe, parts):
    planes, rows, cols = parts[0].shape
    edge = probe.shape[1]
    if rows % 8:
        total = sum(parts[1:], parts[0])
        old = lax.dynamic_slice_in_dim(probe, shard_start(stages, edge), rows, axis=1)
        return old + total[:-1] / (total[-1:] + 1.0)
    return small_call(
        functools.partial(finish_kernel, stages, edge),
        [shape(planes - 1, rows, cols)],
        [IN_VMEM] * (1 + len(parts)),
    )(probe, *parts)[0]


def swap_sides(outs):
    count = lax.axis_size("col")
    if len(outs) == 1:
        return [lax.ppermute(outs[0], "col", [(0, 1), (1, 0)])]
    up = [(i, i + 1) for i in range(count - 1)]
    down = [(i + 1, i) for i in range(count - 1)]
    return [lax.ppermute(outs[1], "col", up), lax.ppermute(outs[0], "col", down)]


def swap_rows(value, number):
    count = lax.axis_size("row")
    pairs = []
    for low in range(number, count - 1, 2):
        pairs += [(low, low + 1), (low + 1, low)]
    return lax.ppermute(value, "row", pairs)


def stages_of(rows, cols):
    stages = [("col", (bit,)) for bit in range(cols.bit_length() - 1)]
    bits = list(range(1, rows.bit_length() - 1))
    if len(bits) > 1:
        stages.append(("row", (bits[0], bits[1])))
        bits = bits[2:]
    stages += [("row", (bit,)) for bit in bits]
    return tuple(stages), ("row", (0,))


def step(object_field, probe_modes, scan_offsets, scan_counts, amplitudes):
    tile_rows, tile_cols = object_field.shape[1:]
    modes = probe_modes.shape[1]
    edge = probe_modes.shape[-1]
    margin = edge // 2
    slots = amplitudes.shape[2]
    tiles = tile_cols // LANES
    sides = 1 if lax.axis_size("col") == 2 else 2
    geometry = (tile_rows, tile_cols, margin, sides)
    stages, last = stages_of(lax.axis_size("row"), lax.axis_size("col"))
    tables = tuple(in_hbm(jnp.asarray(t)) for t in dft_tables(edge))
    tile_hbm, probe_hbm, amps_hbm = in_hbm(object_field), in_hbm(probe_modes), in_hbm(amplitudes)

    straight, diagonal, *edges = small_call(
        functools.partial(pack_kernel, geometry),
        [shape(2, margin, tile_cols)] * 2 + [shape(2, tile_rows, margin)] * sides,
        [IN_HBM],
        limit=8 * MIB,
        scratch=(pltpu.SemaphoreType.DMA((4,)),),
    )(tile_hbm)
    straight = swap_rows(straight, 0)
    diagonal = swap_rows(diagonal, 1)
    halos = swap_sides(edges)

    own = jnp.concatenate(
        [scan_offsets[0, 0], jnp.broadcast_to(scan_counts[0], (1, slots))], axis=0
    )
    stacked = jnp.stack([own, swap_rows(own, 0), swap_rows(own, 1)])
    beside = swap_sides([stacked] * sides)

    ext, acc, sums, *consts = run_interior(
        geometry, scan_offsets, scan_counts, tile_hbm, probe_hbm, amps_hbm, tables, halos
    )

    cut = small_call(
        functools.partial(corner_kernel, geometry),
        [shape(2, 2, margin, margin)] * sides,
        [IN_VMEM] * 2,
    )(straight, diagonal)
    corners = swap_sides(cut)

    _, _, _, mid, *rest = run_boundary(
        geometry, scan_offsets, scan_counts, straight, diagonal, corners, consts, ext, acc, sums
    )
    overs, side_outs, (keep, send) = rest[:2], rest[2 : 2 + sides], rest[2 + sides :]

    parts = [keep]
    for number, stage in enumerate(stages):
        axis, bits = stage
        if number:
            mine, *pieces = combine(stage, parts, 1 << len(bits))
        else:
            mine, pieces = keep, [send]
        parts = [mine] + [
            lax.ppermute(piece, axis, member_perm(axis, bits, member + 1))
            for member, piece in enumerate(pieces)
        ]
    total = combine(last, parts, 1)[0]
    parts = [total, lax.ppermute(total, last[0], member_perm(*last, 1))]

    received = swap_sides(side_outs)
    strip = shape(tiles, 2, margin, LANES)
    out_straight, out_diagonal = small_call(
        functools.partial(fold_kernel, geometry), [strip, strip], [IN_VMEM] * (2 + sides)
    )(*overs, *received)
    from_straight = swap_rows(out_straight, 0)
    from_diagonal = swap_rows(out_diagonal, 1)

    flat = probe_modes.reshape(2 * modes, edge, edge)
    shard = finish(stages, flat, parts)
    for number, stage in reversed(list(enumerate(stages))):
        axis, bits = stage
        pieces = [shard] + [
            lax.ppermute(shard, axis, member_perm(axis, bits, member))
            for member in range(1, 1 << len(bits))
        ]
        shard = place(stage, pieces)
    probe_new = shard.reshape(probe_modes.shape)

    light = small_call(
        functools.partial(light_kernel, geometry),
        [shape(tiles, tile_rows, LANES)],
        [IN_SMEM] * (2 + sides) + [IN_VMEM],
        limit=8 * MIB,
        scratch=(VMEM((tiles + 2 * (edge // LANES), 1, tile_rows + 2 * edge, LANES), F32),),
        cost=10_000_000,
    )(own, stacked[1:], *beside, probe_modes)[0]
    object_new = small_call(
        functools.partial(object_kernel, geometry),
        [shape(2, tile_rows, tile_cols)],
        [IN_HBM, ANYWHERE] + [IN_VMEM] * (3 + sides),
        limit=8 * MIB,
        scratch=(
            VMEM((tiles, 2, tile_rows, LANES), F32),
            VMEM((tiles, 2, tile_rows, LANES), F32),
            pltpu.SemaphoreType.DMA((2 * tiles,)),
            pltpu.SemaphoreType.DMA((tiles,)),
        ),
        out_specs=[IN_HBM],
    )(object_field, mid, light, from_straight, from_diagonal, *received)[0]
    return object_new, probe_new


def solution(mesh):
    in_specs = (
        P(None, "row", "col"),
        P(),
        P("row", "col", None, None),
        P("row", "col"),
        P("row", "col", None, None, None),
    )
    out_specs = (P(None, "row", "col"), P())
    return jax.shard_map(step, mesh=mesh, in_specs=in_specs, out_specs=out_specs, check_vma=False)
```

time: 152 us -> 112 us (0.74)
  the two profiles are of different devices: /device:TPU:27 before, /device:TPU:0 now
where the time goes in v3:
time: 112 us
  waiting for transfers between devices  64.6 us (58%)
  starting transfers between devices  30.8 us (28%)
  Pallas kernels  14.6 us (13%)
  between operations  1.54 us (1%)
    ppermute x6, waiting for transfers between devices, swap_rows(): return lax.ppermute(value, 'row', pairs)  33.7 us
    ppermute x5, starting transfers between devices, step(): lax.ppermute(piece, axis, member_perm(axis, bits, member + 1))  20.4 us
    ppermute x5, waiting for transfers between devices, step(): lax.ppermute(piece, axis, member_perm(axis, bits, member + 1))  16.2 us
    ppermute x5, waiting for transfers between devices, step(): lax.ppermute(shard, axis, member_perm(axis, bits, member))  9.08 us
    pallas_call x1, Pallas kernels, run_interior(): pl.pallas_call(functools.partial(interior_kernel, geometry), out_shape=ou...  6.79 us
    ppermute x6, starting transfers between devices, swap_rows(): return lax.ppermute(value, 'row', pairs)  6.35 us
    ppermute x1, waiting for transfers between devices, step(): parts = [total, lax.ppermute(total, last[0], member_perm(*last, 1))]  4.43 us
    ppermute x5, starting transfers between devices, step(): lax.ppermute(shard, axis, member_perm(axis, bits, member))  3.7 us
  transfers between devices with their start and end apart: 21, of which 12 were waited for; matrix products, arithmetic and copies ran while one was open for 0% of the time, Pallas kernels for 10%

profile of v3, /device:TPU:0, one launch (start us, length us, event | category | flops | bytes accessed | tf_op | source)
XLA Modules:
  0.0 111.5 jit_solution(5605094428910927118)
XLA Ops:
  0.6 1.4 %shard_map.86 = (f32[2,128,512]{2,1,0:T(8,128)S(1)}, f32[2,128,512]{2,1,0:T(8,128)S(1)}, f32[2,512,128]{2,1,0:T(8,128)S(1)}) custom-call(f32[2,512,512]{2,1,0:T(8,128)} %tile.5), custom_call_target="tpu_custom_call" | custom-call | tf_op jit(solution)/shard_map/pallas_call | solution.py:622
  2.1 3.0 %collective-permute-start = (f32[2,128,512]{2,1,0:T(8,128)S(1)}, f32[2,128,512]{2,1,0:T(8,128)S(1)}, u32[]{:S(2)}, u32[]{:S(2)}) collective-permute-start(f32[2,128,512]{2,1,0:T(8,128)S(1)} %get-tuple-element.26), channel_id=1, source_target_pairs={{0,2},{2,0},{4,6},{6,4},{8,10},{10,8},{12,14},{14,12},{16,18},{18,... | collective-permute-start | bytes 1572872 | tf_op jit(solution)/shard_map/ppermute | solution.py:596
  5.1 0.7 collective-permute-start.1
  5.8 0.1 collective-permute-start.3
  6.5 21.0 %collective-permute-done.straight = f32[2,128,512]{2,1,0:T(8,128)S(1)} collective-permute-done((f32[2,128,512]{2,1,0:T(8,128)S(1)}, f32[2,128,512]{2,1,0:T(8,128)S(1)}, u32[]{:S(2)}, u32[]{:S(2)}) %collective-permute-start) | collective-permute-done | bytes 524320 | tf_op jit(solution)/shard_map/ppermute | solution.py:596
  27.6 6.8 %slots_interior.1 = (f32[6,2,768,128]{3,2,1,0:T(8,128)S(1)}, f32[6,2,768,128]{3,2,1,0:T(8,128)S(1)}, f32[5,256,256]{2,1,0:T(8,128)S(1)}, f32[2,2,256,256]{3,2,1,...) custom-call(s32[1,1,2,6]{3,2,1,0:T(2,128)S(1)} %copy-done.2, ...), custom_call_target="tpu_custom_call" | custom-call | flops 10000000000 | bytes 20000000 | tf_op jit(solution)/shard_map/slots_interior/pallas_call | solution.py:358
  34.5 1.5 %slots_boundary.1 = (f32[6,2,768,128]{3,2,1,0:T(8,128)S(1)}, f32[6,2,768,128]{3,2,1,0:T(8,128)S(1)}, f32[5,256,256]{2,1,0:T(8,128)S(1)}, f32[4,2,512,128]{3,2,1,...) custom-call(s32[1,1,2,6]{3,2,1,0:T(2,128)S(1)} %copy-done.2, ...), custom_call_target="tpu_custom_call", output_to_operand_aliasing={{0}: (9, {}), {1}: (10, {}), {2}: (11, {})} | custom-call | flops 10000000000 | bytes 20000000 | tf_op jit(solution)/shard_map/slots_boundary/pallas_call | solution.py:380
  35.9 0.6 collective-permute-start.10
  36.5 0.1 collective-permute-start.7
  36.6 1.6 %collective-permute-done.10.refs_1_ = f32[5,128,256]{2,1,0:T(8,128)S(1)} collective-permute-done((f32[5,128,256]{2,1,0:T(8,128)S(1)}, f32[5,128,256]{2,1,0:T(8,128)S(1)}, u32[]{:S(2)}, u32[]{:S(2)}) %collective-permute-start.10) | collective-permute-done | bytes 655392 | tf_op jit(solution)/shard_map/ppermute | solution.py:663
  38.3 14.6 %collective-permute-start.11 = (f32[5,32,256]{2,1,0:T(8,128)S(1)}, f32[5,32,256]{2,1,0:T(8,128)S(1)}, u32[]{:S(2)}, u32[]{:S(2)}) collective-permute-start(f32[5,32,256]{2,1,0:T(8,128)S(1)} %get-tuple-element.45), channel_id=1, source_target_pairs={{0,4},{2,6},{4,0},{6,2},{8,12},{10,14},{12,8},{14,10},{16,20},{18,... | collective-permute-start | bytes 491528 | tf_op jit(solution)/shard_map/ppermute | solution.py:663
  52.9 5.1 %collective-permute-start.12 = (f32[5,32,256]{2,1,0:T(8,128)S(1)}, f32[5,32,256]{2,1,0:T(8,128)S(1)}, u32[]{:S(2)}, u32[]{:S(2)}) collective-permute-start(f32[5,32,256]{2,1,0:T(8,128)S(1)} %get-tuple-element.46), channel_id=1, source_target_pairs={{0,8},{2,10},{4,12},{6,14},{8,0},{10,2},{12,4},{14,6},{16,24},{18,... | collective-permute-start | bytes 491528 | tf_op jit(solution)/shard_map/ppermute | solution.py:663
  58.1 5.0 %collective-permute-done.12.refs_2_ = f32[5,32,256]{2,1,0:T(8,128)S(1)} collective-permute-done((f32[5,32,256]{2,1,0:T(8,128)S(1)}, f32[5,32,256]{2,1,0:T(8,128)S(1)}, u32[]{:S(2)}, u32[]{:S(2)}) %collective-permute-start.12) | collective-permute-done | bytes 163872 | tf_op jit(solution)/shard_map/ppermute | solution.py:663
  63.1 2.7 %collective-permute-done.13.refs_3_ = f32[5,32,256]{2,1,0:T(8,128)S(1)} collective-permute-done((f32[5,32,256]{2,1,0:T(8,128)S(1)}, f32[5,32,256]{2,1,0:T(8,128)S(1)}, u32[]{:S(2)}, u32[]{:S(2)}) %collective-permute-start.13) | collective-permute-done | bytes 163872 | tf_op jit(solution)/shard_map/ppermute | solution.py:663
  65.9 6.8 %collective-permute-done.14.refs_1_ = f32[5,16,256]{2,1,0:T(8,128)S(1)} collective-permute-done((f32[5,16,256]{2,1,0:T(8,128)S(1)}, f32[5,16,256]{2,1,0:T(8,128)S(1)}, u32[]{:S(2)}, u32[]{:S(2)}) %collective-permute-start.14) | collective-permute-done | bytes 81952 | tf_op jit(solution)/shard_map/ppermute | solution.py:663
  72.8 4.4 %collective-permute-done.15.refs_1_ = f32[5,16,256]{2,1,0:T(8,128)S(1)} collective-permute-done((f32[5,16,256]{2,1,0:T(8,128)S(1)}, f32[5,16,256]{2,1,0:T(8,128)S(1)}, u32[]{:S(2)}, u32[]{:S(2)}) %collective-permute-start.15) | collective-permute-done | bytes 81952 | tf_op jit(solution)/shard_map/ppermute | solution.py:667
  77.4 5.8 %collective-permute-done.16.refs_1_ = f32[4,16,256]{2,1,0:T(8,128)S(1)} collective-permute-done((f32[4,16,256]{2,1,0:T(8,128)S(1)}, f32[4,16,256]{2,1,0:T(8,128)S(1)}, u32[]{:S(2)}, u32[]{:S(2)}) %collective-permute-start.16) | collective-permute-done | bytes 65568 | tf_op jit(solution)/shard_map/ppermute | solution.py:682
  83.1 0.1 collective-permute-start.17
  83.2 1.3 %collective-permute-start.18 = (f32[4,32,256]{2,1,0:T(8,128)S(1)}, f32[4,32,256]{2,1,0:T(8,128)S(1)}, u32[]{:S(2)}, u32[]{:S(2)}) collective-permute-start(f32[4,32,256]{2,1,0:T(8,128)S(1)} %shard_map.95.refs_0_), channel_id=1, source_target_pairs={{0,8},{2,10},{4,12},{6,14},{8,0},{10,2},{12,4},{14,6},{16,24},{18,... | collective-permute-start | bytes 393224 | tf_op jit(solution)/shard_map/ppermute | solution.py:682
  84.6 2.1 %collective-permute-start.19 = (f32[4,32,256]{2,1,0:T(8,128)S(1)}, f32[4,32,256]{2,1,0:T(8,128)S(1)}, u32[]{:S(2)}, u32[]{:S(2)}) collective-permute-start(f32[4,32,256]{2,1,0:T(8,128)S(1)} %shard_map.95.refs_0_), channel_id=1, source_target_pairs={{0,12},{2,14},{4,8},{6,10},{8,4},{10,6},{12,0},{14,2},{16,28},{18,... | collective-permute-start | bytes 393224 | tf_op jit(solution)/shard_map/ppermute | solution.py:682
  86.7 0.1 shard_map.89
  86.9 0.8 collective-permute-start.9
  87.7 0.5 collective-permute-done.17.refs_1_
  88.2 1.5 %collective-permute-done.18.refs_2_ = f32[4,32,256]{2,1,0:T(8,128)S(1)} collective-permute-done((f32[4,32,256]{2,1,0:T(8,128)S(1)}, f32[4,32,256]{2,1,0:T(8,128)S(1)}, u32[]{:S(2)}, u32[]{:S(2)}) %collective-permute-start.18) | collective-permute-done | bytes 131104 | tf_op jit(solution)/shard_map/ppermute | solution.py:682
  89.6 1.4 %collective-permute-done.19.refs_3_ = f32[4,32,256]{2,1,0:T(8,128)S(1)} collective-permute-done((f32[4,32,256]{2,1,0:T(8,128)S(1)}, f32[4,32,256]{2,1,0:T(8,128)S(1)}, u32[]{:S(2)}, u32[]{:S(2)}) %collective-permute-start.19) | collective-permute-done | bytes 131104 | tf_op jit(solution)/shard_map/ppermute | solution.py:682
  91.2 1.1 collective-permute-start.4
  92.3 0.6 collective-permute-start.5
  92.9 12.7 %collective-permute-done.4 = s32[3,6]{1,0:T(4,128)S(1)} collective-permute-done((s32[3,6]{1,0:T(4,128)S(1)}, s32[3,6]{1,0:T(4,128)S(1)}, u32[]{:S(2)}, u32[]{:S(2)}) %collective-permute-start.4) | collective-permute-done | bytes 104 | tf_op jit(solution)/shard_map/ppermute | solution.py:596
  105.7 1.1 %collective-permute-done.6.refs_1_ = s32[3,3,6]{2,1,0:T(4,128)S(1)} collective-permute-done((s32[3,3,6]{2,1,0:T(4,128)S(1)}, s32[3,3,6]{2,1,0:T(4,128)S(1)}, u32[]{:S(2)}, u32[]{:S(2)}) %collective-permute-start.6) | collective-permute-done | bytes 248 | tf_op jit(solution)/shard_map/ppermute | solution.py:585
  106.9 1.6 %shard_map.88.light = f32[4,512,128]{2,1,0:T(8,128)S(1)} custom-call(s32[3,6]{1,0:T(4,128)S(1)} %get-tuple-element.51.own, s32[2,3,6]{2,1,0:T(4,128)S(1)} %pad_add_fusion.1.refs_0_, s32[3,3,6]{2,1,0:T(4,128)S(1)} %collective-permute-done.6.refs_1_, f32[2,2,256,256]{3,2,1,0:T(8,128)S(1)} %copy-done.1), custom_call_target="tpu_custom_call" | custom-call | flops 10000000 | bytes 1000000 | tf_op jit(solution)/shard_map/pallas_call | solution.py:688
  108.5 2.0 %shard_map.90 = f32[2,512,512]{2,1,0:T(8,128)} custom-call(f32[2,512,512]{2,1,0:T(8,128)S(1)} %copy-done, f32[4,2,512,128]{3,2,1,0:T(8,128)S(1)} %get-tuple-element.36.mid, f32[4,512,128]{2,1,0:T(8,128)S(1)} %shard_map.88.light, f32[4,2,128,128]{3,2,1,0:T(8,128)S(1)} %collective-permute-done.8.from_straight, ...), custom_call_target="tpu_custom_call" | custom-call | tf_op jit(solution)/shard_map/pallas_call | solution.py:696
  110.5 1.0 shard_map.97
  (33 shorter events, 0.8 us)
Async XLA Ops:
  0.6 27.0 %copy-start.2 = (s32[1,1,2,6]{3,2,1,0:T(2,128)S(1)}, s32[1,1,2,6]{3,2,1,0:T(2,128)}, u32[]{:S(2)}) copy-start(s32[1,1,2,6]{3,2,1,0:T(2,128)} %offsets.3) | copy-start | bytes 148
  2.1 25.4 %collective-permute-start = (f32[2,128,512]{2,1,0:T(8,128)S(1)}, f32[2,128,512]{2,1,0:T(8,128)S(1)}, u32[]{:S(2)}, u32[]{:S(2)}) collective-permute-start(f32[2,128,512]{2,1,0:T(8,128)S(1)} %get-tuple-element.26), channel_id=1, source_target_pairs={{0,2},{2,0},{4,6},{6,4},{8,10},{10,8},{12,14},{14,12},{16,18},{18,... | collective-permute-start | bytes 1572872 | tf_op jit(solution)/shard_map/ppermute | solution.py:596
  5.1 22.4 %collective-permute-start.1 = (f32[2,128,512]{2,1,0:T(8,128)S(1)}, f32[2,128,512]{2,1,0:T(8,128)S(1)}, u32[]{:S(2)}, u32[]{:S(2)}) collective-permute-start(f32[2,128,512]{2,1,0:T(8,128)S(1)} %get-tuple-element.27), channel_id=1, source_target_pairs={{2,4},{4,2},{6,8},{8,6},{10,12},{12,10},{14,16},{16,14},{18,20},{2... | collective-permute-start | bytes 1572872 | tf_op jit(solution)/shard_map/ppermute | solution.py:596
  5.8 21.9 %collective-permute-start.3 = (f32[2,512,128]{2,1,0:T(8,128)S(1)}, f32[2,512,128]{2,1,0:T(8,128)S(1)}, u32[]{:S(2)}, u32[]{:S(2)}) collective-permute-start(f32[2,512,128]{2,1,0:T(8,128)S(1)} %get-tuple-element.28), channel_id=1, source_target_pairs={{0,1},{1,0},{2,3},{3,2},{4,5},{5,4},{6,7},{7,6},{8,9},{9,8},{10,11... | collective-permute-start | bytes 1572872 | tf_op jit(solution)/shard_map/ppermute | solution.py:585
  27.5 6.9 %collective-permute-start.2 = (f32[2,2,128,128]{3,2,1,0:T(8,128)S(1)}, f32[2,2,128,128]{3,2,1,0:T(8,128)S(1)}, u32[]{:S(2)}, u32[]{:S(2)}) collective-permute-start(f32[2,2,128,128]{3,2,1,0:T(8,128)S(1)} %shard_map.87), channel_id=1, source_target_pairs={{0,1},{1,0},{2,3},{3,2},{4,5},{5,4},{6,7},{7,6},{8,9},{9,8},{10,11... | collective-permute-start | bytes 786440 | tf_op jit(solution)/shard_map/ppermute | solution.py:585
  35.9 41.3 %copy-start.1 = (f32[2,2,256,256]{3,2,1,0:T(8,128)S(1)}, f32[2,2,256,256]{3,2,1,0:T(8,128)}, u32[]{:S(2)}) copy-start(f32[2,2,256,256]{3,2,1,0:T(8,128)} %refs_2_.1) | copy-start | bytes 3145732
  35.9 2.3 %collective-permute-start.10 = (f32[5,128,256]{2,1,0:T(8,128)S(1)}, f32[5,128,256]{2,1,0:T(8,128)S(1)}, u32[]{:S(2)}, u32[]{:S(2)}) collective-permute-start(f32[5,128,256]{2,1,0:T(8,128)S(1)} %get-tuple-element.43), channel_id=1, source_target_pairs={{0,1},{1,0},{2,3},{3,2},{4,5},{5,4},{6,7},{7,6},{8,9},{9,8},{10,11... | collective-permute-start | bytes 1966088 | tf_op jit(solution)/shard_map/ppermute | solution.py:663
  36.5 50.2 %collective-permute-start.7 = (f32[2,768,128]{2,1,0:T(8,128)S(1)}, f32[2,768,128]{2,1,0:T(8,128)S(1)}, u32[]{:S(2)}, u32[]{:S(2)}) collective-permute-start(f32[2,768,128]{2,1,0:T(8,128)S(1)} %get-tuple-element.39), channel_id=1, source_target_pairs={{0,1},{1,0},{2,3},{3,2},{4,5},{5,4},{6,7},{7,6},{8,9},{9,8},{10,11... | collective-permute-start | bytes 2359304 | tf_op jit(solution)/shard_map/ppermute | solution.py:585
  38.3 19.7 %collective-permute-start.11 = (f32[5,32,256]{2,1,0:T(8,128)S(1)}, f32[5,32,256]{2,1,0:T(8,128)S(1)}, u32[]{:S(2)}, u32[]{:S(2)}) collective-permute-start(f32[5,32,256]{2,1,0:T(8,128)S(1)} %get-tuple-element.45), channel_id=1, source_target_pairs={{0,4},{2,6},{4,0},{6,2},{8,12},{10,14},{12,8},{14,10},{16,20},{18,... | collective-permute-start | bytes 491528 | tf_op jit(solution)/shard_map/ppermute | solution.py:663
  52.9 10.2 %collective-permute-start.12 = (f32[5,32,256]{2,1,0:T(8,128)S(1)}, f32[5,32,256]{2,1,0:T(8,128)S(1)}, u32[]{:S(2)}, u32[]{:S(2)}) collective-permute-start(f32[5,32,256]{2,1,0:T(8,128)S(1)} %get-tuple-element.46), channel_id=1, source_target_pairs={{0,8},{2,10},{4,12},{6,14},{8,0},{10,2},{12,4},{14,6},{16,24},{18,... | collective-permute-start | bytes 491528 | tf_op jit(solution)/shard_map/ppermute | solution.py:663
  58.1 7.8 %collective-permute-start.13 = (f32[5,32,256]{2,1,0:T(8,128)S(1)}, f32[5,32,256]{2,1,0:T(8,128)S(1)}, u32[]{:S(2)}, u32[]{:S(2)}) collective-permute-start(f32[5,32,256]{2,1,0:T(8,128)S(1)} %get-tuple-element.47), channel_id=1, source_target_pairs={{0,12},{2,14},{4,8},{6,10},{8,4},{10,6},{12,0},{14,2},{16,28},{18,... | collective-permute-start | bytes 491528 | tf_op jit(solution)/shard_map/ppermute | solution.py:663
  65.9 6.9 %collective-permute-start.14 = (f32[5,16,256]{2,1,0:T(8,128)S(1)}, f32[5,16,256]{2,1,0:T(8,128)S(1)}, u32[]{:S(2)}, u32[]{:S(2)}) collective-permute-start(f32[5,16,256]{2,1,0:T(8,128)S(1)} %get-tuple-element.49), channel_id=1, source_target_pairs={{0,16},{2,18},{4,20},{6,22},{8,24},{10,26},{12,28},{14,30},{16,0},... | collective-permute-start | bytes 245768 | tf_op jit(solution)/shard_map/ppermute | solution.py:663
  72.8 4.5 %collective-permute-start.15 = (f32[5,16,256]{2,1,0:T(8,128)S(1)}, f32[5,16,256]{2,1,0:T(8,128)S(1)}, u32[]{:S(2)}, u32[]{:S(2)}) collective-permute-start(f32[5,16,256]{2,1,0:T(8,128)S(1)} %shard_map.93.refs_0_), channel_id=1, source_target_pairs={{0,2},{2,0},{4,6},{6,4},{8,10},{10,8},{12,14},{14,12},{16,18},{18,... | collective-permute-start | bytes 245768 | tf_op jit(solution)/shard_map/ppermute | solution.py:667
  77.3 5.8 %collective-permute-start.16 = (f32[4,16,256]{2,1,0:T(8,128)S(1)}, f32[4,16,256]{2,1,0:T(8,128)S(1)}, u32[]{:S(2)}, u32[]{:S(2)}) collective-permute-start(f32[4,16,256]{2,1,0:T(8,128)S(1)} %shard_map.94.refs_0_), channel_id=1, source_target_pairs={{0,16},{2,18},{4,20},{6,22},{8,24},{10,26},{12,28},{14,30},{16,0},... | collective-permute-start | bytes 196616 | tf_op jit(solution)/shard_map/ppermute | solution.py:682
  83.1 5.0 %collective-permute-start.17 = (f32[4,32,256]{2,1,0:T(8,128)S(1)}, f32[4,32,256]{2,1,0:T(8,128)S(1)}, u32[]{:S(2)}, u32[]{:S(2)}) collective-permute-start(f32[4,32,256]{2,1,0:T(8,128)S(1)} %shard_map.95.refs_0_), channel_id=1, source_target_pairs={{0,4},{2,6},{4,0},{6,2},{8,12},{10,14},{12,8},{14,10},{16,20},{18,... | collective-permute-start | bytes 393224 | tf_op jit(solution)/shard_map/ppermute | solution.py:682
  83.2 6.4 %collective-permute-start.18 = (f32[4,32,256]{2,1,0:T(8,128)S(1)}, f32[4,32,256]{2,1,0:T(8,128)S(1)}, u32[]{:S(2)}, u32[]{:S(2)}) collective-permute-start(f32[4,32,256]{2,1,0:T(8,128)S(1)} %shard_map.95.refs_0_), channel_id=1, source_target_pairs={{0,8},{2,10},{4,12},{6,14},{8,0},{10,2},{12,4},{14,6},{16,24},{18,... | collective-permute-start | bytes 393224 | tf_op jit(solution)/shard_map/ppermute | solution.py:682
  84.6 6.5 %collective-permute-start.19 = (f32[4,32,256]{2,1,0:T(8,128)S(1)}, f32[4,32,256]{2,1,0:T(8,128)S(1)}, u32[]{:S(2)}, u32[]{:S(2)}) collective-permute-start(f32[4,32,256]{2,1,0:T(8,128)S(1)} %shard_map.95.refs_0_), channel_id=1, source_target_pairs={{0,12},{2,14},{4,8},{6,10},{8,4},{10,6},{12,0},{14,2},{16,28},{18,... | collective-permute-start | bytes 393224 | tf_op jit(solution)/shard_map/ppermute | solution.py:682
  86.7 21.8 %copy-start = (f32[2,512,512]{2,1,0:T(8,128)S(1)}, f32[2,512,512]{2,1,0:T(8,128)}, u32[]{:S(2)}) copy-start(f32[2,512,512]{2,1,0:T(8,128)} %tile.5) | copy-start | bytes 6291460
  86.8 21.6 %collective-permute-start.8 = (f32[4,2,128,128]{3,2,1,0:T(8,128)S(1)}, f32[4,2,128,128]{3,2,1,0:T(8,128)S(1)}, u32[]{:S(2)}, u32[]{:S(2)}) collective-permute-start(f32[4,2,128,128]{3,2,1,0:T(8,128)S(1)} %get-tuple-element.40), channel_id=1, source_target_pairs={{0,2},{2,0},{4,6},{6,4},{8,10},{10,8},{12,14},{14,12},{16,18},{18,... | collective-permute-start | bytes 1572872 | tf_op jit(solution)/shard_map/ppermute | solution.py:596
  86.9 21.6 %collective-permute-start.9 = (f32[4,2,128,128]{3,2,1,0:T(8,128)S(1)}, f32[4,2,128,128]{3,2,1,0:T(8,128)S(1)}, u32[]{:S(2)}, u32[]{:S(2)}) collective-permute-start(f32[4,2,128,128]{3,2,1,0:T(8,128)S(1)} %get-tuple-element.41), channel_id=1, source_target_pairs={{2,4},{4,2},{6,8},{8,6},{10,12},{12,10},{14,16},{16,14},{18,20},{2... | collective-permute-start | bytes 1572872 | tf_op jit(solution)/shard_map/ppermute | solution.py:596
  91.1 19.4 %collective-permute-start.20 = (f32[4,128,256]{2,1,0:T(8,128)S(1)}, f32[4,128,256]{2,1,0:T(8,128)S(1)}, u32[]{:S(2)}, u32[]{:S(2)}) collective-permute-start(f32[4,128,256]{2,1,0:T(8,128)S(1)} %shard_map.96.refs_0_), channel_id=1, source_target_pairs={{0,1},{1,0},{2,3},{3,2},{4,5},{5,4},{6,7},{7,6},{8,9},{9,8},{10,11... | collective-permute-start | bytes 1572872 | tf_op jit(solution)/shard_map/ppermute | solution.py:682
  91.2 14.4 %collective-permute-start.4 = (s32[3,6]{1,0:T(4,128)S(1)}, s32[3,6]{1,0:T(4,128)S(1)}, u32[]{:S(2)}, u32[]{:S(2)}) collective-permute-start(s32[3,6]{1,0:T(4,128)S(1)} %get-tuple-element.51.own), channel_id=1, source_target_pairs={{0,2},{2,0},{4,6},{6,4},{8,10},{10,8},{12,14},{14,12},{16,18},{18,... | collective-permute-start | bytes 224 | tf_op jit(solution)/shard_map/ppermute | solution.py:596
  92.3 13.3 %collective-permute-start.5 = (s32[3,6]{1,0:T(4,128)S(1)}, s32[3,6]{1,0:T(4,128)S(1)}, u32[]{:S(2)}, u32[]{:S(2)}) collective-permute-start(s32[3,6]{1,0:T(4,128)S(1)} %get-tuple-element.51.own), channel_id=1, source_target_pairs={{2,4},{4,2},{6,8},{8,6},{10,12},{12,10},{14,16},{16,14},{18,20},{2... | collective-permute-start | bytes 224 | tf_op jit(solution)/shard_map/ppermute | solution.py:596
  105.6 1.2 %collective-permute-start.6 = (s32[3,3,6]{2,1,0:T(4,128)S(1)}, s32[3,3,6]{2,1,0:T(4,128)S(1)}, u32[]{:S(2)}, u32[]{:S(2)}) collective-permute-start(s32[3,3,6]{2,1,0:T(4,128)S(1)} %pad_add_fusion), channel_id=1, source_target_pairs={{0,1},{1,0},{2,3},{3,2},{4,5},{5,4},{6,7},{7,6},{8,9},{9,8},{10,11... | collective-permute-start | bytes 656 | tf_op jit(solution)/shard_map/ppermute | solution.py:585

commit v4 on v3

--- a/solution.py
+++ b/solution.py
@@ -125,6 +125,9 @@
         start = self.is_below(number) * (self.tile_rows + self.margin)
         return pl.ds(pl.multiple_of(start, self.margin), self.margin)
 
+    def edge_tile(self, number):
+        return self.side_is_east(number) * (self.tiles - 1)
+
     def place_of(self, offsets, slot):
         return (
             offsets[0, 0, 0, slot] - self.row * self.tile_rows + self.margin,
@@ -145,16 +148,43 @@
     )
 
 
-def pack_kernel(geometry, tile, straight, diagonal, *refs):
+WHERE = 8
+
+
+def where_rows(offsets, counts):
+    lane = lax.broadcasted_iota(jnp.int32, (1, LANES), 1)
+    rows = []
+    for axis in range(2):
+        line = jnp.zeros((1, LANES), jnp.int32)
+        for slot in range(offsets.shape[-1]):
+            line = jnp.where(lane == slot, offsets[0, 0, axis, slot], line)
+        rows.append(line)
+    rows.append(jnp.zeros((1, LANES), jnp.int32) + counts[0, 0])
+    return [row.astype(F32) for row in rows]
+
+
+def pack_kernel(geometry, offsets, counts, tile, straight, diagonal, *refs):
     sides, sems = refs[:-1], refs[-1]
     frame = Frame(*geometry)
-    pairs = [
-        (tile.at[:, frame.strip_rows(0), :], straight),
-        (tile.at[:, frame.strip_rows(1), :], diagonal),
-    ]
+    margin = frame.margin
+    pairs = []
+    for number, strip in enumerate((straight, diagonal)):
+        for t in range(frame.tiles):
+            for c in range(2):
+                pairs.append(
+                    (
+                        tile.at[c, frame.strip_rows(number), pl.ds(t * LANES, LANES)],
+                        strip.at[pl.ds((2 * t + c) * margin, margin), :],
+                    )
+                )
     for number, side in enumerate(sides):
         pairs.append((tile.at[:, :, frame.side_cols(number)], side))
-    for copy in copy_all(pairs, sems):
+    copies = copy_all(pairs, sems)
+    rows = where_rows(offsets, counts)
+    for strip in (straight, diagonal):
+        for number, row in enumerate(rows):
+            strip[pl.ds(strip.shape[0] - WHERE + number, 1), :] = row
+    for copy in copies:
         copy.wait()
 
 
@@ -298,14 +328,13 @@
     edge = probe.shape[-1]
     pairs = []
     for number, halo in enumerate((straight, diagonal)):
-        for t in range(tiles):
-            pairs.append(
-                (halo.at[:, :, pl.ds(t * LANES, LANES)], ext.at[1 + t, :, frame.halo_rows(number), :])
-            )
-        for side, corner in enumerate(corners):
-            pairs.append(
-                (corner.at[number], ext.at[frame.side_block(side), :, frame.halo_rows(number), :])
-            )
+        for c in range(2):
+            for t in range(tiles):
+                part = halo.at[pl.ds((2 * t + c) * margin, margin), :]
+                pairs.append((part, ext.at[1 + t, c, frame.halo_rows(number), :]))
+            for side, corner in enumerate(corners):
+                part = corner.at[pl.ds((2 * number + c) * margin, margin), :]
+                pairs.append((part, ext.at[frame.side_block(side), c, frame.halo_rows(number), :]))
     for copy in copy_all(pairs, sems):
         copy.wait()
 
@@ -334,11 +363,19 @@
         copy.wait()
 
 
-def corner_kernel(geometry, straight, diagonal, *outs):
+def corner_kernel(geometry, offsets, counts, straight, diagonal, *outs):
     frame = Frame(*geometry)
+    size = 2 * frame.margin
+    rows = where_rows(offsets, counts)
     for side, out in enumerate(outs):
-        out[0] = straight[:, :, frame.side_cols(side)]
-        out[1] = diagonal[:, :, frame.side_cols(side)]
+        for number, strip in enumerate((straight, diagonal)):
+            edge = frame.edge_tile(side) * size
+            out[pl.ds(number * size, size), :] = strip[aligned(edge, size), :]
+            out[pl.ds(2 * size + (number + 1) * WHERE, WHERE), :] = strip[
+                pl.ds(strip.shape[0] - WHERE, WHERE), :
+            ]
+        for number, row in enumerate(rows):
+            out[pl.ds(2 * size + number, 1), :] = row
 
 
 KERNEL_VMEM = 12 * MIB
@@ -382,7 +419,7 @@
         out_shape=outs,
         in_specs=[IN_SMEM] * 2 + [ANYWHERE] * (2 + sides) + [IN_VMEM] * 7,
         out_specs=[IN_VMEM] * 3 + [IN_HBM] + [IN_VMEM] * (len(outs) - 4),
-        scratch_shapes=[pltpu.SemaphoreType.DMA((16,))],
+        scratch_shapes=[pltpu.SemaphoreType.DMA((4 * (tiles + sides),))],
         input_output_aliases={base: 0, base + 1: 1, base + 2: 2},
         compiler_params=pltpu.CompilerParams(vmem_limit_bytes=KERNEL_VMEM),
         name="slots_boundary",
@@ -399,7 +436,7 @@
             out[frame.side_target(side) - 1] += value[:, frame.halo_rows(number), :]
 
 
-def light_kernel(geometry, own, *refs):
+def light_kernel(geometry, offsets, counts, *refs):
     frame = Frame(*geometry)
     others, (probe, out, canvas) = refs[:-3], refs[-3:]
     tiles = frame.tiles
@@ -430,13 +467,10 @@
 
         lax.fori_loop(0, read(2, 0), visit, 0)
 
-    add_from(lambda plane, slot: own[plane, slot])
+    add_from(lambda plane, slot: counts[0, 0] if plane == 2 else offsets[0, 0, plane, slot])
     for other in others:
-        if len(other.shape) == 2:
-            add_from(lambda plane, slot, other=other: other[plane, slot])
-        else:
-            for tile in range(other.shape[0]):
-                add_from(lambda plane, slot, other=other, tile=tile: other[tile, plane, slot])
+        for first in range(0, other.shape[0], WHERE):
+            add_from(lambda plane, slot, other=other, first=first: other[first + plane, slot])
     for t in range(tiles):
         out[t] = canvas[edge // LANES + t, 0, pl.ds(edge, frame.tile_rows), :]
 
@@ -611,7 +645,6 @@
     modes = probe_modes.shape[1]
     edge = probe_modes.shape[-1]
     margin = edge // 2
-    slots = amplitudes.shape[2]
     tiles = tile_cols // LANES
     sides = 1 if lax.axis_size("col") == 2 else 2
     geometry = (tile_rows, tile_cols, margin, sides)
@@ -621,30 +654,24 @@
 
     straight, diagonal, *edges = small_call(
         functools.partial(pack_kernel, geometry),
-        [shape(2, margin, tile_cols)] * 2 + [shape(2, tile_rows, margin)] * sides,
-        [IN_HBM],
+        [shape(2 * margin * tiles + WHERE, LANES)] * 2 + [shape(2, tile_rows, margin)] * sides,
+        [IN_SMEM, IN_SMEM, IN_HBM],
         limit=8 * MIB,
-        scratch=(pltpu.SemaphoreType.DMA((4,)),),
-    )(tile_hbm)
+        scratch=(pltpu.SemaphoreType.DMA((4 * tiles + sides,)),),
+    )(scan_offsets, scan_counts, tile_hbm)
     straight = swap_rows(straight, 0)
     diagonal = swap_rows(diagonal, 1)
     halos = swap_sides(edges)
 
-    own = jnp.concatenate(
-        [scan_offsets[0, 0], jnp.broadcast_to(scan_counts[0], (1, slots))], axis=0
-    )
-    stacked = jnp.stack([own, swap_rows(own, 0), swap_rows(own, 1)])
-    beside = swap_sides([stacked] * sides)
-
     ext, acc, sums, *consts = run_interior(
         geometry, scan_offsets, scan_counts, tile_hbm, probe_hbm, amps_hbm, tables, halos
     )
 
     cut = small_call(
         functools.partial(corner_kernel, geometry),
-        [shape(2, 2, margin, margin)] * sides,
-        [IN_VMEM] * 2,
-    )(straight, diagonal)
+        [shape(4 * margin + 3 * WHERE, LANES)] * sides,
+        [IN_SMEM] * 2 + [IN_VMEM] * 2,
+    )(scan_offsets, scan_counts, straight, diagonal)
     corners = swap_sides(cut)
 
     _, _, _, mid, *rest = run_boundary(
@@ -685,14 +712,16 @@
         shard = place(stage, pieces)
     probe_new = shard.reshape(probe_modes.shape)
 
+    others = [strip[-WHERE:].astype(jnp.int32) for strip in (straight, diagonal)]
+    others += [corner[-3 * WHERE :].astype(jnp.int32) for corner in corners]
     light = small_call(
         functools.partial(light_kernel, geometry),
         [shape(tiles, tile_rows, LANES)],
-        [IN_SMEM] * (2 + sides) + [IN_VMEM],
+        [IN_SMEM] * (4 + sides) + [IN_VMEM],
         limit=8 * MIB,
         scratch=(VMEM((tiles + 2 * (edge // LANES), 1, tile_rows + 2 * edge, LANES), F32),),
         cost=10_000_000,
-    )(own, stacked[1:], *beside, probe_modes)[0]
+    )(scan_offsets, scan_counts, *others, probe_modes)[0]
     object_new = small_call(
         functools.partial(object_kernel, geometry),
         [shape(2, tile_rows, tile_cols)],

time: 112 us -> 113 us (level)
  Pallas kernels: 14.6 us -> 17.7 us
  starting transfers between devices: 30.8 us -> 28.6 us
    pallas_call x1, Pallas kernels: 1.47 us -> 3.22 us  [run_boundary(): pl.pallas_call(functools.partial(boundary_kernel, geometry), out_shape=ou...]
    ppermute x6 -> x4, starting transfers between devices: 6.35 us -> 4.61 us  [swap_rows(): return lax.ppermute(value, 'row', pairs)]
    pallas_call x2, Pallas kernels: 1.44 us -> 2.77 us  [the longest x1 2.2 us: step(): small_call(functools.partial(pack_kernel, geometry), [shape(2 * margin *...]
    ppermute x4 -> x3, waiting for transfers between devices: 1.15 us -> 0.01 us  [swap_sides(): return [lax.ppermute(outs[0], 'col', [(0, 1), (1, 0)])]]
    ppermute x6 -> x4, waiting for transfers between devices: 33.7 us -> 33.9 us  [swap_rows(): return lax.ppermute(value, 'row', pairs)]
  transfers between devices with their start and end apart: 21 -> 18, of which waited for: 12 -> 11; matrix products, arithmetic and copies ran while one was open for 0% -> 0% of each run, Pallas kernels for 10% -> 10%
where the time goes in v4:
time: 113 us; the launch traced here: 112 us
  waiting for transfers between devices  63.5 us (56%)
  starting transfers between devices  28.6 us (25%)
  Pallas kernels  17.7 us (16%)
  between operations  1.53 us (1%)
    ppermute x4, waiting for transfers between devices, swap_rows(): return lax.ppermute(value, 'row', pairs)  33.9 us
    ppermute x5, starting transfers between devices, step(): lax.ppermute(piece, axis, member_perm(axis, bits, member + 1))  20 us
    ppermute x5, waiting for transfers between devices, step(): lax.ppermute(piece, axis, member_perm(axis, bits, member + 1))  16.3 us
    ppermute x5, waiting for transfers between devices, step(): lax.ppermute(shard, axis, member_perm(axis, bits, member))  8.9 us
    pallas_call x1, Pallas kernels, run_interior(): pl.pallas_call(functools.partial(interior_kernel, geometry), out_shape=ou...  6.68 us
    ppermute x4, starting transfers between devices, swap_rows(): return lax.ppermute(value, 'row', pairs)  4.61 us
    ppermute x1, waiting for transfers between devices, step(): parts = [total, lax.ppermute(total, last[0], member_perm(*last, 1))]  4.43 us
    ppermute x5, starting transfers between devices, step(): lax.ppermute(shard, axis, member_perm(axis, bits, member))  3.7 us
  transfers between devices with their start and end apart: 18, of which 11 were waited for; matrix products, arithmetic and copies ran while one was open for 0% of the time, Pallas kernels for 10%

profile of v4, /device:TPU:0, one launch (start us, length us, event | category | flops | bytes accessed | tf_op | source)
XLA Modules:
  0.0 112.1 jit_solution(3098014905001072938)
XLA Ops:
  1.3 0.7 copy-done.2
  2.0 2.2 %shard_map.86 = (f32[1032,128]{1,0:T(8,128)S(1)}, f32[1032,128]{1,0:T(8,128)S(1)}, f32[2,512,128]{2,1,0:T(8,128)S(1)}) custom-call(s32[1,1,2,6]{3,2,1,0:T(2,128)S(1)} %copy-done.2, s32[1,1]{1,0:T(1,128)S(6)} %copy.15.counts, f32[2,512,512]{2,1,0:T(8,128)} %tile.5), custom_call_target="tpu_custom_call" | custom-call | tf_op jit(solution)/shard_map/pallas_call | solution.py:655
  4.2 3.0 %collective-permute-start = (f32[1032,128]{1,0:T(8,128)S(1)}, f32[1032,128]{1,0:T(8,128)S(1)}, u32[]{:S(2)}, u32[]{:S(2)}) collective-permute-start(f32[1032,128]{1,0:T(8,128)S(1)} %get-tuple-element.26), channel_id=1, source_target_pairs={{0,2},{2,0},{4,6},{6,4},{8,10},{10,8},{12,14},{14,12},{16,18},{18,... | collective-permute-start | bytes 1585160 | tf_op jit(solution)/shard_map/ppermute | solution.py:630
  7.2 0.7 collective-permute-start.1
  8.0 21.8 %collective-permute-done.straight = f32[1032,128]{1,0:T(8,128)S(1)} collective-permute-done((f32[1032,128]{1,0:T(8,128)S(1)}, f32[1032,128]{1,0:T(8,128)S(1)}, u32[]{:S(2)}, u32[]{:S(2)}) %collective-permute-start) | collective-permute-done | bytes 528416 | tf_op jit(solution)/shard_map/ppermute | solution.py:630
  29.8 0.6 shard_map.87
  30.4 0.1 collective-permute-start.2
  30.5 6.7 %slots_interior.1 = (f32[6,2,768,128]{3,2,1,0:T(8,128)S(1)}, f32[6,2,768,128]{3,2,1,0:T(8,128)S(1)}, f32[5,256,256]{2,1,0:T(8,128)S(1)}, f32[2,2,256,256]{3,2,1,...) custom-call(s32[1,1,2,6]{3,2,1,0:T(2,128)S(1)} %copy-done.3, ...), custom_call_target="tpu_custom_call" | custom-call | flops 10000000000 | bytes 20000000 | tf_op jit(solution)/shard_map/slots_interior/pallas_call | solution.py:395
  37.2 3.2 %slots_boundary.1 = (f32[6,2,768,128]{3,2,1,0:T(8,128)S(1)}, f32[6,2,768,128]{3,2,1,0:T(8,128)S(1)}, f32[5,256,256]{2,1,0:T(8,128)S(1)}, f32[4,2,512,128]{3,2,1,...) custom-call(s32[1,1,2,6]{3,2,1,0:T(2,128)S(1)} %copy-done.3, ...), custom_call_target="tpu_custom_call", output_to_operand_aliasing={{0}: (9, {}), {1}: (10, {}), {2}: (11, {})} | custom-call | flops 10000000000 | bytes 20000000 | tf_op jit(solution)/shard_map/slots_boundary/pallas_call | solution.py:417
  40.4 0.6 collective-permute-start.7
  41.0 0.1 collective-permute-start.4
  41.1 1.6 %collective-permute-done.7.refs_1_ = f32[5,128,256]{2,1,0:T(8,128)S(1)} collective-permute-done((f32[5,128,256]{2,1,0:T(8,128)S(1)}, f32[5,128,256]{2,1,0:T(8,128)S(1)}, u32[]{:S(2)}, u32[]{:S(2)}) %collective-permute-start.7) | collective-permute-done | bytes 655392 | tf_op jit(solution)/shard_map/ppermute | solution.py:690
  42.7 0.1 shard_map.91
  42.8 18.7 %collective-permute-start.10 = (f32[5,32,256]{2,1,0:T(8,128)S(1)}, f32[5,32,256]{2,1,0:T(8,128)S(1)}, u32[]{:S(2)}, u32[]{:S(2)}) collective-permute-start(f32[5,32,256]{2,1,0:T(8,128)S(1)} %get-tuple-element.47), channel_id=1, source_target_pairs={{0,12},{2,14},{4,8},{6,10},{8,4},{10,6},{12,0},{14,2},{16,28},{18,... | collective-permute-start | bytes 491528 | tf_op jit(solution)/shard_map/ppermute | solution.py:690
  61.5 0.6 collective-permute-start.9
  62.1 4.4 %collective-permute-done.10.refs_3_ = f32[5,32,256]{2,1,0:T(8,128)S(1)} collective-permute-done((f32[5,32,256]{2,1,0:T(8,128)S(1)}, f32[5,32,256]{2,1,0:T(8,128)S(1)}, u32[]{:S(2)}, u32[]{:S(2)}) %collective-permute-start.10) | collective-permute-done | bytes 163872 | tf_op jit(solution)/shard_map/ppermute | solution.py:690
  66.6 3.2 %collective-permute-done.8.refs_1_ = f32[5,32,256]{2,1,0:T(8,128)S(1)} collective-permute-done((f32[5,32,256]{2,1,0:T(8,128)S(1)}, f32[5,32,256]{2,1,0:T(8,128)S(1)}, u32[]{:S(2)}, u32[]{:S(2)}) %collective-permute-start.8) | collective-permute-done | bytes 163872 | tf_op jit(solution)/shard_map/ppermute | solution.py:690
  69.9 7.0 %collective-permute-done.11.refs_1_ = f32[5,16,256]{2,1,0:T(8,128)S(1)} collective-permute-done((f32[5,16,256]{2,1,0:T(8,128)S(1)}, f32[5,16,256]{2,1,0:T(8,128)S(1)}, u32[]{:S(2)}, u32[]{:S(2)}) %collective-permute-start.11) | collective-permute-done | bytes 81952 | tf_op jit(solution)/shard_map/ppermute | solution.py:690
  77.0 4.4 %collective-permute-done.12.refs_1_ = f32[5,16,256]{2,1,0:T(8,128)S(1)} collective-permute-done((f32[5,16,256]{2,1,0:T(8,128)S(1)}, f32[5,16,256]{2,1,0:T(8,128)S(1)}, u32[]{:S(2)}, u32[]{:S(2)}) %collective-permute-start.12) | collective-permute-done | bytes 81952 | tf_op jit(solution)/shard_map/ppermute | solution.py:694
  81.5 5.6 %collective-permute-done.13.refs_1_ = f32[4,16,256]{2,1,0:T(8,128)S(1)} collective-permute-done((f32[4,16,256]{2,1,0:T(8,128)S(1)}, f32[4,16,256]{2,1,0:T(8,128)S(1)}, u32[]{:S(2)}, u32[]{:S(2)}) %collective-permute-start.13) | collective-permute-done | bytes 65568 | tf_op jit(solution)/shard_map/ppermute | solution.py:709
  87.1 0.6 collective-permute-start.14
  87.7 3.0 %collective-permute-start.16 = (f32[4,32,256]{2,1,0:T(8,128)S(1)}, f32[4,32,256]{2,1,0:T(8,128)S(1)}, u32[]{:S(2)}, u32[]{:S(2)}) collective-permute-start(f32[4,32,256]{2,1,0:T(8,128)S(1)} %shard_map.95.refs_0_), channel_id=1, source_target_pairs={{0,12},{2,14},{4,8},{6,10},{8,4},{10,6},{12,0},{14,2},{16,28},{18,... | collective-permute-start | bytes 393224 | tf_op jit(solution)/shard_map/ppermute | solution.py:709
  90.7 0.1 shard_map.89
  90.8 0.1 collective-permute-start.5
  90.9 0.8 collective-permute-start.6
  91.7 0.5 collective-permute-done.14.refs_1_
  92.1 1.5 %collective-permute-done.15.refs_2_ = f32[4,32,256]{2,1,0:T(8,128)S(1)} collective-permute-done((f32[4,32,256]{2,1,0:T(8,128)S(1)}, f32[4,32,256]{2,1,0:T(8,128)S(1)}, u32[]{:S(2)}, u32[]{:S(2)}) %collective-permute-start.15) | collective-permute-done | bytes 131104 | tf_op jit(solution)/shard_map/ppermute | solution.py:709
  93.7 1.3 %collective-permute-done.16.refs_3_ = f32[4,32,256]{2,1,0:T(8,128)S(1)} collective-permute-done((f32[4,32,256]{2,1,0:T(8,128)S(1)}, f32[4,32,256]{2,1,0:T(8,128)S(1)}, u32[]{:S(2)}, u32[]{:S(2)}) %collective-permute-start.16) | collective-permute-done | bytes 131104 | tf_op jit(solution)/shard_map/ppermute | solution.py:709
  95.2 1.7 %shard_map.88.light = f32[4,512,128]{2,1,0:T(8,128)S(1)} custom-call(s32[1,1,2,6]{3,2,1,0:T(2,128)S(1)} %copy-done.3, s32[1,1]{1,0:T(1,128)S(6)} %copy.15.counts, s32[8,128]{1,0:T(8,128)S(1)} %slice_convert_fusion.2.refs_0_, s32[8,128]{1,0:T(8,128)S(1)} %slice_convert_fusion.1.refs_1_, s32[24,128]{1,0:T(8,128)S(1)} %slice_convert_fusion.refs_2_, ...), custom_call_target="tpu_custom_call" | custom-call | flops 10000000 | bytes 1000000 | tf_op jit(solution)/shard_map/pallas_call | solution.py:717
  96.9 12.1 %collective-permute-done.5.from_straight = f32[4,2,128,128]{3,2,1,0:T(8,128)S(1)} collective-permute-done((f32[4,2,128,128]{3,2,1,0:T(8,128)S(1)}, f32[4,2,128,128]{3,2,1,0:T(8,128)S(1)}, u32[]{:S(2)}, u32[]{:S(2)}) %collective-permute-start.5) | collective-permute-done | bytes 524320 | tf_op jit(solution)/shard_map/ppermute | solution.py:630
  109.0 2.0 %shard_map.90 = f32[2,512,512]{2,1,0:T(8,128)} custom-call(f32[2,512,512]{2,1,0:T(8,128)S(1)} %copy-done, f32[4,2,512,128]{3,2,1,0:T(8,128)S(1)} %get-tuple-element.36.mid, f32[4,512,128]{2,1,0:T(8,128)S(1)} %shard_map.88.light, f32[4,2,128,128]{3,2,1,0:T(8,128)S(1)} %collective-permute-done.5.from_straight, ...), custom_call_target="tpu_custom_call" | custom-call | tf_op jit(solution)/shard_map/pallas_call | solution.py:725
  111.0 1.0 shard_map.97
  (29 shorter events, 0.5 us)
Async XLA Ops:
  0.6 29.9 %copy-start.3 = (s32[1,1,2,6]{3,2,1,0:T(2,128)S(1)}, s32[1,1,2,6]{3,2,1,0:T(2,128)}, u32[]{:S(2)}) copy-start(s32[1,1,2,6]{3,2,1,0:T(2,128)} %offsets.9) | copy-start | bytes 148
  1.3 0.7 copy-start.2
  4.2 25.6 %collective-permute-start = (f32[1032,128]{1,0:T(8,128)S(1)}, f32[1032,128]{1,0:T(8,128)S(1)}, u32[]{:S(2)}, u32[]{:S(2)}) collective-permute-start(f32[1032,128]{1,0:T(8,128)S(1)} %get-tuple-element.26), channel_id=1, source_target_pairs={{0,2},{2,0},{4,6},{6,4},{8,10},{10,8},{12,14},{14,12},{16,18},{18,... | collective-permute-start | bytes 1585160 | tf_op jit(solution)/shard_map/ppermute | solution.py:630
  7.2 22.6 %collective-permute-start.1 = (f32[1032,128]{1,0:T(8,128)S(1)}, f32[1032,128]{1,0:T(8,128)S(1)}, u32[]{:S(2)}, u32[]{:S(2)}) collective-permute-start(f32[1032,128]{1,0:T(8,128)S(1)} %get-tuple-element.27), channel_id=1, source_target_pairs={{2,4},{4,2},{6,8},{8,6},{10,12},{12,10},{14,16},{16,14},{18,20},{2... | collective-permute-start | bytes 1585160 | tf_op jit(solution)/shard_map/ppermute | solution.py:630
  7.9 22.6 %collective-permute-start.3 = (f32[2,512,128]{2,1,0:T(8,128)S(1)}, f32[2,512,128]{2,1,0:T(8,128)S(1)}, u32[]{:S(2)}, u32[]{:S(2)}) collective-permute-start(f32[2,512,128]{2,1,0:T(8,128)S(1)} %get-tuple-element.28), channel_id=1, source_target_pairs={{0,1},{1,0},{2,3},{3,2},{4,5},{5,4},{6,7},{7,6},{8,9},{9,8},{10,11... | collective-permute-start | bytes 1572872 | tf_op jit(solution)/shard_map/ppermute | solution.py:619
  30.4 6.8 %collective-permute-start.2 = (f32[536,128]{1,0:T(8,128)S(1)}, f32[536,128]{1,0:T(8,128)S(1)}, u32[]{:S(2)}, u32[]{:S(2)}) collective-permute-start(f32[536,128]{1,0:T(8,128)S(1)} %shard_map.87), channel_id=1, source_target_pairs={{0,1},{1,0},{2,3},{3,2},{4,5},{5,4},{6,7},{7,6},{8,9},{9,8},{10,11... | collective-permute-start | bytes 823304 | tf_op jit(solution)/shard_map/ppermute | solution.py:619
  40.4 41.0 %copy-start.1 = (f32[2,2,256,256]{3,2,1,0:T(8,128)S(1)}, f32[2,2,256,256]{3,2,1,0:T(8,128)}, u32[]{:S(2)}) copy-start(f32[2,2,256,256]{3,2,1,0:T(8,128)} %refs_3_.1) | copy-start | bytes 3145732
  40.4 2.3 %collective-permute-start.7 = (f32[5,128,256]{2,1,0:T(8,128)S(1)}, f32[5,128,256]{2,1,0:T(8,128)S(1)}, u32[]{:S(2)}, u32[]{:S(2)}) collective-permute-start(f32[5,128,256]{2,1,0:T(8,128)S(1)} %get-tuple-element.43), channel_id=1, source_target_pairs={{0,1},{1,0},{2,3},{3,2},{4,5},{5,4},{6,7},{7,6},{8,9},{9,8},{10,11... | collective-permute-start | bytes 1966088 | tf_op jit(solution)/shard_map/ppermute | solution.py:690
  41.0 49.7 %collective-permute-start.4 = (f32[2,768,128]{2,1,0:T(8,128)S(1)}, f32[2,768,128]{2,1,0:T(8,128)S(1)}, u32[]{:S(2)}, u32[]{:S(2)}) collective-permute-start(f32[2,768,128]{2,1,0:T(8,128)S(1)} %get-tuple-element.39), channel_id=1, source_target_pairs={{0,1},{1,0},{2,3},{3,2},{4,5},{5,4},{6,7},{7,6},{8,9},{9,8},{10,11... | collective-permute-start | bytes 2359304 | tf_op jit(solution)/shard_map/ppermute | solution.py:619
  42.8 23.7 %collective-permute-start.10 = (f32[5,32,256]{2,1,0:T(8,128)S(1)}, f32[5,32,256]{2,1,0:T(8,128)S(1)}, u32[]{:S(2)}, u32[]{:S(2)}) collective-permute-start(f32[5,32,256]{2,1,0:T(8,128)S(1)} %get-tuple-element.47), channel_id=1, source_target_pairs={{0,12},{2,14},{4,8},{6,10},{8,4},{10,6},{12,0},{14,2},{16,28},{18,... | collective-permute-start | bytes 491528 | tf_op jit(solution)/shard_map/ppermute | solution.py:690
  61.5 8.2 %collective-permute-start.8 = (f32[5,32,256]{2,1,0:T(8,128)S(1)}, f32[5,32,256]{2,1,0:T(8,128)S(1)}, u32[]{:S(2)}, u32[]{:S(2)}) collective-permute-start(f32[5,32,256]{2,1,0:T(8,128)S(1)} %get-tuple-element.45), channel_id=1, source_target_pairs={{0,4},{2,6},{4,0},{6,2},{8,12},{10,14},{12,8},{14,10},{16,20},{18,... | collective-permute-start | bytes 491528 | tf_op jit(solution)/shard_map/ppermute | solution.py:690
  61.5 8.2 %collective-permute-start.9 = (f32[5,32,256]{2,1,0:T(8,128)S(1)}, f32[5,32,256]{2,1,0:T(8,128)S(1)}, u32[]{:S(2)}, u32[]{:S(2)}) collective-permute-start(f32[5,32,256]{2,1,0:T(8,128)S(1)} %get-tuple-element.46), channel_id=1, source_target_pairs={{0,8},{2,10},{4,12},{6,14},{8,0},{10,2},{12,4},{14,6},{16,24},{18,... | collective-permute-start | bytes 491528 | tf_op jit(solution)/shard_map/ppermute | solution.py:690
  69.8 7.1 %collective-permute-start.11 = (f32[5,16,256]{2,1,0:T(8,128)S(1)}, f32[5,16,256]{2,1,0:T(8,128)S(1)}, u32[]{:S(2)}, u32[]{:S(2)}) collective-permute-start(f32[5,16,256]{2,1,0:T(8,128)S(1)} %get-tuple-element.49), channel_id=1, source_target_pairs={{0,16},{2,18},{4,20},{6,22},{8,24},{10,26},{12,28},{14,30},{16,0},... | collective-permute-start | bytes 245768 | tf_op jit(solution)/shard_map/ppermute | solution.py:690
  76.9 4.5 %collective-permute-start.12 = (f32[5,16,256]{2,1,0:T(8,128)S(1)}, f32[5,16,256]{2,1,0:T(8,128)S(1)}, u32[]{:S(2)}, u32[]{:S(2)}) collective-permute-start(f32[5,16,256]{2,1,0:T(8,128)S(1)} %shard_map.93.refs_0_), channel_id=1, source_target_pairs={{0,2},{2,0},{4,6},{6,4},{8,10},{10,8},{12,14},{14,12},{16,18},{18,... | collective-permute-start | bytes 245768 | tf_op jit(solution)/shard_map/ppermute | solution.py:694
  81.4 5.7 %collective-permute-start.13 = (f32[4,16,256]{2,1,0:T(8,128)S(1)}, f32[4,16,256]{2,1,0:T(8,128)S(1)}, u32[]{:S(2)}, u32[]{:S(2)}) collective-permute-start(f32[4,16,256]{2,1,0:T(8,128)S(1)} %shard_map.94.refs_0_), channel_id=1, source_target_pairs={{0,16},{2,18},{4,20},{6,22},{8,24},{10,26},{12,28},{14,30},{16,0},... | collective-permute-start | bytes 196616 | tf_op jit(solution)/shard_map/ppermute | solution.py:709
  87.1 5.0 %collective-permute-start.14 = (f32[4,32,256]{2,1,0:T(8,128)S(1)}, f32[4,32,256]{2,1,0:T(8,128)S(1)}, u32[]{:S(2)}, u32[]{:S(2)}) collective-permute-start(f32[4,32,256]{2,1,0:T(8,128)S(1)} %shard_map.95.refs_0_), channel_id=1, source_target_pairs={{0,4},{2,6},{4,0},{6,2},{8,12},{10,14},{12,8},{14,10},{16,20},{18,... | collective-permute-start | bytes 393224 | tf_op jit(solution)/shard_map/ppermute | solution.py:709
  87.7 6.0 %collective-permute-start.15 = (f32[4,32,256]{2,1,0:T(8,128)S(1)}, f32[4,32,256]{2,1,0:T(8,128)S(1)}, u32[]{:S(2)}, u32[]{:S(2)}) collective-permute-start(f32[4,32,256]{2,1,0:T(8,128)S(1)} %shard_map.95.refs_0_), channel_id=1, source_target_pairs={{0,8},{2,10},{4,12},{6,14},{8,0},{10,2},{12,4},{14,6},{16,24},{18,... | collective-permute-start | bytes 393224 | tf_op jit(solution)/shard_map/ppermute | solution.py:709
  87.7 7.3 %collective-permute-start.16 = (f32[4,32,256]{2,1,0:T(8,128)S(1)}, f32[4,32,256]{2,1,0:T(8,128)S(1)}, u32[]{:S(2)}, u32[]{:S(2)}) collective-permute-start(f32[4,32,256]{2,1,0:T(8,128)S(1)} %shard_map.95.refs_0_), channel_id=1, source_target_pairs={{0,12},{2,14},{4,8},{6,10},{8,4},{10,6},{12,0},{14,2},{16,28},{18,... | collective-permute-start | bytes 393224 | tf_op jit(solution)/shard_map/ppermute | solution.py:709
  90.7 18.4 %copy-start = (f32[2,512,512]{2,1,0:T(8,128)S(1)}, f32[2,512,512]{2,1,0:T(8,128)}, u32[]{:S(2)}) copy-start(f32[2,512,512]{2,1,0:T(8,128)} %tile.5) | copy-start | bytes 6291460
  90.8 18.2 %collective-permute-start.5 = (f32[4,2,128,128]{3,2,1,0:T(8,128)S(1)}, f32[4,2,128,128]{3,2,1,0:T(8,128)S(1)}, u32[]{:S(2)}, u32[]{:S(2)}) collective-permute-start(f32[4,2,128,128]{3,2,1,0:T(8,128)S(1)} %get-tuple-element.40), channel_id=1, source_target_pairs={{0,2},{2,0},{4,6},{6,4},{8,10},{10,8},{12,14},{14,12},{16,18},{18,... | collective-permute-start | bytes 1572872 | tf_op jit(solution)/shard_map/ppermute | solution.py:630
  90.9 18.2 %collective-permute-start.6 = (f32[4,2,128,128]{3,2,1,0:T(8,128)S(1)}, f32[4,2,128,128]{3,2,1,0:T(8,128)S(1)}, u32[]{:S(2)}, u32[]{:S(2)}) collective-permute-start(f32[4,2,128,128]{3,2,1,0:T(8,128)S(1)} %get-tuple-element.41), channel_id=1, source_target_pairs={{2,4},{4,2},{6,8},{8,6},{10,12},{12,10},{14,16},{16,14},{18,20},{2... | collective-permute-start | bytes 1572872 | tf_op jit(solution)/shard_map/ppermute | solution.py:630
  95.1 15.9 %collective-permute-start.17 = (f32[4,128,256]{2,1,0:T(8,128)S(1)}, f32[4,128,256]{2,1,0:T(8,128)S(1)}, u32[]{:S(2)}, u32[]{:S(2)}) collective-permute-start(f32[4,128,256]{2,1,0:T(8,128)S(1)} %shard_map.96.refs_0_), channel_id=1, source_target_pairs={{0,1},{1,0},{2,3},{3,2},{4,5},{5,4},{6,7},{7,6},{8,9},{9,8},{10,11... | collective-permute-start | bytes 1572872 | tf_op jit(solution)/shard_map/ppermute | solution.py:709

commit v5 on v3

--- a/solution.py
+++ b/solution.py
@@ -26,24 +26,13 @@
     scale = 1.0 / math.sqrt(edge)
     n = np.arange(half)[:, None]
     k = np.arange(half)[None, :]
-    right, left = [], []
+    mats = []
     for parity in (0, 1):
         angle = (n * (2 * k + parity) % edge) * (2.0 * np.pi / edge)
         cosine, sine = np.cos(angle) * scale, np.sin(angle) * scale
-        w = np.block([[cosine, -sine], [sine, cosine]])
-        right.append(w)
-        left.append(w.T)
-    mats = [right[0], right[1], left[0], left[1]]
-    as_right = []
-    as_left = []
-    for m in mats:
-        high, low = split_host(m)
-        as_right.append(np.concatenate([high, high, low], axis=0))
-        as_left.append(np.concatenate([high, high, low], axis=1))
-    return (
-        np.stack([as_right[0], as_right[1], as_right[2], as_right[3]]),
-        np.stack([as_left[2], as_left[3], as_left[0], as_left[1]]),
-    )
+        mats.append(np.block([[cosine, -sine], [sine, cosine]]))
+    mats += [mats[0].T, mats[1].T]
+    return np.stack([np.stack(split_host(m)) for m in mats])
 
 
 def split_parts(x):
@@ -243,13 +232,18 @@
         add_window(acc, c, update[c], row, block, shift)
 
 
-def interior_kernel(geometry, offsets, counts, tile, probe_in, amps_in, rights_in, lefts_in, *refs):
+def interior_kernel(geometry, offsets, counts, tile, probe_in, amps_in, tables, *refs):
     frame = Frame(*geometry)
     halos = refs[: frame.sides]
     ext, acc, sums, probe, amps, rights, lefts, raw, sems = refs[frame.sides :]
     tiles, body, margin = frame.tiles, frame.body, frame.margin
     edge = probe.shape[-1]
-    pairs = [(amps_in.at[0, 0], raw), (probe_in, probe), (rights_in, rights), (lefts_in, lefts)]
+    pairs = [(amps_in.at[0, 0], raw), (probe_in, probe)]
+    for m in range(4):
+        for third, part in enumerate((0, 0, 1)):
+            span = pl.ds(third * edge, edge)
+            pairs.append((tables.at[m, part], rights.at[m, span, :]))
+            pairs.append((tables.at[(m + 2) % 4, part], lefts.at[m, :, span]))
     for number, halo in enumerate(halos):
         pairs.append((halo, ext.at[frame.side_block(number), :, body, :]))
     for t in range(tiles):
@@ -354,17 +348,23 @@
     window = shape(tile_cols // LANES + 2, 2, tile_rows + 2 * margin, LANES)
     amp_shape = jax.ShapeDtypeStruct(amps.shape[2:], BF16)
     outs = [window, window, shape(2 * modes + 1, edge, edge), shape(*probe.shape), amp_shape]
-    outs += [jax.ShapeDtypeStruct(t.shape, t.dtype) for t in tables]
+    outs += [
+        jax.ShapeDtypeStruct((4, 3 * edge, edge), BF16),
+        jax.ShapeDtypeStruct((4, edge, 3 * edge), BF16),
+    ]
     return pl.pallas_call(
         functools.partial(interior_kernel, geometry),
         out_shape=outs,
-        in_specs=[IN_SMEM] * 2 + [IN_HBM] * 5 + [ANYWHERE] * sides,
+        in_specs=[IN_SMEM] * 2 + [IN_HBM] * 4 + [ANYWHERE] * sides,
         out_specs=[IN_VMEM] * len(outs),
-        scratch_shapes=[VMEM(amp_shape.shape, BF16), pltpu.SemaphoreType.DMA((16,))],
+        scratch_shapes=[
+            VMEM(amp_shape.shape, BF16),
+            pltpu.SemaphoreType.DMA((26 + sides + tile_cols // LANES,)),
+        ],
         compiler_params=pltpu.CompilerParams(vmem_limit_bytes=KERNEL_VMEM),
         name="slots_interior",
         **SLOT_COST,
-    )(offsets, counts, tile, probe, amps, *tables, *halos)
+    )(offsets, counts, tile, probe, amps, tables, *halos)
 
 
 def run_boundary(geometry, offsets, counts, straight, diagonal, corners, consts, ext, acc, sums):
@@ -616,7 +616,7 @@
     sides = 1 if lax.axis_size("col") == 2 else 2
     geometry = (tile_rows, tile_cols, margin, sides)
     stages, last = stages_of(lax.axis_size("row"), lax.axis_size("col"))
-    tables = tuple(in_hbm(jnp.asarray(t)) for t in dft_tables(edge))
+    tables = in_hbm(jnp.asarray(dft_tables(edge)))
     tile_hbm, probe_hbm, amps_hbm = in_hbm(object_field), in_hbm(probe_modes), in_hbm(amplitudes)
 
     straight, diagonal, *edges = small_call(

time: 112 us -> 112 us (level)
  no operation moved by 1% of the time
where the time goes in v5:
time: 112 us
  waiting for transfers between devices  64.6 us (58%)
  starting transfers between devices  30.7 us (27%)
  Pallas kernels  14.8 us (13%)
  between operations  1.54 us (1%)
    ppermute x6, waiting for transfers between devices, swap_rows(): return lax.ppermute(value, 'row', pairs)  33.7 us
    ppermute x5, starting transfers between devices, step(): lax.ppermute(piece, axis, member_perm(axis, bits, member + 1))  20.3 us
    ppermute x5, waiting for transfers between devices, step(): lax.ppermute(piece, axis, member_perm(axis, bits, member + 1))  16.2 us
    ppermute x5, waiting for transfers between devices, step(): lax.ppermute(shard, axis, member_perm(axis, bits, member))  9.08 us
    pallas_call x1, Pallas kernels, run_interior(): pl.pallas_call(functools.partial(interior_kernel, geometry), out_shape=ou...  7.02 us
    ppermute x6, starting transfers between devices, swap_rows(): return lax.ppermute(value, 'row', pairs)  6.35 us
    ppermute x1, waiting for transfers between devices, step(): parts = [total, lax.ppermute(total, last[0], member_perm(*last, 1))]  4.43 us
    ppermute x5, starting transfers between devices, step(): lax.ppermute(shard, axis, member_perm(axis, bits, member))  3.7 us
  transfers between devices with their start and end apart: 21, of which 12 were waited for; matrix products, arithmetic and copies ran while one was open for 0% of the time, Pallas kernels for 10%

profile of v5, /device:TPU:0, one launch (start us, length us, event | category | flops | bytes accessed | tf_op | source)
XLA Modules:
  0.0 111.7 jit_solution(8777285950035922364)
XLA Ops:
  0.6 1.4 %shard_map.77 = (f32[2,128,512]{2,1,0:T(8,128)S(1)}, f32[2,128,512]{2,1,0:T(8,128)S(1)}, f32[2,512,128]{2,1,0:T(8,128)S(1)}) custom-call(f32[2,512,512]{2,1,0:T(8,128)} %tile.5), custom_call_target="tpu_custom_call" | custom-call | tf_op jit(solution)/shard_map/pallas_call | solution.py:622
  2.1 3.0 %collective-permute-start = (f32[2,128,512]{2,1,0:T(8,128)S(1)}, f32[2,128,512]{2,1,0:T(8,128)S(1)}, u32[]{:S(2)}, u32[]{:S(2)}) collective-permute-start(f32[2,128,512]{2,1,0:T(8,128)S(1)} %get-tuple-element.26), channel_id=1, source_target_pairs={{0,2},{2,0},{4,6},{6,4},{8,10},{10,8},{12,14},{14,12},{16,18},{18,... | collective-permute-start | bytes 1572872 | tf_op jit(solution)/shard_map/ppermute | solution.py:596
  5.1 0.7 collective-permute-start.1
  5.8 0.1 collective-permute-start.3
  6.5 21.0 %collective-permute-done.straight = f32[2,128,512]{2,1,0:T(8,128)S(1)} collective-permute-done((f32[2,128,512]{2,1,0:T(8,128)S(1)}, f32[2,128,512]{2,1,0:T(8,128)S(1)}, u32[]{:S(2)}, u32[]{:S(2)}) %collective-permute-start) | collective-permute-done | bytes 524320 | tf_op jit(solution)/shard_map/ppermute | solution.py:596
  27.6 7.0 %slots_interior.1 = (f32[6,2,768,128]{3,2,1,0:T(8,128)S(1)}, f32[6,2,768,128]{3,2,1,0:T(8,128)S(1)}, f32[5,256,256]{2,1,0:T(8,128)S(1)}, f32[2,2,256,256]{3,2,1,...) custom-call(s32[1,1,2,6]{3,2,1,0:T(2,128)S(1)} %copy-done.2, ...), custom_call_target="tpu_custom_call" | custom-call | flops 10000000000 | bytes 20000000 | tf_op jit(solution)/shard_map/slots_interior/pallas_call | solution.py:355
  34.7 1.5 %slots_boundary.1 = (f32[6,2,768,128]{3,2,1,0:T(8,128)S(1)}, f32[6,2,768,128]{3,2,1,0:T(8,128)S(1)}, f32[5,256,256]{2,1,0:T(8,128)S(1)}, f32[4,2,512,128]{3,2,1,...) custom-call(s32[1,1,2,6]{3,2,1,0:T(2,128)S(1)} %copy-done.2, ...), custom_call_target="tpu_custom_call", output_to_operand_aliasing={{0}: (9, {}), {1}: (10, {}), {2}: (11, {})} | custom-call | flops 10000000000 | bytes 20000000 | tf_op jit(solution)/shard_map/slots_boundary/pallas_call | solution.py:380
  36.2 0.6 collective-permute-start.10
  36.7 0.1 collective-permute-start.7
  36.8 1.6 %collective-permute-done.10.refs_1_ = f32[5,128,256]{2,1,0:T(8,128)S(1)} collective-permute-done((f32[5,128,256]{2,1,0:T(8,128)S(1)}, f32[5,128,256]{2,1,0:T(8,128)S(1)}, u32[]{:S(2)}, u32[]{:S(2)}) %collective-permute-start.10) | collective-permute-done | bytes 655392 | tf_op jit(solution)/shard_map/ppermute | solution.py:663
  38.5 14.6 %collective-permute-start.11 = (f32[5,32,256]{2,1,0:T(8,128)S(1)}, f32[5,32,256]{2,1,0:T(8,128)S(1)}, u32[]{:S(2)}, u32[]{:S(2)}) collective-permute-start(f32[5,32,256]{2,1,0:T(8,128)S(1)} %get-tuple-element.45), channel_id=1, source_target_pairs={{0,4},{2,6},{4,0},{6,2},{8,12},{10,14},{12,8},{14,10},{16,20},{18,... | collective-permute-start | bytes 491528 | tf_op jit(solution)/shard_map/ppermute | solution.py:663
  53.1 5.1 %collective-permute-start.12 = (f32[5,32,256]{2,1,0:T(8,128)S(1)}, f32[5,32,256]{2,1,0:T(8,128)S(1)}, u32[]{:S(2)}, u32[]{:S(2)}) collective-permute-start(f32[5,32,256]{2,1,0:T(8,128)S(1)} %get-tuple-element.46), channel_id=1, source_target_pairs={{0,8},{2,10},{4,12},{6,14},{8,0},{10,2},{12,4},{14,6},{16,24},{18,... | collective-permute-start | bytes 491528 | tf_op jit(solution)/shard_map/ppermute | solution.py:663
  58.2 5.0 %collective-permute-done.12.refs_2_ = f32[5,32,256]{2,1,0:T(8,128)S(1)} collective-permute-done((f32[5,32,256]{2,1,0:T(8,128)S(1)}, f32[5,32,256]{2,1,0:T(8,128)S(1)}, u32[]{:S(2)}, u32[]{:S(2)}) %collective-permute-start.12) | collective-permute-done | bytes 163872 | tf_op jit(solution)/shard_map/ppermute | solution.py:663
  63.3 2.7 %collective-permute-done.13.refs_3_ = f32[5,32,256]{2,1,0:T(8,128)S(1)} collective-permute-done((f32[5,32,256]{2,1,0:T(8,128)S(1)}, f32[5,32,256]{2,1,0:T(8,128)S(1)}, u32[]{:S(2)}, u32[]{:S(2)}) %collective-permute-start.13) | collective-permute-done | bytes 163872 | tf_op jit(solution)/shard_map/ppermute | solution.py:663
  66.1 6.8 %collective-permute-done.14.refs_1_ = f32[5,16,256]{2,1,0:T(8,128)S(1)} collective-permute-done((f32[5,16,256]{2,1,0:T(8,128)S(1)}, f32[5,16,256]{2,1,0:T(8,128)S(1)}, u32[]{:S(2)}, u32[]{:S(2)}) %collective-permute-start.14) | collective-permute-done | bytes 81952 | tf_op jit(solution)/shard_map/ppermute | solution.py:663
  73.0 4.4 %collective-permute-done.15.refs_1_ = f32[5,16,256]{2,1,0:T(8,128)S(1)} collective-permute-done((f32[5,16,256]{2,1,0:T(8,128)S(1)}, f32[5,16,256]{2,1,0:T(8,128)S(1)}, u32[]{:S(2)}, u32[]{:S(2)}) %collective-permute-start.15) | collective-permute-done | bytes 81952 | tf_op jit(solution)/shard_map/ppermute | solution.py:667
  77.5 5.8 %collective-permute-done.16.refs_1_ = f32[4,16,256]{2,1,0:T(8,128)S(1)} collective-permute-done((f32[4,16,256]{2,1,0:T(8,128)S(1)}, f32[4,16,256]{2,1,0:T(8,128)S(1)}, u32[]{:S(2)}, u32[]{:S(2)}) %collective-permute-start.16) | collective-permute-done | bytes 65568 | tf_op jit(solution)/shard_map/ppermute | solution.py:682
  83.3 0.1 collective-permute-start.17
  83.4 1.3 %collective-permute-start.18 = (f32[4,32,256]{2,1,0:T(8,128)S(1)}, f32[4,32,256]{2,1,0:T(8,128)S(1)}, u32[]{:S(2)}, u32[]{:S(2)}) collective-permute-start(f32[4,32,256]{2,1,0:T(8,128)S(1)} %shard_map.86.refs_0_), channel_id=1, source_target_pairs={{0,8},{2,10},{4,12},{6,14},{8,0},{10,2},{12,4},{14,6},{16,24},{18,... | collective-permute-start | bytes 393224 | tf_op jit(solution)/shard_map/ppermute | solution.py:682
  84.7 2.1 %collective-permute-start.19 = (f32[4,32,256]{2,1,0:T(8,128)S(1)}, f32[4,32,256]{2,1,0:T(8,128)S(1)}, u32[]{:S(2)}, u32[]{:S(2)}) collective-permute-start(f32[4,32,256]{2,1,0:T(8,128)S(1)} %shard_map.86.refs_0_), channel_id=1, source_target_pairs={{0,12},{2,14},{4,8},{6,10},{8,4},{10,6},{12,0},{14,2},{16,28},{18,... | collective-permute-start | bytes 393224 | tf_op jit(solution)/shard_map/ppermute | solution.py:682
  86.9 0.1 shard_map.80
  87.0 0.8 collective-permute-start.9
  87.9 0.5 collective-permute-done.17.refs_1_
  88.3 1.5 %collective-permute-done.18.refs_2_ = f32[4,32,256]{2,1,0:T(8,128)S(1)} collective-permute-done((f32[4,32,256]{2,1,0:T(8,128)S(1)}, f32[4,32,256]{2,1,0:T(8,128)S(1)}, u32[]{:S(2)}, u32[]{:S(2)}) %collective-permute-start.18) | collective-permute-done | bytes 131104 | tf_op jit(solution)/shard_map/ppermute | solution.py:682
  89.8 1.4 %collective-permute-done.19.refs_3_ = f32[4,32,256]{2,1,0:T(8,128)S(1)} collective-permute-done((f32[4,32,256]{2,1,0:T(8,128)S(1)}, f32[4,32,256]{2,1,0:T(8,128)S(1)}, u32[]{:S(2)}, u32[]{:S(2)}) %collective-permute-start.19) | collective-permute-done | bytes 131104 | tf_op jit(solution)/shard_map/ppermute | solution.py:682
  91.3 1.1 collective-permute-start.4
  92.4 0.6 collective-permute-start.5
  93.1 12.7 %collective-permute-done.4 = s32[3,6]{1,0:T(4,128)S(1)} collective-permute-done((s32[3,6]{1,0:T(4,128)S(1)}, s32[3,6]{1,0:T(4,128)S(1)}, u32[]{:S(2)}, u32[]{:S(2)}) %collective-permute-start.4) | collective-permute-done | bytes 104 | tf_op jit(solution)/shard_map/ppermute | solution.py:596
  105.9 1.1 %collective-permute-done.6.refs_1_ = s32[3,3,6]{2,1,0:T(4,128)S(1)} collective-permute-done((s32[3,3,6]{2,1,0:T(4,128)S(1)}, s32[3,3,6]{2,1,0:T(4,128)S(1)}, u32[]{:S(2)}, u32[]{:S(2)}) %collective-permute-start.6) | collective-permute-done | bytes 248 | tf_op jit(solution)/shard_map/ppermute | solution.py:585
  107.0 1.6 %shard_map.79.light = f32[4,512,128]{2,1,0:T(8,128)S(1)} custom-call(s32[3,6]{1,0:T(4,128)S(1)} %get-tuple-element.51.own, s32[2,3,6]{2,1,0:T(4,128)S(1)} %pad_add_fusion.1.refs_0_, s32[3,3,6]{2,1,0:T(4,128)S(1)} %collective-permute-done.6.refs_1_, f32[2,2,256,256]{3,2,1,0:T(8,128)S(1)} %copy-done.1), custom_call_target="tpu_custom_call" | custom-call | flops 10000000 | bytes 1000000 | tf_op jit(solution)/shard_map/pallas_call | solution.py:688
  108.6 2.0 %shard_map.81 = f32[2,512,512]{2,1,0:T(8,128)} custom-call(f32[2,512,512]{2,1,0:T(8,128)S(1)} %copy-done, f32[4,2,512,128]{3,2,1,0:T(8,128)S(1)} %get-tuple-element.36.mid, f32[4,512,128]{2,1,0:T(8,128)S(1)} %shard_map.79.light, f32[4,2,128,128]{3,2,1,0:T(8,128)S(1)} %collective-permute-done.8.from_straight, ...), custom_call_target="tpu_custom_call" | custom-call | tf_op jit(solution)/shard_map/pallas_call | solution.py:696
  110.6 1.0 shard_map.88
  (33 shorter events, 0.8 us)
Async XLA Ops:
  0.6 27.0 %copy-start.2 = (s32[1,1,2,6]{3,2,1,0:T(2,128)S(1)}, s32[1,1,2,6]{3,2,1,0:T(2,128)}, u32[]{:S(2)}) copy-start(s32[1,1,2,6]{3,2,1,0:T(2,128)} %offsets.3) | copy-start | bytes 148
  2.1 25.4 %collective-permute-start = (f32[2,128,512]{2,1,0:T(8,128)S(1)}, f32[2,128,512]{2,1,0:T(8,128)S(1)}, u32[]{:S(2)}, u32[]{:S(2)}) collective-permute-start(f32[2,128,512]{2,1,0:T(8,128)S(1)} %get-tuple-element.26), channel_id=1, source_target_pairs={{0,2},{2,0},{4,6},{6,4},{8,10},{10,8},{12,14},{14,12},{16,18},{18,... | collective-permute-start | bytes 1572872 | tf_op jit(solution)/shard_map/ppermute | solution.py:596
  5.1 22.4 %collective-permute-start.1 = (f32[2,128,512]{2,1,0:T(8,128)S(1)}, f32[2,128,512]{2,1,0:T(8,128)S(1)}, u32[]{:S(2)}, u32[]{:S(2)}) collective-permute-start(f32[2,128,512]{2,1,0:T(8,128)S(1)} %get-tuple-element.27), channel_id=1, source_target_pairs={{2,4},{4,2},{6,8},{8,6},{10,12},{12,10},{14,16},{16,14},{18,20},{2... | collective-permute-start | bytes 1572872 | tf_op jit(solution)/shard_map/ppermute | solution.py:596
  5.8 21.9 %collective-permute-start.3 = (f32[2,512,128]{2,1,0:T(8,128)S(1)}, f32[2,512,128]{2,1,0:T(8,128)S(1)}, u32[]{:S(2)}, u32[]{:S(2)}) collective-permute-start(f32[2,512,128]{2,1,0:T(8,128)S(1)} %get-tuple-element.28), channel_id=1, source_target_pairs={{0,1},{1,0},{2,3},{3,2},{4,5},{5,4},{6,7},{7,6},{8,9},{9,8},{10,11... | collective-permute-start | bytes 1572872 | tf_op jit(solution)/shard_map/ppermute | solution.py:585
  27.5 7.1 %collective-permute-start.2 = (f32[2,2,128,128]{3,2,1,0:T(8,128)S(1)}, f32[2,2,128,128]{3,2,1,0:T(8,128)S(1)}, u32[]{:S(2)}, u32[]{:S(2)}) collective-permute-start(f32[2,2,128,128]{3,2,1,0:T(8,128)S(1)} %shard_map.78), channel_id=1, source_target_pairs={{0,1},{1,0},{2,3},{3,2},{4,5},{5,4},{6,7},{7,6},{8,9},{9,8},{10,11... | collective-permute-start | bytes 786440 | tf_op jit(solution)/shard_map/ppermute | solution.py:585
  36.2 41.3 %copy-start.1 = (f32[2,2,256,256]{3,2,1,0:T(8,128)S(1)}, f32[2,2,256,256]{3,2,1,0:T(8,128)}, u32[]{:S(2)}) copy-start(f32[2,2,256,256]{3,2,1,0:T(8,128)} %refs_2_.1) | copy-start | bytes 3145732
  36.2 2.3 %collective-permute-start.10 = (f32[5,128,256]{2,1,0:T(8,128)S(1)}, f32[5,128,256]{2,1,0:T(8,128)S(1)}, u32[]{:S(2)}, u32[]{:S(2)}) collective-permute-start(f32[5,128,256]{2,1,0:T(8,128)S(1)} %get-tuple-element.43), channel_id=1, source_target_pairs={{0,1},{1,0},{2,3},{3,2},{4,5},{5,4},{6,7},{7,6},{8,9},{9,8},{10,11... | collective-permute-start | bytes 1966088 | tf_op jit(solution)/shard_map/ppermute | solution.py:663
  36.7 50.1 %collective-permute-start.7 = (f32[2,768,128]{2,1,0:T(8,128)S(1)}, f32[2,768,128]{2,1,0:T(8,128)S(1)}, u32[]{:S(2)}, u32[]{:S(2)}) collective-permute-start(f32[2,768,128]{2,1,0:T(8,128)S(1)} %get-tuple-element.39), channel_id=1, source_target_pairs={{0,1},{1,0},{2,3},{3,2},{4,5},{5,4},{6,7},{7,6},{8,9},{9,8},{10,11... | collective-permute-start | bytes 2359304 | tf_op jit(solution)/shard_map/ppermute | solution.py:585
  38.5 19.7 %collective-permute-start.11 = (f32[5,32,256]{2,1,0:T(8,128)S(1)}, f32[5,32,256]{2,1,0:T(8,128)S(1)}, u32[]{:S(2)}, u32[]{:S(2)}) collective-permute-start(f32[5,32,256]{2,1,0:T(8,128)S(1)} %get-tuple-element.45), channel_id=1, source_target_pairs={{0,4},{2,6},{4,0},{6,2},{8,12},{10,14},{12,8},{14,10},{16,20},{18,... | collective-permute-start | bytes 491528 | tf_op jit(solution)/shard_map/ppermute | solution.py:663
  53.1 10.2 %collective-permute-start.12 = (f32[5,32,256]{2,1,0:T(8,128)S(1)}, f32[5,32,256]{2,1,0:T(8,128)S(1)}, u32[]{:S(2)}, u32[]{:S(2)}) collective-permute-start(f32[5,32,256]{2,1,0:T(8,128)S(1)} %get-tuple-element.46), channel_id=1, source_target_pairs={{0,8},{2,10},{4,12},{6,14},{8,0},{10,2},{12,4},{14,6},{16,24},{18,... | collective-permute-start | bytes 491528 | tf_op jit(solution)/shard_map/ppermute | solution.py:663
  58.2 7.8 %collective-permute-start.13 = (f32[5,32,256]{2,1,0:T(8,128)S(1)}, f32[5,32,256]{2,1,0:T(8,128)S(1)}, u32[]{:S(2)}, u32[]{:S(2)}) collective-permute-start(f32[5,32,256]{2,1,0:T(8,128)S(1)} %get-tuple-element.47), channel_id=1, source_target_pairs={{0,12},{2,14},{4,8},{6,10},{8,4},{10,6},{12,0},{14,2},{16,28},{18,... | collective-permute-start | bytes 491528 | tf_op jit(solution)/shard_map/ppermute | solution.py:663
  66.0 6.9 %collective-permute-start.14 = (f32[5,16,256]{2,1,0:T(8,128)S(1)}, f32[5,16,256]{2,1,0:T(8,128)S(1)}, u32[]{:S(2)}, u32[]{:S(2)}) collective-permute-start(f32[5,16,256]{2,1,0:T(8,128)S(1)} %get-tuple-element.49), channel_id=1, source_target_pairs={{0,16},{2,18},{4,20},{6,22},{8,24},{10,26},{12,28},{14,30},{16,0},... | collective-permute-start | bytes 245768 | tf_op jit(solution)/shard_map/ppermute | solution.py:663
  72.9 4.5 %collective-permute-start.15 = (f32[5,16,256]{2,1,0:T(8,128)S(1)}, f32[5,16,256]{2,1,0:T(8,128)S(1)}, u32[]{:S(2)}, u32[]{:S(2)}) collective-permute-start(f32[5,16,256]{2,1,0:T(8,128)S(1)} %shard_map.84.refs_0_), channel_id=1, source_target_pairs={{0,2},{2,0},{4,6},{6,4},{8,10},{10,8},{12,14},{14,12},{16,18},{18,... | collective-permute-start | bytes 245768 | tf_op jit(solution)/shard_map/ppermute | solution.py:667
  77.5 5.8 %collective-permute-start.16 = (f32[4,16,256]{2,1,0:T(8,128)S(1)}, f32[4,16,256]{2,1,0:T(8,128)S(1)}, u32[]{:S(2)}, u32[]{:S(2)}) collective-permute-start(f32[4,16,256]{2,1,0:T(8,128)S(1)} %shard_map.85.refs_0_), channel_id=1, source_target_pairs={{0,16},{2,18},{4,20},{6,22},{8,24},{10,26},{12,28},{14,30},{16,0},... | collective-permute-start | bytes 196616 | tf_op jit(solution)/shard_map/ppermute | solution.py:682
  83.3 5.0 %collective-permute-start.17 = (f32[4,32,256]{2,1,0:T(8,128)S(1)}, f32[4,32,256]{2,1,0:T(8,128)S(1)}, u32[]{:S(2)}, u32[]{:S(2)}) collective-permute-start(f32[4,32,256]{2,1,0:T(8,128)S(1)} %shard_map.86.refs_0_), channel_id=1, source_target_pairs={{0,4},{2,6},{4,0},{6,2},{8,12},{10,14},{12,8},{14,10},{16,20},{18,... | collective-permute-start | bytes 393224 | tf_op jit(solution)/shard_map/ppermute | solution.py:682
  83.4 6.4 %collective-permute-start.18 = (f32[4,32,256]{2,1,0:T(8,128)S(1)}, f32[4,32,256]{2,1,0:T(8,128)S(1)}, u32[]{:S(2)}, u32[]{:S(2)}) collective-permute-start(f32[4,32,256]{2,1,0:T(8,128)S(1)} %shard_map.86.refs_0_), channel_id=1, source_target_pairs={{0,8},{2,10},{4,12},{6,14},{8,0},{10,2},{12,4},{14,6},{16,24},{18,... | collective-permute-start | bytes 393224 | tf_op jit(solution)/shard_map/ppermute | solution.py:682
  84.7 6.5 %collective-permute-start.19 = (f32[4,32,256]{2,1,0:T(8,128)S(1)}, f32[4,32,256]{2,1,0:T(8,128)S(1)}, u32[]{:S(2)}, u32[]{:S(2)}) collective-permute-start(f32[4,32,256]{2,1,0:T(8,128)S(1)} %shard_map.86.refs_0_), channel_id=1, source_target_pairs={{0,12},{2,14},{4,8},{6,10},{8,4},{10,6},{12,0},{14,2},{16,28},{18,... | collective-permute-start | bytes 393224 | tf_op jit(solution)/shard_map/ppermute | solution.py:682
  86.9 21.8 %copy-start = (f32[2,512,512]{2,1,0:T(8,128)S(1)}, f32[2,512,512]{2,1,0:T(8,128)}, u32[]{:S(2)}) copy-start(f32[2,512,512]{2,1,0:T(8,128)} %tile.5) | copy-start | bytes 6291460
  87.0 21.6 %collective-permute-start.8 = (f32[4,2,128,128]{3,2,1,0:T(8,128)S(1)}, f32[4,2,128,128]{3,2,1,0:T(8,128)S(1)}, u32[]{:S(2)}, u32[]{:S(2)}) collective-permute-start(f32[4,2,128,128]{3,2,1,0:T(8,128)S(1)} %get-tuple-element.40), channel_id=1, source_target_pairs={{0,2},{2,0},{4,6},{6,4},{8,10},{10,8},{12,14},{14,12},{16,18},{18,... | collective-permute-start | bytes 1572872 | tf_op jit(solution)/shard_map/ppermute | solution.py:596
  87.0 21.6 %collective-permute-start.9 = (f32[4,2,128,128]{3,2,1,0:T(8,128)S(1)}, f32[4,2,128,128]{3,2,1,0:T(8,128)S(1)}, u32[]{:S(2)}, u32[]{:S(2)}) collective-permute-start(f32[4,2,128,128]{3,2,1,0:T(8,128)S(1)} %get-tuple-element.41), channel_id=1, source_target_pairs={{2,4},{4,2},{6,8},{8,6},{10,12},{12,10},{14,16},{16,14},{18,20},{2... | collective-permute-start | bytes 1572872 | tf_op jit(solution)/shard_map/ppermute | solution.py:596
  91.3 19.4 %collective-permute-start.20 = (f32[4,128,256]{2,1,0:T(8,128)S(1)}, f32[4,128,256]{2,1,0:T(8,128)S(1)}, u32[]{:S(2)}, u32[]{:S(2)}) collective-permute-start(f32[4,128,256]{2,1,0:T(8,128)S(1)} %shard_map.87.refs_0_), channel_id=1, source_target_pairs={{0,1},{1,0},{2,3},{3,2},{4,5},{5,4},{6,7},{7,6},{8,9},{9,8},{10,11... | collective-permute-start | bytes 1572872 | tf_op jit(solution)/shard_map/ppermute | solution.py:682
  91.3 14.4 %collective-permute-start.4 = (s32[3,6]{1,0:T(4,128)S(1)}, s32[3,6]{1,0:T(4,128)S(1)}, u32[]{:S(2)}, u32[]{:S(2)}) collective-permute-start(s32[3,6]{1,0:T(4,128)S(1)} %get-tuple-element.51.own), channel_id=1, source_target_pairs={{0,2},{2,0},{4,6},{6,4},{8,10},{10,8},{12,14},{14,12},{16,18},{18,... | collective-permute-start | bytes 224 | tf_op jit(solution)/shard_map/ppermute | solution.py:596
  92.4 13.3 %collective-permute-start.5 = (s32[3,6]{1,0:T(4,128)S(1)}, s32[3,6]{1,0:T(4,128)S(1)}, u32[]{:S(2)}, u32[]{:S(2)}) collective-permute-start(s32[3,6]{1,0:T(4,128)S(1)} %get-tuple-element.51.own), channel_id=1, source_target_pairs={{2,4},{4,2},{6,8},{8,6},{10,12},{12,10},{14,16},{16,14},{18,20},{2... | collective-permute-start | bytes 224 | tf_op jit(solution)/shard_map/ppermute | solution.py:596
  105.8 1.2 %collective-permute-start.6 = (s32[3,3,6]{2,1,0:T(4,128)S(1)}, s32[3,3,6]{2,1,0:T(4,128)S(1)}, u32[]{:S(2)}, u32[]{:S(2)}) collective-permute-start(s32[3,3,6]{2,1,0:T(4,128)S(1)} %pad_add_fusion), channel_id=1, source_target_pairs={{0,1},{1,0},{2,3},{3,2},{4,5},{5,4},{6,7},{7,6},{8,9},{9,8},{10,11... | collective-permute-start | bytes 656 | tf_op jit(solution)/shard_map/ppermute | solution.py:585

commit v6 on v5

--- a/solution.py
+++ b/solution.py
@@ -134,14 +134,11 @@
     )
 
 
-def pack_kernel(geometry, tile, straight, diagonal, *refs):
-    sides, sems = refs[:-1], refs[-1]
+def pack_kernel(geometry, first, tile, *refs):
+    outs, sems = refs[:-1], refs[-1]
     frame = Frame(*geometry)
-    pairs = [
-        (tile.at[:, frame.strip_rows(0), :], straight),
-        (tile.at[:, frame.strip_rows(1), :], diagonal),
-    ]
-    for number, side in enumerate(sides):
+    pairs = [(tile.at[:, frame.strip_rows(0 if first else 1), :], outs[0])]
+    for number, side in enumerate(outs[1:]):
         pairs.append((tile.at[:, :, frame.side_cols(number)], side))
     for copy in copy_all(pairs, sems):
         copy.wait()
@@ -161,7 +158,7 @@
     acc[last, channel, rows, :] += jnp.where(keep, zero, second)
 
 
-def slot_body(slot, row, col, ext, acc, sums, probe, amps, rights, lefts):
+def slot_stages(slot, row, col, ext, acc, sums, probe, amps, rights, lefts):
     edge = probe.shape[-1]
     modes = probe.shape[1]
     half = edge // 2
@@ -181,19 +178,29 @@
     def probe_at(c, k, t):
         return probe[c, k, :, pl.ds(t * LANES, LANES)]
 
-    evens, odds = [], []
+    def both_modes(parts):
+        return jnp.concatenate(parts, axis=0)
+
+    yield
+    plus, minus = [], []
     for k in range(modes):
         re = [probe_at(0, k, t) * patch[0][t] - probe_at(1, k, t) * patch[1][t] for t in range(2)]
         im = [probe_at(0, k, t) * patch[1][t] + probe_at(1, k, t) * patch[0][t] for t in range(2)]
-        evens.append(right_dot(jnp.concatenate([re[0] + re[1], im[0] + im[1]], axis=1), rights[0]))
-        odds.append(right_dot(jnp.concatenate([re[0] - re[1], im[0] - im[1]], axis=1), rights[1]))
+        plus.append(jnp.concatenate([re[0] + re[1], im[0] + im[1]], axis=1))
+        minus.append(jnp.concatenate([re[0] - re[1], im[0] - im[1]], axis=1))
+    even = right_dot(both_modes(plus), rights[0])
+    yield
+    odd = right_dot(both_modes(minus), rights[1])
+    yield
     far = []
     for k in range(modes):
-        re = jnp.concatenate([evens[k][:, :half], odds[k][:, :half]], axis=1)
-        im = jnp.concatenate([evens[k][:, half:], odds[k][:, half:]], axis=1)
+        rows = slice(k * edge, (k + 1) * edge)
+        re = jnp.concatenate([even[rows, :half], odd[rows, :half]], axis=1)
+        im = jnp.concatenate([even[rows, half:], odd[rows, half:]], axis=1)
         plus = jnp.concatenate([re[:half] + re[half:], im[:half] + im[half:]], axis=0)
         minus = jnp.concatenate([re[:half] - re[half:], im[:half] - im[half:]], axis=0)
         far.append([left_dot(lefts[0], plus), left_dot(lefts[1], minus)])
+        yield
     factor = []
     for p in range(2):
         total = sum(
@@ -201,20 +208,29 @@
             for k in range(modes)
         )
         amp = amps[slot, pl.ds(p * half, half), :].astype(F32)
-        one = amp / jnp.sqrt(jnp.maximum(total, 0.25)) - 1.0
+        one = amp * lax.rsqrt(jnp.maximum(total, 0.25)) - 1.0
         factor.append(jnp.concatenate([one, one], axis=0))
-    update = [[None, None], [None, None]]
+    yield
+    evens, odds = [], []
     for k in range(modes):
         even = left_dot(lefts[2], far[k][0] * factor[0])
         odd = left_dot(lefts[3], far[k][1] * factor[1])
         plus, minus = even + odd, even - odd
         re = jnp.concatenate([plus[:half], minus[:half]], axis=0)
         im = jnp.concatenate([plus[half:], minus[half:]], axis=0)
-        even = right_dot(jnp.concatenate([re[:, :half], im[:, :half]], axis=1), rights[2])
-        odd = right_dot(jnp.concatenate([re[:, half:], im[:, half:]], axis=1), rights[3])
-        plus, minus = even + odd, even - odd
-        back_re = [plus[:, :half], minus[:, :half]]
-        back_im = [plus[:, half:], minus[:, half:]]
+        evens.append(jnp.concatenate([re[:, :half], im[:, :half]], axis=1))
+        odds.append(jnp.concatenate([re[:, half:], im[:, half:]], axis=1))
+        yield
+    even = right_dot(both_modes(evens), rights[2])
+    yield
+    odd = right_dot(both_modes(odds), rights[3])
+    plus, minus = even + odd, even - odd
+    yield
+    update = [[None, None], [None, None]]
+    for k in range(modes):
+        rows = slice(k * edge, (k + 1) * edge)
+        back_re = [plus[rows, :half], minus[rows, :half]]
+        back_im = [plus[rows, half:], minus[rows, half:]]
         for t in range(2):
             pr, pi = probe_at(0, k, t), probe_at(1, k, t)
             u_re = pr * back_re[t] + pi * back_im[t]
@@ -225,11 +241,30 @@
             xr, xi = patch[0][t], patch[1][t]
             sums[k, :, lanes] += xr * back_re[t] + xi * back_im[t]
             sums[modes + k, :, lanes] += xr * back_im[t] - xi * back_re[t]
+        yield
     for t in range(2):
         lanes = pl.ds(t * LANES, LANES)
-        sums[2 * modes, :, lanes] += patch[0][t] * patch[0][t] + patch[1][t] * patch[1][t]
+        power = patch[0][t] * patch[0][t] + patch[1][t] * patch[1][t]
+        sums[2 * modes, :, lanes] += power
     for c in range(2):
         add_window(acc, c, update[c], row, block, shift)
+
+
+def run_stages(works, lag):
+    pending = [(number * lag, work) for number, work in enumerate(works)]
+    turn = 0
+    while pending:
+        kept = []
+        for start, work in pending:
+            if turn >= start and next(work, work) is work:
+                continue
+            kept.append((start, work))
+        pending = kept
+        turn += 1
+
+
+def slot_body(slot, row, col, *refs):
+    run_stages([slot_stages(slot, row, col, *refs)], 0)
 
 
 def interior_kernel(geometry, offsets, counts, tile, probe_in, amps_in, tables, *refs):
@@ -287,7 +322,7 @@
     probe, amps, rights, lefts = refs[:4]
     ext, acc, sums, mid, over_straight, over_diagonal = refs[7:13]
     side_outs, refs = refs[13 : 13 + sides], refs[13 + sides :]
-    keep, send, sems = refs
+    keep, send, todo, sems = refs
     tiles, margin, body = frame.tiles, frame.margin, frame.body
     edge = probe.shape[-1]
     pairs = []
@@ -303,16 +338,33 @@
     for copy in copy_all(pairs, sems):
         copy.wait()
 
-    def visit(slot, carry):
+    def note(slot, found):
+        row, _ = frame.place_of(offsets, slot)
+        chosen = jnp.logical_or(row < margin, row + edge > margin + frame.tile_rows)
+        todo[found] = slot
+        return found + chosen.astype(jnp.int32)
+
+    found = lax.fori_loop(0, counts[0, 0], note, jnp.int32(0))
+
+    shared = (ext, acc, sums, probe, amps, rights, lefts)
+
+    def visit(pair, carry):
+        works = []
+        for member in range(2):
+            slot = todo[2 * pair + member]
+            row, col = frame.place_of(offsets, slot)
+            works.append(slot_stages(slot, row, col, *shared))
+        run_stages(works, LAG)
+        return carry
+
+    lax.fori_loop(0, lax.div(found, 2), visit, 0)
+
+    @pl.when(lax.rem(found, 2) == 1)
+    def _():
+        slot = todo[found - 1]
         row, col = frame.place_of(offsets, slot)
-
-        @pl.when(jnp.logical_or(row < margin, row + edge > margin + frame.tile_rows))
-        def _():
-            slot_body(slot, row, col, ext, acc, sums, probe, amps, rights, lefts)
-
-        return carry
-
-    lax.fori_loop(0, counts[0, 0], visit, 0)
+        slot_body(slot, row, col, *shared)
+
     out = [(acc.at[1 + t, :, body, :], mid.at[t]) for t in range(tiles)]
     copies = copy_all(out, sems)
     rows = keep.shape[1]
@@ -335,7 +387,8 @@
         out[1] = diagonal[:, :, frame.side_cols(side)]
 
 
-KERNEL_VMEM = 12 * MIB
+KERNEL_VMEM = 20 * MIB
+LAG = 4
 SLOT_COST = dict(
     cost_estimate=pl.CostEstimate(flops=int(1e10), bytes_accessed=20_000_000, transcendentals=0),
 )
@@ -382,7 +435,7 @@
         out_shape=outs,
         in_specs=[IN_SMEM] * 2 + [ANYWHERE] * (2 + sides) + [IN_VMEM] * 7,
         out_specs=[IN_VMEM] * 3 + [IN_HBM] + [IN_VMEM] * (len(outs) - 4),
-        scratch_shapes=[pltpu.SemaphoreType.DMA((16,))],
+        scratch_shapes=[pltpu.SMEM((8,), jnp.int32), pltpu.SemaphoreType.DMA((16,))],
         input_output_aliases={base: 0, base + 1: 1, base + 2: 2},
         compiler_params=pltpu.CompilerParams(vmem_limit_bytes=KERNEL_VMEM),
         name="slots_boundary",
@@ -392,11 +445,13 @@
 
 def fold_kernel(geometry, over_straight, over_diagonal, *refs):
     frame = Frame(*geometry)
-    received, outs = refs[: frame.sides], refs[frame.sides : frame.sides + 2]
-    for number, (over, out) in enumerate(((over_straight, outs[0]), (over_diagonal, outs[1]))):
+    received, (straight, low, high, diagonal) = refs[: frame.sides], refs[frame.sides :]
+    for number, (over, out) in enumerate(((over_straight, straight), (over_diagonal, diagonal))):
         out[...] = over[...]
         for side, value in enumerate(received):
             out[frame.side_target(side) - 1] += value[:, frame.halo_rows(number), :]
+    low[...] = diagonal[pl.ds(0, low.shape[0])]
+    high[...] = diagonal[pl.ds(low.shape[0], low.shape[0])]
 
 
 def light_kernel(geometry, own, *refs):
@@ -441,7 +496,7 @@
         out[t] = canvas[edge // LANES + t, 0, pl.ds(edge, frame.tile_rows), :]
 
 
-def object_kernel(geometry, tile, mid, light, from_straight, from_diagonal, *refs):
+def object_kernel(geometry, tile, mid, light, from_straight, from_low, from_high, *refs):
     frame = Frame(*geometry)
     received, (out, old, stage, sems_in, sems_out) = refs[: frame.sides], refs[frame.sides :]
     tiles = frame.tiles
@@ -467,8 +522,9 @@
             def _(value=value, t=t):
                 stage[t] += value[:, frame.body, :]
 
-        for number, value in enumerate((from_straight, from_diagonal)):
-            stage[t, :, frame.strip_rows(number), :] += value[t]
+        stage[t, :, frame.strip_rows(0), :] += from_straight[t]
+        half = from_low.shape[0]
+        stage[t, :, frame.strip_rows(1), :] += from_low[t] if t < half else from_high[t - half]
         scale = 1.0 / (light[t] + 1.0)
         for c in range(2):
             stage[t, c] = old[t, c] + stage[t, c] * scale
@@ -619,15 +675,19 @@
     tables = in_hbm(jnp.asarray(dft_tables(edge)))
     tile_hbm, probe_hbm, amps_hbm = in_hbm(object_field), in_hbm(probe_modes), in_hbm(amplitudes)
 
-    straight, diagonal, *edges = small_call(
-        functools.partial(pack_kernel, geometry),
-        [shape(2, margin, tile_cols)] * 2 + [shape(2, tile_rows, margin)] * sides,
-        [IN_HBM],
-        limit=8 * MIB,
-        scratch=(pltpu.SemaphoreType.DMA((4,)),),
-    )(tile_hbm)
-    straight = swap_rows(straight, 0)
-    diagonal = swap_rows(diagonal, 1)
+    def pack(first, outs):
+        return small_call(
+            functools.partial(pack_kernel, geometry, first),
+            outs,
+            [IN_HBM],
+            limit=8 * MIB,
+            scratch=(pltpu.SemaphoreType.DMA((3,)),),
+        )(tile_hbm)
+
+    strip = shape(2, margin, tile_cols)
+    straight = swap_rows(pack(True, [strip])[0], 0)
+    packed, *edges = pack(False, [strip] + [shape(2, tile_rows, margin)] * sides)
+    diagonal = swap_rows(packed, 1)
     halos = swap_sides(edges)
 
     own = jnp.concatenate(
@@ -668,11 +728,16 @@
 
     received = swap_sides(side_outs)
     strip = shape(tiles, 2, margin, LANES)
-    out_straight, out_diagonal = small_call(
-        functools.partial(fold_kernel, geometry), [strip, strip], [IN_VMEM] * (2 + sides)
+    chunk = shape(tiles // 2, 2, margin, LANES)
+    out_straight, out_low, out_high = small_call(
+        functools.partial(fold_kernel, geometry),
+        [strip, chunk, chunk],
+        [IN_VMEM] * (2 + sides),
+        scratch=(VMEM(strip.shape, F32),),
     )(*overs, *received)
     from_straight = swap_rows(out_straight, 0)
-    from_diagonal = swap_rows(out_diagonal, 1)
+    from_low = swap_rows(out_low, 1)
+    from_high = swap_rows(out_high, 1)
 
     flat = probe_modes.reshape(2 * modes, edge, edge)
     shard = finish(stages, flat, parts)
@@ -696,7 +761,7 @@
     object_new = small_call(
         functools.partial(object_kernel, geometry),
         [shape(2, tile_rows, tile_cols)],
-        [IN_HBM, ANYWHERE] + [IN_VMEM] * (3 + sides),
+        [IN_HBM, ANYWHERE] + [IN_VMEM] * (4 + sides),
         limit=8 * MIB,
         scratch=(
             VMEM((tiles, 2, tile_rows, LANES), F32),
@@ -705,7 +770,7 @@
             pltpu.SemaphoreType.DMA((tiles,)),
         ),
         out_specs=[IN_HBM],
-    )(object_field, mid, light, from_straight, from_diagonal, *received)[0]
+    )(object_field, mid, light, from_straight, from_low, from_high, *received)[0]
     return object_new, probe_new
 
 

time: 112 us -> 121 us (1.080)
  the two profiles are of different devices: /device:TPU:0 before, /device:TPU:9 now
where the time goes in v6:
time: 121 us
  waiting for transfers between devices  56.3 us (47%)
  starting transfers between devices  43.7 us (36%)
  Pallas kernels  19.5 us (16%)
  between operations  1.52 us (1%)
    ppermute x7, waiting for transfers between devices, swap_rows(): return lax.ppermute(value, 'row', pairs)  33.5 us
    ppermute x7, starting transfers between devices, swap_rows(): return lax.ppermute(value, 'row', pairs)  14.3 us
    ppermute x5, waiting for transfers between devices, step(): lax.ppermute(piece, axis, member_perm(axis, bits, member + 1))  13.5 us
    ppermute x5, starting transfers between devices, step(): lax.ppermute(piece, axis, member_perm(axis, bits, member + 1))  13.5 us
    ppermute x5, starting transfers between devices, step(): lax.ppermute(shard, axis, member_perm(axis, bits, member))  11.5 us
    pallas_call x1, Pallas kernels, run_interior(): pl.pallas_call(functools.partial(interior_kernel, geometry), out_shape=ou...  6.93 us
    ppermute x5, waiting for transfers between devices, step(): lax.ppermute(shard, axis, member_perm(axis, bits, member))  5.19 us
    pallas_call x1, Pallas kernels, run_boundary(): pl.pallas_call(functools.partial(boundary_kernel, geometry), out_shape=ou...  4.66 us
  transfers between devices with their start and end apart: 22, of which 15 were waited for; matrix products, arithmetic and copies ran while one was open for 0% of the time, Pallas kernels for 10%

profile of v6, /device:TPU:9, one launch (start us, length us, event | category | flops | bytes accessed | tf_op | source)
XLA Modules:
  0.0 121.0 jit_solution(1115426298190693192)
XLA Ops:
  0.6 1.2 %shard_map.78 = (f32[2,128,512]{2,1,0:T(8,128)S(1)}, f32[2,512,128]{2,1,0:T(8,128)S(1)}) custom-call(f32[2,512,512]{2,1,0:T(8,128)} %tile.7), custom_call_target="tpu_custom_call" | custom-call | tf_op jit(solution)/shard_map/pallas_call | solution.py:679
  1.9 4.0 %collective-permute-start.1 = (f32[2,128,512]{2,1,0:T(8,128)S(1)}, f32[2,128,512]{2,1,0:T(8,128)S(1)}, u32[]{:S(2)}, u32[]{:S(2)}) collective-permute-start(f32[2,128,512]{2,1,0:T(8,128)S(1)} %get-tuple-element.26), channel_id=1, source_target_pairs={{2,4},{4,2},{6,8},{8,6},{10,12},{12,10},{14,16},{16,14},{18,20},{2... | collective-permute-start | bytes 1572872 | tf_op jit(solution)/shard_map/ppermute | solution.py:652
  5.9 1.1 shard_map.77
  7.4 1.2 %collective-permute-start.3 = (f32[2,512,128]{2,1,0:T(8,128)S(1)}, f32[2,512,128]{2,1,0:T(8,128)S(1)}, u32[]{:S(2)}, u32[]{:S(2)}) collective-permute-start(f32[2,512,128]{2,1,0:T(8,128)S(1)} %get-tuple-element.27), channel_id=1, source_target_pairs={{0,1},{1,0},{2,3},{3,2},{4,5},{5,4},{6,7},{7,6},{8,9},{9,8},{10,11... | collective-permute-start | bytes 1572872 | tf_op jit(solution)/shard_map/ppermute | solution.py:641
  9.3 9.2 %collective-permute-done.1.diagonal = f32[2,128,512]{2,1,0:T(8,128)S(1)} collective-permute-done((f32[2,128,512]{2,1,0:T(8,128)S(1)}, f32[2,128,512]{2,1,0:T(8,128)S(1)}, u32[]{:S(2)}, u32[]{:S(2)}) %collective-permute-start.1) | collective-permute-done | bytes 524320 | tf_op jit(solution)/shard_map/ppermute | solution.py:652
  18.4 11.3 %collective-permute-done.straight = f32[2,128,512]{2,1,0:T(8,128)S(1)} collective-permute-done((f32[2,128,512]{2,1,0:T(8,128)S(1)}, f32[2,128,512]{2,1,0:T(8,128)S(1)}, u32[]{:S(2)}, u32[]{:S(2)}) %collective-permute-start) | collective-permute-done | bytes 524320 | tf_op jit(solution)/shard_map/ppermute | solution.py:652
  30.4 6.9 %slots_interior.1 = (f32[6,2,768,128]{3,2,1,0:T(8,128)S(1)}, f32[6,2,768,128]{3,2,1,0:T(8,128)S(1)}, f32[5,256,256]{2,1,0:T(8,128)S(1)}, f32[2,2,256,256]{3,2,1,...) custom-call(s32[1,1,2,6]{3,2,1,0:T(2,128)S(1)} %copy-done.2, ...), custom_call_target="tpu_custom_call" | custom-call | flops 10000000000 | bytes 20000000 | tf_op jit(solution)/shard_map/slots_interior/pallas_call | solution.py:408
  37.4 4.7 %slots_boundary.1 = (f32[6,2,768,128]{3,2,1,0:T(8,128)S(1)}, f32[6,2,768,128]{3,2,1,0:T(8,128)S(1)}, f32[5,256,256]{2,1,0:T(8,128)S(1)}, f32[4,2,512,128]{3,2,1,...) custom-call(s32[1,1,2,6]{3,2,1,0:T(2,128)S(1)} %copy-done.2, ...), custom_call_target="tpu_custom_call", output_to_operand_aliasing={{0}: (9, {}), {1}: (10, {}), {2}: (11, {})} | custom-call | flops 10000000000 | bytes 20000000 | tf_op jit(solution)/shard_map/slots_boundary/pallas_call | solution.py:433
  42.6 1.6 %collective-permute-done.11.refs_1_ = f32[5,128,256]{2,1,0:T(8,128)S(1)} collective-permute-done((f32[5,128,256]{2,1,0:T(8,128)S(1)}, f32[5,128,256]{2,1,0:T(8,128)S(1)}, u32[]{:S(2)}, u32[]{:S(2)}) %collective-permute-start.11) | collective-permute-done | bytes 655392 | tf_op jit(solution)/shard_map/ppermute | solution.py:723
  44.3 12.1 %collective-permute-start.12 = (f32[5,32,256]{2,1,0:T(8,128)S(1)}, f32[5,32,256]{2,1,0:T(8,128)S(1)}, u32[]{:S(2)}, u32[]{:S(2)}) collective-permute-start(f32[5,32,256]{2,1,0:T(8,128)S(1)} %get-tuple-element.45), channel_id=1, source_target_pairs={{0,4},{2,6},{4,0},{6,2},{8,12},{10,14},{12,8},{14,10},{16,20},{18,... | collective-permute-start | bytes 491528 | tf_op jit(solution)/shard_map/ppermute | solution.py:723
  56.4 1.3 %collective-permute-start.14 = (f32[5,32,256]{2,1,0:T(8,128)S(1)}, f32[5,32,256]{2,1,0:T(8,128)S(1)}, u32[]{:S(2)}, u32[]{:S(2)}) collective-permute-start(f32[5,32,256]{2,1,0:T(8,128)S(1)} %get-tuple-element.47), channel_id=1, source_target_pairs={{0,12},{2,14},{4,8},{6,10},{8,4},{10,6},{12,0},{14,2},{16,28},{18,... | collective-permute-start | bytes 491528 | tf_op jit(solution)/shard_map/ppermute | solution.py:723
  57.6 3.2 %collective-permute-done.12.refs_1_ = f32[5,32,256]{2,1,0:T(8,128)S(1)} collective-permute-done((f32[5,32,256]{2,1,0:T(8,128)S(1)}, f32[5,32,256]{2,1,0:T(8,128)S(1)}, u32[]{:S(2)}, u32[]{:S(2)}) %collective-permute-start.12) | collective-permute-done | bytes 163872 | tf_op jit(solution)/shard_map/ppermute | solution.py:723
  61.7 3.6 %collective-permute-done.14.refs_3_ = f32[5,32,256]{2,1,0:T(8,128)S(1)} collective-permute-done((f32[5,32,256]{2,1,0:T(8,128)S(1)}, f32[5,32,256]{2,1,0:T(8,128)S(1)}, u32[]{:S(2)}, u32[]{:S(2)}) %collective-permute-start.14) | collective-permute-done | bytes 163872 | tf_op jit(solution)/shard_map/ppermute | solution.py:723
  65.4 4.2 %collective-permute-done.15.refs_1_ = f32[5,16,256]{2,1,0:T(8,128)S(1)} collective-permute-done((f32[5,16,256]{2,1,0:T(8,128)S(1)}, f32[5,16,256]{2,1,0:T(8,128)S(1)}, u32[]{:S(2)}, u32[]{:S(2)}) %collective-permute-start.15) | collective-permute-done | bytes 81952 | tf_op jit(solution)/shard_map/ppermute | solution.py:723
  69.7 3.3 %collective-permute-done.16.refs_1_ = f32[5,16,256]{2,1,0:T(8,128)S(1)} collective-permute-done((f32[5,16,256]{2,1,0:T(8,128)S(1)}, f32[5,16,256]{2,1,0:T(8,128)S(1)}, u32[]{:S(2)}, u32[]{:S(2)}) %collective-permute-start.16) | collective-permute-done | bytes 81952 | tf_op jit(solution)/shard_map/ppermute | solution.py:727
  73.0 2.6 %collective-permute-start.17 = (f32[4,16,256]{2,1,0:T(8,128)S(1)}, f32[4,16,256]{2,1,0:T(8,128)S(1)}, u32[]{:S(2)}, u32[]{:S(2)}) collective-permute-start(f32[4,16,256]{2,1,0:T(8,128)S(1)} %shard_map.86.refs_0_), channel_id=1, source_target_pairs={{0,16},{2,18},{4,20},{6,22},{8,24},{10,26},{12,28},{14,30},{16,0},... | collective-permute-start | bytes 196616 | tf_op jit(solution)/shard_map/ppermute | solution.py:747
  75.6 1.7 %collective-permute-done.17.refs_1_ = f32[4,16,256]{2,1,0:T(8,128)S(1)} collective-permute-done((f32[4,16,256]{2,1,0:T(8,128)S(1)}, f32[4,16,256]{2,1,0:T(8,128)S(1)}, u32[]{:S(2)}, u32[]{:S(2)}) %collective-permute-start.17) | collective-permute-done | bytes 65568 | tf_op jit(solution)/shard_map/ppermute | solution.py:747
  77.3 1.1 collective-permute-start.18
  78.5 1.5 %collective-permute-start.20 = (f32[4,32,256]{2,1,0:T(8,128)S(1)}, f32[4,32,256]{2,1,0:T(8,128)S(1)}, u32[]{:S(2)}, u32[]{:S(2)}) collective-permute-start(f32[4,32,256]{2,1,0:T(8,128)S(1)} %shard_map.87.refs_0_), channel_id=1, source_target_pairs={{0,12},{2,14},{4,8},{6,10},{8,4},{10,6},{12,0},{14,2},{16,28},{18,... | collective-permute-start | bytes 393224 | tf_op jit(solution)/shard_map/ppermute | solution.py:747
  80.2 1.0 collective-permute-done.18.refs_1_
  81.2 1.0 collective-permute-done.19.refs_2_
  82.2 1.6 %collective-permute-done.20.refs_3_ = f32[4,32,256]{2,1,0:T(8,128)S(1)} collective-permute-done((f32[4,32,256]{2,1,0:T(8,128)S(1)}, f32[4,32,256]{2,1,0:T(8,128)S(1)}, u32[]{:S(2)}, u32[]{:S(2)}) %collective-permute-start.20) | collective-permute-done | bytes 131104 | tf_op jit(solution)/shard_map/ppermute | solution.py:747
  83.8 6.2 %collective-permute-start.21 = (f32[4,128,256]{2,1,0:T(8,128)S(1)}, f32[4,128,256]{2,1,0:T(8,128)S(1)}, u32[]{:S(2)}, u32[]{:S(2)}) collective-permute-start(f32[4,128,256]{2,1,0:T(8,128)S(1)} %shard_map.88.refs_0_), channel_id=1, source_target_pairs={{0,1},{1,0},{2,3},{3,2},{4,5},{5,4},{6,7},{7,6},{8,9},{9,8},{10,11... | collective-permute-start | bytes 1572872 | tf_op jit(solution)/shard_map/ppermute | solution.py:747
  90.0 2.7 %collective-permute-start.10 = (f32[2,2,128,128]{3,2,1,0:T(8,128)S(1)}, f32[2,2,128,128]{3,2,1,0:T(8,128)S(1)}, u32[]{:S(2)}, u32[]{:S(2)}) collective-permute-start(f32[2,2,128,128]{3,2,1,0:T(8,128)S(1)} %get-tuple-element.41), channel_id=1, source_target_pairs={{2,4},{4,2},{6,8},{8,6},{10,12},{12,10},{14,16},{16,14},{18,20},{2... | collective-permute-start | bytes 786440 | tf_op jit(solution)/shard_map/ppermute | solution.py:652
  92.7 4.4 %collective-permute-start.9 = (f32[2,2,128,128]{3,2,1,0:T(8,128)S(1)}, f32[2,2,128,128]{3,2,1,0:T(8,128)S(1)}, u32[]{:S(2)}, u32[]{:S(2)}) collective-permute-start(f32[2,2,128,128]{3,2,1,0:T(8,128)S(1)} %get-tuple-element.40), channel_id=1, source_target_pairs={{2,4},{4,2},{6,8},{8,6},{10,12},{12,10},{14,16},{16,14},{18,20},{2... | collective-permute-start | bytes 786440 | tf_op jit(solution)/shard_map/ppermute | solution.py:652
  97.2 9.6 %collective-permute-done.4 = s32[3,6]{1,0:T(4,128)S(1)} collective-permute-done((s32[3,6]{1,0:T(4,128)S(1)}, s32[3,6]{1,0:T(4,128)S(1)}, u32[]{:S(2)}, u32[]{:S(2)}) %collective-permute-start.4) | collective-permute-done | bytes 104 | tf_op jit(solution)/shard_map/ppermute | solution.py:652
  106.8 2.7 %collective-permute-start.5 = (s32[3,6]{1,0:T(4,128)S(1)}, s32[3,6]{1,0:T(4,128)S(1)}, u32[]{:S(2)}, u32[]{:S(2)}) collective-permute-start(s32[3,6]{1,0:T(4,128)S(1)} %get-tuple-element.51.own), channel_id=1, source_target_pairs={{2,4},{4,2},{6,8},{8,6},{10,12},{12,10},{14,16},{16,14},{18,20},{2... | collective-permute-start | bytes 224 | tf_op jit(solution)/shard_map/ppermute | solution.py:652
  109.5 3.4 %collective-permute-done.5 = s32[3,6]{1,0:T(4,128)S(1)} collective-permute-done((s32[3,6]{1,0:T(4,128)S(1)}, s32[3,6]{1,0:T(4,128)S(1)}, u32[]{:S(2)}, u32[]{:S(2)}) %collective-permute-start.5) | collective-permute-done | bytes 104 | tf_op jit(solution)/shard_map/ppermute | solution.py:652
  112.9 2.0 %collective-permute-start.6 = (s32[3,3,6]{2,1,0:T(4,128)S(1)}, s32[3,3,6]{2,1,0:T(4,128)S(1)}, u32[]{:S(2)}, u32[]{:S(2)}) collective-permute-start(s32[3,3,6]{2,1,0:T(4,128)S(1)} %pad_add_fusion), channel_id=1, source_target_pairs={{0,1},{1,0},{2,3},{3,2},{4,5},{5,4},{6,7},{7,6},{8,9},{9,8},{10,11... | collective-permute-start | bytes 656 | tf_op jit(solution)/shard_map/ppermute | solution.py:641
  115.8 2.1 %shard_map.80.light = f32[4,512,128]{2,1,0:T(8,128)S(1)} custom-call(s32[3,6]{1,0:T(4,128)S(1)} %get-tuple-element.51.own, s32[2,3,6]{2,1,0:T(4,128)S(1)} %pad_add_fusion.1.refs_0_, s32[3,3,6]{2,1,0:T(4,128)S(1)} %collective-permute-done.6.refs_1_, f32[2,2,256,256]{3,2,1,0:T(8,128)S(1)} %copy-done.1), custom_call_target="tpu_custom_call" | custom-call | flops 10000000 | bytes 1000000 | tf_op jit(solution)/shard_map/pallas_call | solution.py:753
  117.9 2.0 %shard_map.82 = f32[2,512,512]{2,1,0:T(8,128)} custom-call(f32[2,512,512]{2,1,0:T(8,128)S(1)} %copy-done, f32[4,2,512,128]{3,2,1,0:T(8,128)S(1)} %get-tuple-element.35.mid, f32[4,512,128]{2,1,0:T(8,128)S(1)} %shard_map.80.light, f32[4,2,128,128]{3,2,1,0:T(8,128)S(1)} %collective-permute-done.8.from_straight, ...), custom_call_target="tpu_custom_call" | custom-call | tf_op jit(solution)/shard_map/pallas_call | solution.py:761
  120.0 1.0 shard_map.89
  (36 shorter events, 4.2 us)
Async XLA Ops:
  1.9 28.5 %copy-start.2 = (s32[1,1,2,6]{3,2,1,0:T(2,128)S(1)}, s32[1,1,2,6]{3,2,1,0:T(2,128)}, u32[]{:S(2)}) copy-start(s32[1,1,2,6]{3,2,1,0:T(2,128)} %offsets.3) | copy-start | bytes 148
  1.9 16.5 %collective-permute-start.1 = (f32[2,128,512]{2,1,0:T(8,128)S(1)}, f32[2,128,512]{2,1,0:T(8,128)S(1)}, u32[]{:S(2)}, u32[]{:S(2)}) collective-permute-start(f32[2,128,512]{2,1,0:T(8,128)S(1)} %get-tuple-element.26), channel_id=1, source_target_pairs={{2,4},{4,2},{6,8},{8,6},{10,12},{12,10},{14,16},{16,14},{18,20},{2... | collective-permute-start | bytes 1572872 | tf_op jit(solution)/shard_map/ppermute | solution.py:652
  6.9 22.8 %collective-permute-start = (f32[2,128,512]{2,1,0:T(8,128)S(1)}, f32[2,128,512]{2,1,0:T(8,128)S(1)}, u32[]{:S(2)}, u32[]{:S(2)}) collective-permute-start(f32[2,128,512]{2,1,0:T(8,128)S(1)} %shard_map.77), channel_id=1, source_target_pairs={{0,2},{2,0},{4,6},{6,4},{8,10},{10,8},{12,14},{14,12},{16,18},{18,... | collective-permute-start | bytes 1572872 | tf_op jit(solution)/shard_map/ppermute | solution.py:652
  7.4 23.0 %collective-permute-start.3 = (f32[2,512,128]{2,1,0:T(8,128)S(1)}, f32[2,512,128]{2,1,0:T(8,128)S(1)}, u32[]{:S(2)}, u32[]{:S(2)}) collective-permute-start(f32[2,512,128]{2,1,0:T(8,128)S(1)} %get-tuple-element.27), channel_id=1, source_target_pairs={{0,1},{1,0},{2,3},{3,2},{4,5},{5,4},{6,7},{7,6},{8,9},{9,8},{10,11... | collective-permute-start | bytes 1572872 | tf_op jit(solution)/shard_map/ppermute | solution.py:641
  29.8 7.6 %collective-permute-start.2 = (f32[2,2,128,128]{3,2,1,0:T(8,128)S(1)}, f32[2,2,128,128]{3,2,1,0:T(8,128)S(1)}, u32[]{:S(2)}, u32[]{:S(2)}) collective-permute-start(f32[2,2,128,128]{3,2,1,0:T(8,128)S(1)} %shard_map.79), channel_id=1, source_target_pairs={{0,1},{1,0},{2,3},{3,2},{4,5},{5,4},{6,7},{7,6},{8,9},{9,8},{10,11... | collective-permute-start | bytes 786440 | tf_op jit(solution)/shard_map/ppermute | solution.py:641
  42.0 31.0 %copy-start.1 = (f32[2,2,256,256]{3,2,1,0:T(8,128)S(1)}, f32[2,2,256,256]{3,2,1,0:T(8,128)}, u32[]{:S(2)}) copy-start(f32[2,2,256,256]{3,2,1,0:T(8,128)} %refs_2_.1) | copy-start | bytes 3145732
  42.1 2.2 %collective-permute-start.11 = (f32[5,128,256]{2,1,0:T(8,128)S(1)}, f32[5,128,256]{2,1,0:T(8,128)S(1)}, u32[]{:S(2)}, u32[]{:S(2)}) collective-permute-start(f32[5,128,256]{2,1,0:T(8,128)S(1)} %get-tuple-element.43), channel_id=1, source_target_pairs={{0,1},{1,0},{2,3},{3,2},{4,5},{5,4},{6,7},{7,6},{8,9},{9,8},{10,11... | collective-permute-start | bytes 1966088 | tf_op jit(solution)/shard_map/ppermute | solution.py:723
  42.1 37.9 %collective-permute-start.7 = (f32[2,768,128]{2,1,0:T(8,128)S(1)}, f32[2,768,128]{2,1,0:T(8,128)S(1)}, u32[]{:S(2)}, u32[]{:S(2)}) collective-permute-start(f32[2,768,128]{2,1,0:T(8,128)S(1)} %get-tuple-element.38), channel_id=1, source_target_pairs={{0,1},{1,0},{2,3},{3,2},{4,5},{5,4},{6,7},{7,6},{8,9},{9,8},{10,11... | collective-permute-start | bytes 2359304 | tf_op jit(solution)/shard_map/ppermute | solution.py:641
  44.3 16.5 %collective-permute-start.12 = (f32[5,32,256]{2,1,0:T(8,128)S(1)}, f32[5,32,256]{2,1,0:T(8,128)S(1)}, u32[]{:S(2)}, u32[]{:S(2)}) collective-permute-start(f32[5,32,256]{2,1,0:T(8,128)S(1)} %get-tuple-element.45), channel_id=1, source_target_pairs={{0,4},{2,6},{4,0},{6,2},{8,12},{10,14},{12,8},{14,10},{16,20},{18,... | collective-permute-start | bytes 491528 | tf_op jit(solution)/shard_map/ppermute | solution.py:723
  56.4 5.3 %collective-permute-start.13 = (f32[5,32,256]{2,1,0:T(8,128)S(1)}, f32[5,32,256]{2,1,0:T(8,128)S(1)}, u32[]{:S(2)}, u32[]{:S(2)}) collective-permute-start(f32[5,32,256]{2,1,0:T(8,128)S(1)} %get-tuple-element.46), channel_id=1, source_target_pairs={{0,8},{2,10},{4,12},{6,14},{8,0},{10,2},{12,4},{14,6},{16,24},{18,... | collective-permute-start | bytes 491528 | tf_op jit(solution)/shard_map/ppermute | solution.py:723
  56.4 8.9 %collective-permute-start.14 = (f32[5,32,256]{2,1,0:T(8,128)S(1)}, f32[5,32,256]{2,1,0:T(8,128)S(1)}, u32[]{:S(2)}, u32[]{:S(2)}) collective-permute-start(f32[5,32,256]{2,1,0:T(8,128)S(1)} %get-tuple-element.47), channel_id=1, source_target_pairs={{0,12},{2,14},{4,8},{6,10},{8,4},{10,6},{12,0},{14,2},{16,28},{18,... | collective-permute-start | bytes 491528 | tf_op jit(solution)/shard_map/ppermute | solution.py:723
  65.3 4.3 %collective-permute-start.15 = (f32[5,16,256]{2,1,0:T(8,128)S(1)}, f32[5,16,256]{2,1,0:T(8,128)S(1)}, u32[]{:S(2)}, u32[]{:S(2)}) collective-permute-start(f32[5,16,256]{2,1,0:T(8,128)S(1)} %get-tuple-element.49), channel_id=1, source_target_pairs={{0,16},{2,18},{4,20},{6,22},{8,24},{10,26},{12,28},{14,30},{16,0},... | collective-permute-start | bytes 245768 | tf_op jit(solution)/shard_map/ppermute | solution.py:723
  69.7 3.4 %collective-permute-start.16 = (f32[5,16,256]{2,1,0:T(8,128)S(1)}, f32[5,16,256]{2,1,0:T(8,128)S(1)}, u32[]{:S(2)}, u32[]{:S(2)}) collective-permute-start(f32[5,16,256]{2,1,0:T(8,128)S(1)} %shard_map.85.refs_0_), channel_id=1, source_target_pairs={{0,2},{2,0},{4,6},{6,4},{8,10},{10,8},{12,14},{14,12},{16,18},{18,... | collective-permute-start | bytes 245768 | tf_op jit(solution)/shard_map/ppermute | solution.py:727
  73.0 4.2 %collective-permute-start.17 = (f32[4,16,256]{2,1,0:T(8,128)S(1)}, f32[4,16,256]{2,1,0:T(8,128)S(1)}, u32[]{:S(2)}, u32[]{:S(2)}) collective-permute-start(f32[4,16,256]{2,1,0:T(8,128)S(1)} %shard_map.86.refs_0_), channel_id=1, source_target_pairs={{0,16},{2,18},{4,20},{6,22},{8,24},{10,26},{12,28},{14,30},{16,0},... | collective-permute-start | bytes 196616 | tf_op jit(solution)/shard_map/ppermute | solution.py:747
  77.3 3.9 %collective-permute-start.18 = (f32[4,32,256]{2,1,0:T(8,128)S(1)}, f32[4,32,256]{2,1,0:T(8,128)S(1)}, u32[]{:S(2)}, u32[]{:S(2)}) collective-permute-start(f32[4,32,256]{2,1,0:T(8,128)S(1)} %shard_map.87.refs_0_), channel_id=1, source_target_pairs={{0,4},{2,6},{4,0},{6,2},{8,12},{10,14},{12,8},{14,10},{16,20},{18,... | collective-permute-start | bytes 393224 | tf_op jit(solution)/shard_map/ppermute | solution.py:747
  78.4 3.8 %collective-permute-start.19 = (f32[4,32,256]{2,1,0:T(8,128)S(1)}, f32[4,32,256]{2,1,0:T(8,128)S(1)}, u32[]{:S(2)}, u32[]{:S(2)}) collective-permute-start(f32[4,32,256]{2,1,0:T(8,128)S(1)} %shard_map.87.refs_0_), channel_id=1, source_target_pairs={{0,8},{2,10},{4,12},{6,14},{8,0},{10,2},{12,4},{14,6},{16,24},{18,... | collective-permute-start | bytes 393224 | tf_op jit(solution)/shard_map/ppermute | solution.py:747
  78.5 5.2 %collective-permute-start.20 = (f32[4,32,256]{2,1,0:T(8,128)S(1)}, f32[4,32,256]{2,1,0:T(8,128)S(1)}, u32[]{:S(2)}, u32[]{:S(2)}) collective-permute-start(f32[4,32,256]{2,1,0:T(8,128)S(1)} %shard_map.87.refs_0_), channel_id=1, source_target_pairs={{0,12},{2,14},{4,8},{6,10},{8,4},{10,6},{12,0},{14,2},{16,28},{18,... | collective-permute-start | bytes 393224 | tf_op jit(solution)/shard_map/ppermute | solution.py:747
  80.0 37.9 %copy-start = (f32[2,512,512]{2,1,0:T(8,128)S(1)}, f32[2,512,512]{2,1,0:T(8,128)}, u32[]{:S(2)}) copy-start(f32[2,512,512]{2,1,0:T(8,128)} %tile.7) | copy-start | bytes 6291460
  80.1 37.8 %collective-permute-start.8 = (f32[4,2,128,128]{3,2,1,0:T(8,128)S(1)}, f32[4,2,128,128]{3,2,1,0:T(8,128)S(1)}, u32[]{:S(2)}, u32[]{:S(2)}) collective-permute-start(f32[4,2,128,128]{3,2,1,0:T(8,128)S(1)} %get-tuple-element.39), channel_id=1, source_target_pairs={{0,2},{2,0},{4,6},{6,4},{8,10},{10,8},{12,14},{14,12},{16,18},{18,... | collective-permute-start | bytes 1572872 | tf_op jit(solution)/shard_map/ppermute | solution.py:652
  83.8 36.2 %collective-permute-start.21 = (f32[4,128,256]{2,1,0:T(8,128)S(1)}, f32[4,128,256]{2,1,0:T(8,128)S(1)}, u32[]{:S(2)}, u32[]{:S(2)}) collective-permute-start(f32[4,128,256]{2,1,0:T(8,128)S(1)} %shard_map.88.refs_0_), channel_id=1, source_target_pairs={{0,1},{1,0},{2,3},{3,2},{4,5},{5,4},{6,7},{7,6},{8,9},{9,8},{10,11... | collective-permute-start | bytes 1572872 | tf_op jit(solution)/shard_map/ppermute | solution.py:747
  90.0 27.9 %collective-permute-start.10 = (f32[2,2,128,128]{3,2,1,0:T(8,128)S(1)}, f32[2,2,128,128]{3,2,1,0:T(8,128)S(1)}, u32[]{:S(2)}, u32[]{:S(2)}) collective-permute-start(f32[2,2,128,128]{3,2,1,0:T(8,128)S(1)} %get-tuple-element.41), channel_id=1, source_target_pairs={{2,4},{4,2},{6,8},{8,6},{10,12},{12,10},{14,16},{16,14},{18,20},{2... | collective-permute-start | bytes 786440 | tf_op jit(solution)/shard_map/ppermute | solution.py:652
  92.7 25.2 %collective-permute-start.9 = (f32[2,2,128,128]{3,2,1,0:T(8,128)S(1)}, f32[2,2,128,128]{3,2,1,0:T(8,128)S(1)}, u32[]{:S(2)}, u32[]{:S(2)}) collective-permute-start(f32[2,2,128,128]{3,2,1,0:T(8,128)S(1)} %get-tuple-element.40), channel_id=1, source_target_pairs={{2,4},{4,2},{6,8},{8,6},{10,12},{12,10},{14,16},{16,14},{18,20},{2... | collective-permute-start | bytes 786440 | tf_op jit(solution)/shard_map/ppermute | solution.py:652
  97.1 9.7 %collective-permute-start.4 = (s32[3,6]{1,0:T(4,128)S(1)}, s32[3,6]{1,0:T(4,128)S(1)}, u32[]{:S(2)}, u32[]{:S(2)}) collective-permute-start(s32[3,6]{1,0:T(4,128)S(1)} %get-tuple-element.51.own), channel_id=1, source_target_pairs={{0,2},{2,0},{4,6},{6,4},{8,10},{10,8},{12,14},{14,12},{16,18},{18,... | collective-permute-start | bytes 224 | tf_op jit(solution)/shard_map/ppermute | solution.py:652
  106.8 6.1 %collective-permute-start.5 = (s32[3,6]{1,0:T(4,128)S(1)}, s32[3,6]{1,0:T(4,128)S(1)}, u32[]{:S(2)}, u32[]{:S(2)}) collective-permute-start(s32[3,6]{1,0:T(4,128)S(1)} %get-tuple-element.51.own), channel_id=1, source_target_pairs={{2,4},{4,2},{6,8},{8,6},{10,12},{12,10},{14,16},{16,14},{18,20},{2... | collective-permute-start | bytes 224 | tf_op jit(solution)/shard_map/ppermute | solution.py:652
  112.9 2.9 %collective-permute-start.6 = (s32[3,3,6]{2,1,0:T(4,128)S(1)}, s32[3,3,6]{2,1,0:T(4,128)S(1)}, u32[]{:S(2)}, u32[]{:S(2)}) collective-permute-start(s32[3,3,6]{2,1,0:T(4,128)S(1)} %pad_add_fusion), channel_id=1, source_target_pairs={{0,1},{1,0},{2,3},{3,2},{4,5},{5,4},{6,7},{7,6},{8,9},{9,8},{10,11... | collective-permute-start | bytes 656 | tf_op jit(solution)/shard_map/ppermute | solution.py:641

commit v7 on v6

--- a/solution.py
+++ b/solution.py
@@ -654,12 +654,11 @@
 
 def stages_of(rows, cols):
     stages = [("col", (bit,)) for bit in range(cols.bit_length() - 1)]
-    bits = list(range(1, rows.bit_length() - 1))
-    if len(bits) > 1:
-        stages.append(("row", (bits[0], bits[1])))
+    bits = list(range(1, rows.bit_length() - 1)) + [0]
+    while bits:
+        stages.append(("row", tuple(bits[:2])))
         bits = bits[2:]
-    stages += [("row", (bit,)) for bit in bits]
-    return tuple(stages), ("row", (0,))
+    return tuple(stages)
 
 
 def step(object_field, probe_modes, scan_offsets, scan_counts, amplitudes):
@@ -671,7 +670,7 @@
     tiles = tile_cols // LANES
     sides = 1 if lax.axis_size("col") == 2 else 2
     geometry = (tile_rows, tile_cols, margin, sides)
-    stages, last = stages_of(lax.axis_size("row"), lax.axis_size("col"))
+    stages = stages_of(lax.axis_size("row"), lax.axis_size("col"))
     tables = in_hbm(jnp.asarray(dft_tables(edge)))
     tile_hbm, probe_hbm, amps_hbm = in_hbm(object_field), in_hbm(probe_modes), in_hbm(amplitudes)
 
@@ -723,9 +722,6 @@
             lax.ppermute(piece, axis, member_perm(axis, bits, member + 1))
             for member, piece in enumerate(pieces)
         ]
-    total = combine(last, parts, 1)[0]
-    parts = [total, lax.ppermute(total, last[0], member_perm(*last, 1))]
-
     received = swap_sides(side_outs)
     strip = shape(tiles, 2, margin, LANES)
     chunk = shape(tiles // 2, 2, margin, LANES)

time: 121 us -> 122 us (level)
  starting transfers between devices: 43.7 us -> 48.3 us
  waiting for transfers between devices: 56.3 us -> 52.6 us
    ppermute x5 -> x7, starting transfers between devices: 13.5 us -> 17 us  [step(): lax.ppermute(piece, axis, member_perm(axis, bits, member + 1))]
    ppermute x1 -> x0, waiting for transfers between devices: 3.28 us -> none  [step(): parts = [total, lax.ppermute(total, last[0], member_perm(*last, 1))]]
    ppermute x5 -> x7, waiting for transfers between devices: 5.19 us -> 8.13 us  [step(): lax.ppermute(shard, axis, member_perm(axis, bits, member))]
    ppermute x5 -> x7, waiting for transfers between devices: 13.5 us -> 11 us  [step(): lax.ppermute(piece, axis, member_perm(axis, bits, member + 1))]
    ppermute x5 -> x7, starting transfers between devices: 11.5 us -> 12.4 us  [step(): lax.ppermute(shard, axis, member_perm(axis, bits, member))]
  transfers between devices with their start and end apart: 22 -> 25, of which waited for: 15 -> 16; matrix products, arithmetic and copies ran while one was open for 0% -> 0% of each run, Pallas kernels for 10% -> 10%
where the time goes in v7:
time: 122 us
  waiting for transfers between devices  52.6 us (43%)
  starting transfers between devices  48.3 us (40%)
  Pallas kernels  19.5 us (16%)
  between operations  1.52 us (1%)
    ppermute x7, waiting for transfers between devices, swap_rows(): return lax.ppermute(value, 'row', pairs)  32.7 us
    ppermute x7, starting transfers between devices, step(): lax.ppermute(piece, axis, member_perm(axis, bits, member + 1))  17 us
    ppermute x7, starting transfers between devices, swap_rows(): return lax.ppermute(value, 'row', pairs)  14.5 us
    ppermute x7, starting transfers between devices, step(): lax.ppermute(shard, axis, member_perm(axis, bits, member))  12.4 us
    ppermute x7, waiting for transfers between devices, step(): lax.ppermute(piece, axis, member_perm(axis, bits, member + 1))  11 us
    ppermute x7, waiting for transfers between devices, step(): lax.ppermute(shard, axis, member_perm(axis, bits, member))  8.13 us
    pallas_call x1, Pallas kernels, run_interior(): pl.pallas_call(functools.partial(interior_kernel, geometry), out_shape=ou...  6.93 us
    pallas_call x1, Pallas kernels, run_boundary(): pl.pallas_call(functools.partial(boundary_kernel, geometry), out_shape=ou...  4.66 us
  transfers between devices with their start and end apart: 25, of which 16 were waited for; matrix products, arithmetic and copies ran while one was open for 0% of the time, Pallas kernels for 10%

profile of v7, /device:TPU:9, one launch (start us, length us, event | category | flops | bytes accessed | tf_op | source)
XLA Modules:
  0.0 121.9 jit_solution(12739066118138373569)
XLA Ops:
  0.6 1.2 %shard_map.78 = (f32[2,128,512]{2,1,0:T(8,128)S(1)}, f32[2,512,128]{2,1,0:T(8,128)S(1)}) custom-call(f32[2,512,512]{2,1,0:T(8,128)} %tile.7), custom_call_target="tpu_custom_call" | custom-call | tf_op jit(solution)/shard_map/pallas_call | solution.py:678
  1.9 4.0 %collective-permute-start.1 = (f32[2,128,512]{2,1,0:T(8,128)S(1)}, f32[2,128,512]{2,1,0:T(8,128)S(1)}, u32[]{:S(2)}, u32[]{:S(2)}) collective-permute-start(f32[2,128,512]{2,1,0:T(8,128)S(1)} %get-tuple-element.28), channel_id=1, source_target_pairs={{2,4},{4,2},{6,8},{8,6},{10,12},{12,10},{14,16},{16,14},{18,20},{2... | collective-permute-start | bytes 1572872 | tf_op jit(solution)/shard_map/ppermute | solution.py:652
  5.9 1.1 shard_map.77
  7.4 1.2 %collective-permute-start.3 = (f32[2,512,128]{2,1,0:T(8,128)S(1)}, f32[2,512,128]{2,1,0:T(8,128)S(1)}, u32[]{:S(2)}, u32[]{:S(2)}) collective-permute-start(f32[2,512,128]{2,1,0:T(8,128)S(1)} %get-tuple-element.29), channel_id=1, source_target_pairs={{0,1},{1,0},{2,3},{3,2},{4,5},{5,4},{6,7},{7,6},{8,9},{9,8},{10,11... | collective-permute-start | bytes 1572872 | tf_op jit(solution)/shard_map/ppermute | solution.py:641
  9.3 9.2 %collective-permute-done.1.diagonal = f32[2,128,512]{2,1,0:T(8,128)S(1)} collective-permute-done((f32[2,128,512]{2,1,0:T(8,128)S(1)}, f32[2,128,512]{2,1,0:T(8,128)S(1)}, u32[]{:S(2)}, u32[]{:S(2)}) %collective-permute-start.1) | collective-permute-done | bytes 524320 | tf_op jit(solution)/shard_map/ppermute | solution.py:652
  18.4 11.3 %collective-permute-done.straight = f32[2,128,512]{2,1,0:T(8,128)S(1)} collective-permute-done((f32[2,128,512]{2,1,0:T(8,128)S(1)}, f32[2,128,512]{2,1,0:T(8,128)S(1)}, u32[]{:S(2)}, u32[]{:S(2)}) %collective-permute-start) | collective-permute-done | bytes 524320 | tf_op jit(solution)/shard_map/ppermute | solution.py:652
  30.4 6.9 %slots_interior.1 = (f32[6,2,768,128]{3,2,1,0:T(8,128)S(1)}, f32[6,2,768,128]{3,2,1,0:T(8,128)S(1)}, f32[5,256,256]{2,1,0:T(8,128)S(1)}, f32[2,2,256,256]{3,2,1,...) custom-call(s32[1,1,2,6]{3,2,1,0:T(2,128)S(1)} %copy-done.2, ...), custom_call_target="tpu_custom_call" | custom-call | flops 10000000000 | bytes 20000000 | tf_op jit(solution)/shard_map/slots_interior/pallas_call | solution.py:408
  37.4 4.7 %slots_boundary.1 = (f32[6,2,768,128]{3,2,1,0:T(8,128)S(1)}, f32[6,2,768,128]{3,2,1,0:T(8,128)S(1)}, f32[5,256,256]{2,1,0:T(8,128)S(1)}, f32[4,2,512,128]{3,2,1,...) custom-call(s32[1,1,2,6]{3,2,1,0:T(2,128)S(1)} %copy-done.2, ...), custom_call_target="tpu_custom_call", output_to_operand_aliasing={{0}: (9, {}), {1}: (10, {}), {2}: (11, {})} | custom-call | flops 10000000000 | bytes 20000000 | tf_op jit(solution)/shard_map/slots_boundary/pallas_call | solution.py:433
  42.6 1.6 %collective-permute-done.11.refs_1_ = f32[5,128,256]{2,1,0:T(8,128)S(1)} collective-permute-done((f32[5,128,256]{2,1,0:T(8,128)S(1)}, f32[5,128,256]{2,1,0:T(8,128)S(1)}, u32[]{:S(2)}, u32[]{:S(2)}) %collective-permute-start.11) | collective-permute-done | bytes 655392 | tf_op jit(solution)/shard_map/ppermute | solution.py:722
  44.3 12.1 %collective-permute-start.12 = (f32[5,32,256]{2,1,0:T(8,128)S(1)}, f32[5,32,256]{2,1,0:T(8,128)S(1)}, u32[]{:S(2)}, u32[]{:S(2)}) collective-permute-start(f32[5,32,256]{2,1,0:T(8,128)S(1)} %get-tuple-element.47), channel_id=1, source_target_pairs={{0,4},{2,6},{4,0},{6,2},{8,12},{10,14},{12,8},{14,10},{16,20},{18,... | collective-permute-start | bytes 491528 | tf_op jit(solution)/shard_map/ppermute | solution.py:722
  56.4 1.3 %collective-permute-start.14 = (f32[5,32,256]{2,1,0:T(8,128)S(1)}, f32[5,32,256]{2,1,0:T(8,128)S(1)}, u32[]{:S(2)}, u32[]{:S(2)}) collective-permute-start(f32[5,32,256]{2,1,0:T(8,128)S(1)} %get-tuple-element.49), channel_id=1, source_target_pairs={{0,12},{2,14},{4,8},{6,10},{8,4},{10,6},{12,0},{14,2},{16,28},{18,... | collective-permute-start | bytes 491528 | tf_op jit(solution)/shard_map/ppermute | solution.py:722
  57.6 3.2 %collective-permute-done.12.refs_1_ = f32[5,32,256]{2,1,0:T(8,128)S(1)} collective-permute-done((f32[5,32,256]{2,1,0:T(8,128)S(1)}, f32[5,32,256]{2,1,0:T(8,128)S(1)}, u32[]{:S(2)}, u32[]{:S(2)}) %collective-permute-start.12) | collective-permute-done | bytes 163872 | tf_op jit(solution)/shard_map/ppermute | solution.py:722
  61.7 3.6 %collective-permute-done.14.refs_3_ = f32[5,32,256]{2,1,0:T(8,128)S(1)} collective-permute-done((f32[5,32,256]{2,1,0:T(8,128)S(1)}, f32[5,32,256]{2,1,0:T(8,128)S(1)}, u32[]{:S(2)}, u32[]{:S(2)}) %collective-permute-start.14) | collective-permute-done | bytes 163872 | tf_op jit(solution)/shard_map/ppermute | solution.py:722
  65.5 3.5 %collective-permute-start.17 = (f32[5,8,256]{2,1,0:T(8,128)S(1)}, f32[5,8,256]{2,1,0:T(8,128)S(1)}, u32[]{:S(2)}, u32[]{:S(2)}) collective-permute-start(f32[5,8,256]{2,1,0:T(8,128)S(1)} %get-tuple-element.53), channel_id=1, source_target_pairs={{0,18},{2,16},{4,22},{6,20},{8,26},{10,24},{12,30},{14,28},{16,2},... | collective-permute-start | bytes 122888 | tf_op jit(solution)/shard_map/ppermute | solution.py:722
  69.2 1.5 %collective-permute-done.17.refs_3_ = f32[5,8,256]{2,1,0:T(8,128)S(1)} collective-permute-done((f32[5,8,256]{2,1,0:T(8,128)S(1)}, f32[5,8,256]{2,1,0:T(8,128)S(1)}, u32[]{:S(2)}, u32[]{:S(2)}) %collective-permute-start.17) | collective-permute-done | bytes 40992 | tf_op jit(solution)/shard_map/ppermute | solution.py:722
  70.7 2.3 %collective-permute-start.18 = (f32[4,8,256]{2,1,0:T(8,128)S(1)}, f32[4,8,256]{2,1,0:T(8,128)S(1)}, u32[]{:S(2)}, u32[]{:S(2)}) collective-permute-start(f32[4,8,256]{2,1,0:T(8,128)S(1)} %shard_map.85.refs_0_), channel_id=1, source_target_pairs={{0,16},{2,18},{4,20},{6,22},{8,24},{10,26},{12,28},{14,30},{16,0},... | collective-permute-start | bytes 98312 | tf_op jit(solution)/shard_map/ppermute | solution.py:743
  73.0 1.5 %collective-permute-start.19 = (f32[4,8,256]{2,1,0:T(8,128)S(1)}, f32[4,8,256]{2,1,0:T(8,128)S(1)}, u32[]{:S(2)}, u32[]{:S(2)}) collective-permute-start(f32[4,8,256]{2,1,0:T(8,128)S(1)} %shard_map.85.refs_0_), channel_id=1, source_target_pairs={{0,2},{2,0},{4,6},{6,4},{8,10},{10,8},{12,14},{14,12},{16,18},{18,... | collective-permute-start | bytes 98312 | tf_op jit(solution)/shard_map/ppermute | solution.py:743
  74.4 1.3 %collective-permute-done.19.refs_2_ = f32[4,8,256]{2,1,0:T(8,128)S(1)} collective-permute-done((f32[4,8,256]{2,1,0:T(8,128)S(1)}, f32[4,8,256]{2,1,0:T(8,128)S(1)}, u32[]{:S(2)}, u32[]{:S(2)}) %collective-permute-start.19) | collective-permute-done | bytes 32800 | tf_op jit(solution)/shard_map/ppermute | solution.py:743
  75.7 3.3 %collective-permute-done.20.refs_3_ = f32[4,8,256]{2,1,0:T(8,128)S(1)} collective-permute-done((f32[4,8,256]{2,1,0:T(8,128)S(1)}, f32[4,8,256]{2,1,0:T(8,128)S(1)}, u32[]{:S(2)}, u32[]{:S(2)}) %collective-permute-start.20) | collective-permute-done | bytes 32800 | tf_op jit(solution)/shard_map/ppermute | solution.py:743
  79.0 1.2 %collective-permute-start.21 = (f32[4,32,256]{2,1,0:T(8,128)S(1)}, f32[4,32,256]{2,1,0:T(8,128)S(1)}, u32[]{:S(2)}, u32[]{:S(2)}) collective-permute-start(f32[4,32,256]{2,1,0:T(8,128)S(1)} %shard_map.86.refs_0_), channel_id=1, source_target_pairs={{0,4},{2,6},{4,0},{6,2},{8,12},{10,14},{12,8},{14,10},{16,20},{18,... | collective-permute-start | bytes 393224 | tf_op jit(solution)/shard_map/ppermute | solution.py:743
  80.3 1.5 %collective-permute-start.23 = (f32[4,32,256]{2,1,0:T(8,128)S(1)}, f32[4,32,256]{2,1,0:T(8,128)S(1)}, u32[]{:S(2)}, u32[]{:S(2)}) collective-permute-start(f32[4,32,256]{2,1,0:T(8,128)S(1)} %shard_map.86.refs_0_), channel_id=1, source_target_pairs={{0,12},{2,14},{4,8},{6,10},{8,4},{10,6},{12,0},{14,2},{16,28},{18,... | collective-permute-start | bytes 393224 | tf_op jit(solution)/shard_map/ppermute | solution.py:743
  82.0 1.1 collective-permute-done.21.refs_1_
  84.1 1.4 %collective-permute-done.23.refs_3_ = f32[4,32,256]{2,1,0:T(8,128)S(1)} collective-permute-done((f32[4,32,256]{2,1,0:T(8,128)S(1)}, f32[4,32,256]{2,1,0:T(8,128)S(1)}, u32[]{:S(2)}, u32[]{:S(2)}) %collective-permute-start.23) | collective-permute-done | bytes 131104 | tf_op jit(solution)/shard_map/ppermute | solution.py:743
  85.6 5.9 %collective-permute-start.24 = (f32[4,128,256]{2,1,0:T(8,128)S(1)}, f32[4,128,256]{2,1,0:T(8,128)S(1)}, u32[]{:S(2)}, u32[]{:S(2)}) collective-permute-start(f32[4,128,256]{2,1,0:T(8,128)S(1)} %shard_map.87.refs_0_), channel_id=1, source_target_pairs={{0,1},{1,0},{2,3},{3,2},{4,5},{5,4},{6,7},{7,6},{8,9},{9,8},{10,11... | collective-permute-start | bytes 1572872 | tf_op jit(solution)/shard_map/ppermute | solution.py:743
  91.5 2.6 %collective-permute-start.10 = (f32[2,2,128,128]{3,2,1,0:T(8,128)S(1)}, f32[2,2,128,128]{3,2,1,0:T(8,128)S(1)}, u32[]{:S(2)}, u32[]{:S(2)}) collective-permute-start(f32[2,2,128,128]{3,2,1,0:T(8,128)S(1)} %get-tuple-element.43), channel_id=1, source_target_pairs={{2,4},{4,2},{6,8},{8,6},{10,12},{12,10},{14,16},{16,14},{18,20},{2... | collective-permute-start | bytes 786440 | tf_op jit(solution)/shard_map/ppermute | solution.py:652
  94.1 4.4 %collective-permute-start.9 = (f32[2,2,128,128]{3,2,1,0:T(8,128)S(1)}, f32[2,2,128,128]{3,2,1,0:T(8,128)S(1)}, u32[]{:S(2)}, u32[]{:S(2)}) collective-permute-start(f32[2,2,128,128]{3,2,1,0:T(8,128)S(1)} %get-tuple-element.42), channel_id=1, source_target_pairs={{2,4},{4,2},{6,8},{8,6},{10,12},{12,10},{14,16},{16,14},{18,20},{2... | collective-permute-start | bytes 786440 | tf_op jit(solution)/shard_map/ppermute | solution.py:652
  98.7 9.0 %collective-permute-done.4 = s32[3,6]{1,0:T(4,128)S(1)} collective-permute-done((s32[3,6]{1,0:T(4,128)S(1)}, s32[3,6]{1,0:T(4,128)S(1)}, u32[]{:S(2)}, u32[]{:S(2)}) %collective-permute-start.4) | collective-permute-done | bytes 104 | tf_op jit(solution)/shard_map/ppermute | solution.py:652
  107.6 2.9 %collective-permute-start.5 = (s32[3,6]{1,0:T(4,128)S(1)}, s32[3,6]{1,0:T(4,128)S(1)}, u32[]{:S(2)}, u32[]{:S(2)}) collective-permute-start(s32[3,6]{1,0:T(4,128)S(1)} %get-tuple-element.55.own), channel_id=1, source_target_pairs={{2,4},{4,2},{6,8},{8,6},{10,12},{12,10},{14,16},{16,14},{18,20},{2... | collective-permute-start | bytes 224 | tf_op jit(solution)/shard_map/ppermute | solution.py:652
  110.5 3.2 %collective-permute-done.5 = s32[3,6]{1,0:T(4,128)S(1)} collective-permute-done((s32[3,6]{1,0:T(4,128)S(1)}, s32[3,6]{1,0:T(4,128)S(1)}, u32[]{:S(2)}, u32[]{:S(2)}) %collective-permute-start.5) | collective-permute-done | bytes 104 | tf_op jit(solution)/shard_map/ppermute | solution.py:652
  113.8 2.0 %collective-permute-start.6 = (s32[3,3,6]{2,1,0:T(4,128)S(1)}, s32[3,3,6]{2,1,0:T(4,128)S(1)}, u32[]{:S(2)}, u32[]{:S(2)}) collective-permute-start(s32[3,3,6]{2,1,0:T(4,128)S(1)} %pad_add_fusion), channel_id=1, source_target_pairs={{0,1},{1,0},{2,3},{3,2},{4,5},{5,4},{6,7},{7,6},{8,9},{9,8},{10,11... | collective-permute-start | bytes 656 | tf_op jit(solution)/shard_map/ppermute | solution.py:641
  116.6 2.1 %shard_map.80.light = f32[4,512,128]{2,1,0:T(8,128)S(1)} custom-call(s32[3,6]{1,0:T(4,128)S(1)} %get-tuple-element.55.own, s32[2,3,6]{2,1,0:T(4,128)S(1)} %pad_add_fusion.1.refs_0_, s32[3,3,6]{2,1,0:T(4,128)S(1)} %collective-permute-done.6.refs_1_, f32[2,2,256,256]{3,2,1,0:T(8,128)S(1)} %copy-done.1), custom_call_target="tpu_custom_call" | custom-call | flops 10000000 | bytes 1000000 | tf_op jit(solution)/shard_map/pallas_call | solution.py:749
  118.8 2.0 %shard_map.82 = f32[2,512,512]{2,1,0:T(8,128)} custom-call(f32[2,512,512]{2,1,0:T(8,128)S(1)} %copy-done, f32[4,2,512,128]{3,2,1,0:T(8,128)S(1)} %get-tuple-element.37.mid, f32[4,512,128]{2,1,0:T(8,128)S(1)} %shard_map.80.light, f32[4,2,128,128]{3,2,1,0:T(8,128)S(1)} %collective-permute-done.8.from_straight, ...), custom_call_target="tpu_custom_call" | custom-call | tf_op jit(solution)/shard_map/pallas_call | solution.py:757
  (41 shorter events, 6.4 us)
Async XLA Ops:
  1.9 28.5 %copy-start.2 = (s32[1,1,2,6]{3,2,1,0:T(2,128)S(1)}, s32[1,1,2,6]{3,2,1,0:T(2,128)}, u32[]{:S(2)}) copy-start(s32[1,1,2,6]{3,2,1,0:T(2,128)} %offsets.3) | copy-start | bytes 148
  1.9 16.5 %collective-permute-start.1 = (f32[2,128,512]{2,1,0:T(8,128)S(1)}, f32[2,128,512]{2,1,0:T(8,128)S(1)}, u32[]{:S(2)}, u32[]{:S(2)}) collective-permute-start(f32[2,128,512]{2,1,0:T(8,128)S(1)} %get-tuple-element.28), channel_id=1, source_target_pairs={{2,4},{4,2},{6,8},{8,6},{10,12},{12,10},{14,16},{16,14},{18,20},{2... | collective-permute-start | bytes 1572872 | tf_op jit(solution)/shard_map/ppermute | solution.py:652
  6.9 22.8 %collective-permute-start = (f32[2,128,512]{2,1,0:T(8,128)S(1)}, f32[2,128,512]{2,1,0:T(8,128)S(1)}, u32[]{:S(2)}, u32[]{:S(2)}) collective-permute-start(f32[2,128,512]{2,1,0:T(8,128)S(1)} %shard_map.77), channel_id=1, source_target_pairs={{0,2},{2,0},{4,6},{6,4},{8,10},{10,8},{12,14},{14,12},{16,18},{18,... | collective-permute-start | bytes 1572872 | tf_op jit(solution)/shard_map/ppermute | solution.py:652
  7.4 23.0 %collective-permute-start.3 = (f32[2,512,128]{2,1,0:T(8,128)S(1)}, f32[2,512,128]{2,1,0:T(8,128)S(1)}, u32[]{:S(2)}, u32[]{:S(2)}) collective-permute-start(f32[2,512,128]{2,1,0:T(8,128)S(1)} %get-tuple-element.29), channel_id=1, source_target_pairs={{0,1},{1,0},{2,3},{3,2},{4,5},{5,4},{6,7},{7,6},{8,9},{9,8},{10,11... | collective-permute-start | bytes 1572872 | tf_op jit(solution)/shard_map/ppermute | solution.py:641
  29.8 7.6 %collective-permute-start.2 = (f32[2,2,128,128]{3,2,1,0:T(8,128)S(1)}, f32[2,2,128,128]{3,2,1,0:T(8,128)S(1)}, u32[]{:S(2)}, u32[]{:S(2)}) collective-permute-start(f32[2,2,128,128]{3,2,1,0:T(8,128)S(1)} %shard_map.79), channel_id=1, source_target_pairs={{0,1},{1,0},{2,3},{3,2},{4,5},{5,4},{6,7},{7,6},{8,9},{9,8},{10,11... | collective-permute-start | bytes 786440 | tf_op jit(solution)/shard_map/ppermute | solution.py:641
  42.0 28.6 %copy-start.1 = (f32[2,2,256,256]{3,2,1,0:T(8,128)S(1)}, f32[2,2,256,256]{3,2,1,0:T(8,128)}, u32[]{:S(2)}) copy-start(f32[2,2,256,256]{3,2,1,0:T(8,128)} %refs_2_.1) | copy-start | bytes 3145732
  42.1 2.2 %collective-permute-start.11 = (f32[5,128,256]{2,1,0:T(8,128)S(1)}, f32[5,128,256]{2,1,0:T(8,128)S(1)}, u32[]{:S(2)}, u32[]{:S(2)}) collective-permute-start(f32[5,128,256]{2,1,0:T(8,128)S(1)} %get-tuple-element.45), channel_id=1, source_target_pairs={{0,1},{1,0},{2,3},{3,2},{4,5},{5,4},{6,7},{7,6},{8,9},{9,8},{10,11... | collective-permute-start | bytes 1966088 | tf_op jit(solution)/shard_map/ppermute | solution.py:722
  42.1 39.6 %collective-permute-start.7 = (f32[2,768,128]{2,1,0:T(8,128)S(1)}, f32[2,768,128]{2,1,0:T(8,128)S(1)}, u32[]{:S(2)}, u32[]{:S(2)}) collective-permute-start(f32[2,768,128]{2,1,0:T(8,128)S(1)} %get-tuple-element.40), channel_id=1, source_target_pairs={{0,1},{1,0},{2,3},{3,2},{4,5},{5,4},{6,7},{7,6},{8,9},{9,8},{10,11... | collective-permute-start | bytes 2359304 | tf_op jit(solution)/shard_map/ppermute | solution.py:641
  44.3 16.5 %collective-permute-start.12 = (f32[5,32,256]{2,1,0:T(8,128)S(1)}, f32[5,32,256]{2,1,0:T(8,128)S(1)}, u32[]{:S(2)}, u32[]{:S(2)}) collective-permute-start(f32[5,32,256]{2,1,0:T(8,128)S(1)} %get-tuple-element.47), channel_id=1, source_target_pairs={{0,4},{2,6},{4,0},{6,2},{8,12},{10,14},{12,8},{14,10},{16,20},{18,... | collective-permute-start | bytes 491528 | tf_op jit(solution)/shard_map/ppermute | solution.py:722
  56.4 5.3 %collective-permute-start.13 = (f32[5,32,256]{2,1,0:T(8,128)S(1)}, f32[5,32,256]{2,1,0:T(8,128)S(1)}, u32[]{:S(2)}, u32[]{:S(2)}) collective-permute-start(f32[5,32,256]{2,1,0:T(8,128)S(1)} %get-tuple-element.48), channel_id=1, source_target_pairs={{0,8},{2,10},{4,12},{6,14},{8,0},{10,2},{12,4},{14,6},{16,24},{18,... | collective-permute-start | bytes 491528 | tf_op jit(solution)/shard_map/ppermute | solution.py:722
  56.4 8.9 %collective-permute-start.14 = (f32[5,32,256]{2,1,0:T(8,128)S(1)}, f32[5,32,256]{2,1,0:T(8,128)S(1)}, u32[]{:S(2)}, u32[]{:S(2)}) collective-permute-start(f32[5,32,256]{2,1,0:T(8,128)S(1)} %get-tuple-element.49), channel_id=1, source_target_pairs={{0,12},{2,14},{4,8},{6,10},{8,4},{10,6},{12,0},{14,2},{16,28},{18,... | collective-permute-start | bytes 491528 | tf_op jit(solution)/shard_map/ppermute | solution.py:722
  65.3 3.8 %collective-permute-start.15 = (f32[5,8,256]{2,1,0:T(8,128)S(1)}, f32[5,8,256]{2,1,0:T(8,128)S(1)}, u32[]{:S(2)}, u32[]{:S(2)}) collective-permute-start(f32[5,8,256]{2,1,0:T(8,128)S(1)} %get-tuple-element.51), channel_id=1, source_target_pairs={{0,16},{2,18},{4,20},{6,22},{8,24},{10,26},{12,28},{14,30},{16,0},... | collective-permute-start | bytes 122888 | tf_op jit(solution)/shard_map/ppermute | solution.py:722
  65.4 3.8 %collective-permute-start.16 = (f32[5,8,256]{2,1,0:T(8,128)S(1)}, f32[5,8,256]{2,1,0:T(8,128)S(1)}, u32[]{:S(2)}, u32[]{:S(2)}) collective-permute-start(f32[5,8,256]{2,1,0:T(8,128)S(1)} %get-tuple-element.52), channel_id=1, source_target_pairs={{0,2},{2,0},{4,6},{6,4},{8,10},{10,8},{12,14},{14,12},{16,18},{18,... | collective-permute-start | bytes 122888 | tf_op jit(solution)/shard_map/ppermute | solution.py:722
  65.5 5.2 %collective-permute-start.17 = (f32[5,8,256]{2,1,0:T(8,128)S(1)}, f32[5,8,256]{2,1,0:T(8,128)S(1)}, u32[]{:S(2)}, u32[]{:S(2)}) collective-permute-start(f32[5,8,256]{2,1,0:T(8,128)S(1)} %get-tuple-element.53), channel_id=1, source_target_pairs={{0,18},{2,16},{4,22},{6,20},{8,26},{10,24},{12,30},{14,28},{16,2},... | collective-permute-start | bytes 122888 | tf_op jit(solution)/shard_map/ppermute | solution.py:722
  70.7 3.7 %collective-permute-start.18 = (f32[4,8,256]{2,1,0:T(8,128)S(1)}, f32[4,8,256]{2,1,0:T(8,128)S(1)}, u32[]{:S(2)}, u32[]{:S(2)}) collective-permute-start(f32[4,8,256]{2,1,0:T(8,128)S(1)} %shard_map.85.refs_0_), channel_id=1, source_target_pairs={{0,16},{2,18},{4,20},{6,22},{8,24},{10,26},{12,28},{14,30},{16,0},... | collective-permute-start | bytes 98312 | tf_op jit(solution)/shard_map/ppermute | solution.py:743
  73.0 2.8 %collective-permute-start.19 = (f32[4,8,256]{2,1,0:T(8,128)S(1)}, f32[4,8,256]{2,1,0:T(8,128)S(1)}, u32[]{:S(2)}, u32[]{:S(2)}) collective-permute-start(f32[4,8,256]{2,1,0:T(8,128)S(1)} %shard_map.85.refs_0_), channel_id=1, source_target_pairs={{0,2},{2,0},{4,6},{6,4},{8,10},{10,8},{12,14},{14,12},{16,18},{18,... | collective-permute-start | bytes 98312 | tf_op jit(solution)/shard_map/ppermute | solution.py:743
  74.4 4.6 %collective-permute-start.20 = (f32[4,8,256]{2,1,0:T(8,128)S(1)}, f32[4,8,256]{2,1,0:T(8,128)S(1)}, u32[]{:S(2)}, u32[]{:S(2)}) collective-permute-start(f32[4,8,256]{2,1,0:T(8,128)S(1)} %shard_map.85.refs_0_), channel_id=1, source_target_pairs={{0,18},{2,16},{4,22},{6,20},{8,26},{10,24},{12,30},{14,28},{16,2},... | collective-permute-start | bytes 98312 | tf_op jit(solution)/shard_map/ppermute | solution.py:743
  79.0 4.0 %collective-permute-start.21 = (f32[4,32,256]{2,1,0:T(8,128)S(1)}, f32[4,32,256]{2,1,0:T(8,128)S(1)}, u32[]{:S(2)}, u32[]{:S(2)}) collective-permute-start(f32[4,32,256]{2,1,0:T(8,128)S(1)} %shard_map.86.refs_0_), channel_id=1, source_target_pairs={{0,4},{2,6},{4,0},{6,2},{8,12},{10,14},{12,8},{14,10},{16,20},{18,... | collective-permute-start | bytes 393224 | tf_op jit(solution)/shard_map/ppermute | solution.py:743
  80.3 3.8 %collective-permute-start.22 = (f32[4,32,256]{2,1,0:T(8,128)S(1)}, f32[4,32,256]{2,1,0:T(8,128)S(1)}, u32[]{:S(2)}, u32[]{:S(2)}) collective-permute-start(f32[4,32,256]{2,1,0:T(8,128)S(1)} %shard_map.86.refs_0_), channel_id=1, source_target_pairs={{0,8},{2,10},{4,12},{6,14},{8,0},{10,2},{12,4},{14,6},{16,24},{18,... | collective-permute-start | bytes 393224 | tf_op jit(solution)/shard_map/ppermute | solution.py:743
  80.3 5.2 %collective-permute-start.23 = (f32[4,32,256]{2,1,0:T(8,128)S(1)}, f32[4,32,256]{2,1,0:T(8,128)S(1)}, u32[]{:S(2)}, u32[]{:S(2)}) collective-permute-start(f32[4,32,256]{2,1,0:T(8,128)S(1)} %shard_map.86.refs_0_), channel_id=1, source_target_pairs={{0,12},{2,14},{4,8},{6,10},{8,4},{10,6},{12,0},{14,2},{16,28},{18,... | collective-permute-start | bytes 393224 | tf_op jit(solution)/shard_map/ppermute | solution.py:743
  81.7 37.0 %copy-start = (f32[2,512,512]{2,1,0:T(8,128)S(1)}, f32[2,512,512]{2,1,0:T(8,128)}, u32[]{:S(2)}) copy-start(f32[2,512,512]{2,1,0:T(8,128)} %tile.7) | copy-start | bytes 6291460
  81.9 36.9 %collective-permute-start.8 = (f32[4,2,128,128]{3,2,1,0:T(8,128)S(1)}, f32[4,2,128,128]{3,2,1,0:T(8,128)S(1)}, u32[]{:S(2)}, u32[]{:S(2)}) collective-permute-start(f32[4,2,128,128]{3,2,1,0:T(8,128)S(1)} %get-tuple-element.41), channel_id=1, source_target_pairs={{0,2},{2,0},{4,6},{6,4},{8,10},{10,8},{12,14},{14,12},{16,18},{18,... | collective-permute-start | bytes 1572872 | tf_op jit(solution)/shard_map/ppermute | solution.py:652
  85.6 35.3 %collective-permute-start.24 = (f32[4,128,256]{2,1,0:T(8,128)S(1)}, f32[4,128,256]{2,1,0:T(8,128)S(1)}, u32[]{:S(2)}, u32[]{:S(2)}) collective-permute-start(f32[4,128,256]{2,1,0:T(8,128)S(1)} %shard_map.87.refs_0_), channel_id=1, source_target_pairs={{0,1},{1,0},{2,3},{3,2},{4,5},{5,4},{6,7},{7,6},{8,9},{9,8},{10,11... | collective-permute-start | bytes 1572872 | tf_op jit(solution)/shard_map/ppermute | solution.py:743
  91.5 27.2 %collective-permute-start.10 = (f32[2,2,128,128]{3,2,1,0:T(8,128)S(1)}, f32[2,2,128,128]{3,2,1,0:T(8,128)S(1)}, u32[]{:S(2)}, u32[]{:S(2)}) collective-permute-start(f32[2,2,128,128]{3,2,1,0:T(8,128)S(1)} %get-tuple-element.43), channel_id=1, source_target_pairs={{2,4},{4,2},{6,8},{8,6},{10,12},{12,10},{14,16},{16,14},{18,20},{2... | collective-permute-start | bytes 786440 | tf_op jit(solution)/shard_map/ppermute | solution.py:652
  94.1 24.6 %collective-permute-start.9 = (f32[2,2,128,128]{3,2,1,0:T(8,128)S(1)}, f32[2,2,128,128]{3,2,1,0:T(8,128)S(1)}, u32[]{:S(2)}, u32[]{:S(2)}) collective-permute-start(f32[2,2,128,128]{3,2,1,0:T(8,128)S(1)} %get-tuple-element.42), channel_id=1, source_target_pairs={{2,4},{4,2},{6,8},{8,6},{10,12},{12,10},{14,16},{16,14},{18,20},{2... | collective-permute-start | bytes 786440 | tf_op jit(solution)/shard_map/ppermute | solution.py:652
  98.6 9.0 %collective-permute-start.4 = (s32[3,6]{1,0:T(4,128)S(1)}, s32[3,6]{1,0:T(4,128)S(1)}, u32[]{:S(2)}, u32[]{:S(2)}) collective-permute-start(s32[3,6]{1,0:T(4,128)S(1)} %get-tuple-element.55.own), channel_id=1, source_target_pairs={{0,2},{2,0},{4,6},{6,4},{8,10},{10,8},{12,14},{14,12},{16,18},{18,... | collective-permute-start | bytes 224 | tf_op jit(solution)/shard_map/ppermute | solution.py:652
  107.6 6.1 %collective-permute-start.5 = (s32[3,6]{1,0:T(4,128)S(1)}, s32[3,6]{1,0:T(4,128)S(1)}, u32[]{:S(2)}, u32[]{:S(2)}) collective-permute-start(s32[3,6]{1,0:T(4,128)S(1)} %get-tuple-element.55.own), channel_id=1, source_target_pairs={{2,4},{4,2},{6,8},{8,6},{10,12},{12,10},{14,16},{16,14},{18,20},{2... | collective-permute-start | bytes 224 | tf_op jit(solution)/shard_map/ppermute | solution.py:652
  113.8 2.9 %collective-permute-start.6 = (s32[3,3,6]{2,1,0:T(4,128)S(1)}, s32[3,3,6]{2,1,0:T(4,128)S(1)}, u32[]{:S(2)}, u32[]{:S(2)}) collective-permute-start(s32[3,3,6]{2,1,0:T(4,128)S(1)} %pad_add_fusion), channel_id=1, source_target_pairs={{0,1},{1,0},{2,3},{3,2},{4,5},{5,4},{6,7},{7,6},{8,9},{9,8},{10,11... | collective-permute-start | bytes 656 | tf_op jit(solution)/shard_map/ppermute | solution.py:641

commit v8 on v7

--- a/solution.py
+++ b/solution.py
@@ -498,24 +498,11 @@
 
 def object_kernel(geometry, tile, mid, light, from_straight, from_low, from_high, *refs):
     frame = Frame(*geometry)
-    received, (out, old, stage, sems_in, sems_out) = refs[: frame.sides], refs[frame.sides :]
-    tiles = frame.tiles
-    loads = []
-    for t in range(tiles):
-        loads.append(
-            (
-                pltpu.make_async_copy(
-                    tile.at[:, :, pl.ds(t * LANES, LANES)], old.at[t], sems_in.at[2 * t]
-                ),
-                pltpu.make_async_copy(mid.at[t], stage.at[t], sems_in.at[2 * t + 1]),
-            )
-        )
-        for copy in loads[-1]:
-            copy.start()
+    received, (out, stage, sems) = refs[: frame.sides], refs[frame.sides :]
+    half = from_low.shape[0]
     copies = []
-    for t in range(tiles):
-        for copy in loads[t]:
-            copy.wait()
+    for t in range(frame.tiles):
+        stage[t] = mid[t]
         for side, value in enumerate(received):
 
             @pl.when(frame.side_target(side) == 1 + t)
@@ -523,14 +510,12 @@
                 stage[t] += value[:, frame.body, :]
 
         stage[t, :, frame.strip_rows(0), :] += from_straight[t]
-        half = from_low.shape[0]
         stage[t, :, frame.strip_rows(1), :] += from_low[t] if t < half else from_high[t - half]
         scale = 1.0 / (light[t] + 1.0)
+        cols = pl.ds(t * LANES, LANES)
         for c in range(2):
-            stage[t, c] = old[t, c] + stage[t, c] * scale
-        copy = pltpu.make_async_copy(
-            stage.at[t], out.at[:, :, pl.ds(t * LANES, LANES)], sems_out.at[t]
-        )
+            stage[t, c] = tile[c, :, cols] + stage[t, c] * scale
+        copy = pltpu.make_async_copy(stage.at[t], out.at[:, :, cols], sems.at[t])
         copy.start()
         copies.append(copy)
     for copy in copies:
@@ -757,12 +742,10 @@
     object_new = small_call(
         functools.partial(object_kernel, geometry),
         [shape(2, tile_rows, tile_cols)],
-        [IN_HBM, ANYWHERE] + [IN_VMEM] * (4 + sides),
+        [IN_VMEM] * (6 + sides),
         limit=8 * MIB,
         scratch=(
             VMEM((tiles, 2, tile_rows, LANES), F32),
-            VMEM((tiles, 2, tile_rows, LANES), F32),
-            pltpu.SemaphoreType.DMA((2 * tiles,)),
             pltpu.SemaphoreType.DMA((tiles,)),
         ),
         out_specs=[IN_HBM],

time: 122 us -> 122 us (level)
  no operation moved by 1% of the time
where the time goes in v8:
time: 122 us
  waiting for transfers between devices  52.6 us (43%)
  starting transfers between devices  48.3 us (40%)
  Pallas kernels  19.1 us (16%)
  between operations  1.52 us (1%)
    ppermute x7, waiting for transfers between devices, swap_rows(): return lax.ppermute(value, 'row', pairs)  32.7 us
    ppermute x7, starting transfers between devices, step(): lax.ppermute(piece, axis, member_perm(axis, bits, member + 1))  17 us
    ppermute x7, starting transfers between devices, swap_rows(): return lax.ppermute(value, 'row', pairs)  14.5 us
    ppermute x7, starting transfers between devices, step(): lax.ppermute(shard, axis, member_perm(axis, bits, member))  12.4 us
    ppermute x7, waiting for transfers between devices, step(): lax.ppermute(piece, axis, member_perm(axis, bits, member + 1))  11 us
    ppermute x7, waiting for transfers between devices, step(): lax.ppermute(shard, axis, member_perm(axis, bits, member))  8.13 us
    pallas_call x1, Pallas kernels, run_interior(): pl.pallas_call(functools.partial(interior_kernel, geometry), out_shape=ou...  6.93 us
    pallas_call x1, Pallas kernels, run_boundary(): pl.pallas_call(functools.partial(boundary_kernel, geometry), out_shape=ou...  4.66 us
  transfers between devices with their start and end apart: 25, of which 16 were waited for; matrix products, arithmetic and copies ran while one was open for 0% of the time, Pallas kernels for 10%

profile of v8, /device:TPU:9, one launch (start us, length us, event | category | flops | bytes accessed | tf_op | source)
XLA Modules:
  0.0 121.5 jit_solution(7491936512504753079)
XLA Ops:
  0.6 1.2 %shard_map.78 = (f32[2,128,512]{2,1,0:T(8,128)S(1)}, f32[2,512,128]{2,1,0:T(8,128)S(1)}) custom-call(f32[2,512,512]{2,1,0:T(8,128)} %tile.7), custom_call_target="tpu_custom_call" | custom-call | tf_op jit(solution)/shard_map/pallas_call | solution.py:663
  1.9 4.0 %collective-permute-start.1 = (f32[2,128,512]{2,1,0:T(8,128)S(1)}, f32[2,128,512]{2,1,0:T(8,128)S(1)}, u32[]{:S(2)}, u32[]{:S(2)}) collective-permute-start(f32[2,128,512]{2,1,0:T(8,128)S(1)} %get-tuple-element.28), channel_id=1, source_target_pairs={{2,4},{4,2},{6,8},{8,6},{10,12},{12,10},{14,16},{16,14},{18,20},{2... | collective-permute-start | bytes 1572872 | tf_op jit(solution)/shard_map/ppermute | solution.py:637
  5.9 1.1 shard_map.77
  7.4 1.2 %collective-permute-start.3 = (f32[2,512,128]{2,1,0:T(8,128)S(1)}, f32[2,512,128]{2,1,0:T(8,128)S(1)}, u32[]{:S(2)}, u32[]{:S(2)}) collective-permute-start(f32[2,512,128]{2,1,0:T(8,128)S(1)} %get-tuple-element.29), channel_id=1, source_target_pairs={{0,1},{1,0},{2,3},{3,2},{4,5},{5,4},{6,7},{7,6},{8,9},{9,8},{10,11... | collective-permute-start | bytes 1572872 | tf_op jit(solution)/shard_map/ppermute | solution.py:626
  9.3 9.2 %collective-permute-done.1.diagonal = f32[2,128,512]{2,1,0:T(8,128)S(1)} collective-permute-done((f32[2,128,512]{2,1,0:T(8,128)S(1)}, f32[2,128,512]{2,1,0:T(8,128)S(1)}, u32[]{:S(2)}, u32[]{:S(2)}) %collective-permute-start.1) | collective-permute-done | bytes 524320 | tf_op jit(solution)/shard_map/ppermute | solution.py:637
  18.4 11.3 %collective-permute-done.straight = f32[2,128,512]{2,1,0:T(8,128)S(1)} collective-permute-done((f32[2,128,512]{2,1,0:T(8,128)S(1)}, f32[2,128,512]{2,1,0:T(8,128)S(1)}, u32[]{:S(2)}, u32[]{:S(2)}) %collective-permute-start) | collective-permute-done | bytes 524320 | tf_op jit(solution)/shard_map/ppermute | solution.py:637
  30.4 6.9 %slots_interior.1 = (f32[6,2,768,128]{3,2,1,0:T(8,128)S(1)}, f32[6,2,768,128]{3,2,1,0:T(8,128)S(1)}, f32[5,256,256]{2,1,0:T(8,128)S(1)}, f32[2,2,256,256]{3,2,1,...) custom-call(s32[1,1,2,6]{3,2,1,0:T(2,128)S(1)} %copy-done.2, ...), custom_call_target="tpu_custom_call" | custom-call | flops 10000000000 | bytes 20000000 | tf_op jit(solution)/shard_map/slots_interior/pallas_call | solution.py:408
  37.4 4.7 %slots_boundary.1 = (f32[6,2,768,128]{3,2,1,0:T(8,128)S(1)}, f32[6,2,768,128]{3,2,1,0:T(8,128)S(1)}, f32[5,256,256]{2,1,0:T(8,128)S(1)}, f32[4,2,512,128]{3,2,1,...) custom-call(s32[1,1,2,6]{3,2,1,0:T(2,128)S(1)} %copy-done.2, ...), custom_call_target="tpu_custom_call", output_to_operand_aliasing={{0}: (9, {}), {1}: (10, {}), {2}: (11, {})} | custom-call | flops 10000000000 | bytes 20000000 | tf_op jit(solution)/shard_map/slots_boundary/pallas_call | solution.py:433
  42.6 1.6 %collective-permute-done.11.refs_1_ = f32[5,128,256]{2,1,0:T(8,128)S(1)} collective-permute-done((f32[5,128,256]{2,1,0:T(8,128)S(1)}, f32[5,128,256]{2,1,0:T(8,128)S(1)}, u32[]{:S(2)}, u32[]{:S(2)}) %collective-permute-start.11) | collective-permute-done | bytes 655392 | tf_op jit(solution)/shard_map/ppermute | solution.py:707
  44.3 12.1 %collective-permute-start.12 = (f32[5,32,256]{2,1,0:T(8,128)S(1)}, f32[5,32,256]{2,1,0:T(8,128)S(1)}, u32[]{:S(2)}, u32[]{:S(2)}) collective-permute-start(f32[5,32,256]{2,1,0:T(8,128)S(1)} %get-tuple-element.47), channel_id=1, source_target_pairs={{0,4},{2,6},{4,0},{6,2},{8,12},{10,14},{12,8},{14,10},{16,20},{18,... | collective-permute-start | bytes 491528 | tf_op jit(solution)/shard_map/ppermute | solution.py:707
  56.4 1.3 %collective-permute-start.14 = (f32[5,32,256]{2,1,0:T(8,128)S(1)}, f32[5,32,256]{2,1,0:T(8,128)S(1)}, u32[]{:S(2)}, u32[]{:S(2)}) collective-permute-start(f32[5,32,256]{2,1,0:T(8,128)S(1)} %get-tuple-element.49), channel_id=1, source_target_pairs={{0,12},{2,14},{4,8},{6,10},{8,4},{10,6},{12,0},{14,2},{16,28},{18,... | collective-permute-start | bytes 491528 | tf_op jit(solution)/shard_map/ppermute | solution.py:707
  57.6 3.2 %collective-permute-done.12.refs_1_ = f32[5,32,256]{2,1,0:T(8,128)S(1)} collective-permute-done((f32[5,32,256]{2,1,0:T(8,128)S(1)}, f32[5,32,256]{2,1,0:T(8,128)S(1)}, u32[]{:S(2)}, u32[]{:S(2)}) %collective-permute-start.12) | collective-permute-done | bytes 163872 | tf_op jit(solution)/shard_map/ppermute | solution.py:707
  61.7 3.6 %collective-permute-done.14.refs_3_ = f32[5,32,256]{2,1,0:T(8,128)S(1)} collective-permute-done((f32[5,32,256]{2,1,0:T(8,128)S(1)}, f32[5,32,256]{2,1,0:T(8,128)S(1)}, u32[]{:S(2)}, u32[]{:S(2)}) %collective-permute-start.14) | collective-permute-done | bytes 163872 | tf_op jit(solution)/shard_map/ppermute | solution.py:707
  65.5 3.5 %collective-permute-start.17 = (f32[5,8,256]{2,1,0:T(8,128)S(1)}, f32[5,8,256]{2,1,0:T(8,128)S(1)}, u32[]{:S(2)}, u32[]{:S(2)}) collective-permute-start(f32[5,8,256]{2,1,0:T(8,128)S(1)} %get-tuple-element.53), channel_id=1, source_target_pairs={{0,18},{2,16},{4,22},{6,20},{8,26},{10,24},{12,30},{14,28},{16,2},... | collective-permute-start | bytes 122888 | tf_op jit(solution)/shard_map/ppermute | solution.py:707
  69.2 1.5 %collective-permute-done.17.refs_3_ = f32[5,8,256]{2,1,0:T(8,128)S(1)} collective-permute-done((f32[5,8,256]{2,1,0:T(8,128)S(1)}, f32[5,8,256]{2,1,0:T(8,128)S(1)}, u32[]{:S(2)}, u32[]{:S(2)}) %collective-permute-start.17) | collective-permute-done | bytes 40992 | tf_op jit(solution)/shard_map/ppermute | solution.py:707
  70.7 2.3 %collective-permute-start.18 = (f32[4,8,256]{2,1,0:T(8,128)S(1)}, f32[4,8,256]{2,1,0:T(8,128)S(1)}, u32[]{:S(2)}, u32[]{:S(2)}) collective-permute-start(f32[4,8,256]{2,1,0:T(8,128)S(1)} %shard_map.85.refs_0_), channel_id=1, source_target_pairs={{0,16},{2,18},{4,20},{6,22},{8,24},{10,26},{12,28},{14,30},{16,0},... | collective-permute-start | bytes 98312 | tf_op jit(solution)/shard_map/ppermute | solution.py:728
  73.0 1.5 %collective-permute-start.19 = (f32[4,8,256]{2,1,0:T(8,128)S(1)}, f32[4,8,256]{2,1,0:T(8,128)S(1)}, u32[]{:S(2)}, u32[]{:S(2)}) collective-permute-start(f32[4,8,256]{2,1,0:T(8,128)S(1)} %shard_map.85.refs_0_), channel_id=1, source_target_pairs={{0,2},{2,0},{4,6},{6,4},{8,10},{10,8},{12,14},{14,12},{16,18},{18,... | collective-permute-start | bytes 98312 | tf_op jit(solution)/shard_map/ppermute | solution.py:728
  74.4 1.3 %collective-permute-done.19.refs_2_ = f32[4,8,256]{2,1,0:T(8,128)S(1)} collective-permute-done((f32[4,8,256]{2,1,0:T(8,128)S(1)}, f32[4,8,256]{2,1,0:T(8,128)S(1)}, u32[]{:S(2)}, u32[]{:S(2)}) %collective-permute-start.19) | collective-permute-done | bytes 32800 | tf_op jit(solution)/shard_map/ppermute | solution.py:728
  75.7 3.3 %collective-permute-done.20.refs_3_ = f32[4,8,256]{2,1,0:T(8,128)S(1)} collective-permute-done((f32[4,8,256]{2,1,0:T(8,128)S(1)}, f32[4,8,256]{2,1,0:T(8,128)S(1)}, u32[]{:S(2)}, u32[]{:S(2)}) %collective-permute-start.20) | collective-permute-done | bytes 32800 | tf_op jit(solution)/shard_map/ppermute | solution.py:728
  79.0 1.2 %collective-permute-start.21 = (f32[4,32,256]{2,1,0:T(8,128)S(1)}, f32[4,32,256]{2,1,0:T(8,128)S(1)}, u32[]{:S(2)}, u32[]{:S(2)}) collective-permute-start(f32[4,32,256]{2,1,0:T(8,128)S(1)} %shard_map.86.refs_0_), channel_id=1, source_target_pairs={{0,4},{2,6},{4,0},{6,2},{8,12},{10,14},{12,8},{14,10},{16,20},{18,... | collective-permute-start | bytes 393224 | tf_op jit(solution)/shard_map/ppermute | solution.py:728
  80.3 1.5 %collective-permute-start.23 = (f32[4,32,256]{2,1,0:T(8,128)S(1)}, f32[4,32,256]{2,1,0:T(8,128)S(1)}, u32[]{:S(2)}, u32[]{:S(2)}) collective-permute-start(f32[4,32,256]{2,1,0:T(8,128)S(1)} %shard_map.86.refs_0_), channel_id=1, source_target_pairs={{0,12},{2,14},{4,8},{6,10},{8,4},{10,6},{12,0},{14,2},{16,28},{18,... | collective-permute-start | bytes 393224 | tf_op jit(solution)/shard_map/ppermute | solution.py:728
  82.0 1.1 collective-permute-done.21.refs_1_
  84.1 1.4 %collective-permute-done.23.refs_3_ = f32[4,32,256]{2,1,0:T(8,128)S(1)} collective-permute-done((f32[4,32,256]{2,1,0:T(8,128)S(1)}, f32[4,32,256]{2,1,0:T(8,128)S(1)}, u32[]{:S(2)}, u32[]{:S(2)}) %collective-permute-start.23) | collective-permute-done | bytes 131104 | tf_op jit(solution)/shard_map/ppermute | solution.py:728
  85.6 5.9 %collective-permute-start.24 = (f32[4,128,256]{2,1,0:T(8,128)S(1)}, f32[4,128,256]{2,1,0:T(8,128)S(1)}, u32[]{:S(2)}, u32[]{:S(2)}) collective-permute-start(f32[4,128,256]{2,1,0:T(8,128)S(1)} %shard_map.87.refs_0_), channel_id=1, source_target_pairs={{0,1},{1,0},{2,3},{3,2},{4,5},{5,4},{6,7},{7,6},{8,9},{9,8},{10,11... | collective-permute-start | bytes 1572872 | tf_op jit(solution)/shard_map/ppermute | solution.py:728
  91.5 2.6 %collective-permute-start.10 = (f32[2,2,128,128]{3,2,1,0:T(8,128)S(1)}, f32[2,2,128,128]{3,2,1,0:T(8,128)S(1)}, u32[]{:S(2)}, u32[]{:S(2)}) collective-permute-start(f32[2,2,128,128]{3,2,1,0:T(8,128)S(1)} %get-tuple-element.43), channel_id=1, source_target_pairs={{2,4},{4,2},{6,8},{8,6},{10,12},{12,10},{14,16},{16,14},{18,20},{2... | collective-permute-start | bytes 786440 | tf_op jit(solution)/shard_map/ppermute | solution.py:637
  94.1 4.4 %collective-permute-start.9 = (f32[2,2,128,128]{3,2,1,0:T(8,128)S(1)}, f32[2,2,128,128]{3,2,1,0:T(8,128)S(1)}, u32[]{:S(2)}, u32[]{:S(2)}) collective-permute-start(f32[2,2,128,128]{3,2,1,0:T(8,128)S(1)} %get-tuple-element.42), channel_id=1, source_target_pairs={{2,4},{4,2},{6,8},{8,6},{10,12},{12,10},{14,16},{16,14},{18,20},{2... | collective-permute-start | bytes 786440 | tf_op jit(solution)/shard_map/ppermute | solution.py:637
  98.7 9.0 %collective-permute-done.4 = s32[3,6]{1,0:T(4,128)S(1)} collective-permute-done((s32[3,6]{1,0:T(4,128)S(1)}, s32[3,6]{1,0:T(4,128)S(1)}, u32[]{:S(2)}, u32[]{:S(2)}) %collective-permute-start.4) | collective-permute-done | bytes 104 | tf_op jit(solution)/shard_map/ppermute | solution.py:637
  107.6 2.9 %collective-permute-start.5 = (s32[3,6]{1,0:T(4,128)S(1)}, s32[3,6]{1,0:T(4,128)S(1)}, u32[]{:S(2)}, u32[]{:S(2)}) collective-permute-start(s32[3,6]{1,0:T(4,128)S(1)} %get-tuple-element.55.own), channel_id=1, source_target_pairs={{2,4},{4,2},{6,8},{8,6},{10,12},{12,10},{14,16},{16,14},{18,20},{2... | collective-permute-start | bytes 224 | tf_op jit(solution)/shard_map/ppermute | solution.py:637
  110.5 3.2 %collective-permute-done.5 = s32[3,6]{1,0:T(4,128)S(1)} collective-permute-done((s32[3,6]{1,0:T(4,128)S(1)}, s32[3,6]{1,0:T(4,128)S(1)}, u32[]{:S(2)}, u32[]{:S(2)}) %collective-permute-start.5) | collective-permute-done | bytes 104 | tf_op jit(solution)/shard_map/ppermute | solution.py:637
  113.8 2.0 %collective-permute-start.6 = (s32[3,3,6]{2,1,0:T(4,128)S(1)}, s32[3,3,6]{2,1,0:T(4,128)S(1)}, u32[]{:S(2)}, u32[]{:S(2)}) collective-permute-start(s32[3,3,6]{2,1,0:T(4,128)S(1)} %pad_add_fusion), channel_id=1, source_target_pairs={{0,1},{1,0},{2,3},{3,2},{4,5},{5,4},{6,7},{7,6},{8,9},{9,8},{10,11... | collective-permute-start | bytes 656 | tf_op jit(solution)/shard_map/ppermute | solution.py:626
  116.6 2.1 %shard_map.80.light = f32[4,512,128]{2,1,0:T(8,128)S(1)} custom-call(s32[3,6]{1,0:T(4,128)S(1)} %get-tuple-element.55.own, s32[2,3,6]{2,1,0:T(4,128)S(1)} %pad_add_fusion.1.refs_0_, s32[3,3,6]{2,1,0:T(4,128)S(1)} %collective-permute-done.6.refs_1_, f32[2,2,256,256]{3,2,1,0:T(8,128)S(1)} %copy-done.1), custom_call_target="tpu_custom_call" | custom-call | flops 10000000 | bytes 1000000 | tf_op jit(solution)/shard_map/pallas_call | solution.py:734
  118.8 1.7 %shard_map.82 = f32[2,512,512]{2,1,0:T(8,128)} custom-call(f32[2,512,512]{2,1,0:T(8,128)S(1)} %copy-done, f32[4,2,512,128]{3,2,1,0:T(8,128)S(1)} %get-tuple-element.37.mid, f32[4,512,128]{2,1,0:T(8,128)S(1)} %shard_map.80.light, f32[4,2,128,128]{3,2,1,0:T(8,128)S(1)} %collective-permute-done.8.from_straight, ...), custom_call_target="tpu_custom_call" | custom-call | tf_op jit(solution)/shard_map/pallas_call | solution.py:742
  (41 shorter events, 6.4 us)
Async XLA Ops:
  1.9 28.5 %copy-start.2 = (s32[1,1,2,6]{3,2,1,0:T(2,128)S(1)}, s32[1,1,2,6]{3,2,1,0:T(2,128)}, u32[]{:S(2)}) copy-start(s32[1,1,2,6]{3,2,1,0:T(2,128)} %offsets.3) | copy-start | bytes 148
  1.9 16.5 %collective-permute-start.1 = (f32[2,128,512]{2,1,0:T(8,128)S(1)}, f32[2,128,512]{2,1,0:T(8,128)S(1)}, u32[]{:S(2)}, u32[]{:S(2)}) collective-permute-start(f32[2,128,512]{2,1,0:T(8,128)S(1)} %get-tuple-element.28), channel_id=1, source_target_pairs={{2,4},{4,2},{6,8},{8,6},{10,12},{12,10},{14,16},{16,14},{18,20},{2... | collective-permute-start | bytes 1572872 | tf_op jit(solution)/shard_map/ppermute | solution.py:637
  6.9 22.8 %collective-permute-start = (f32[2,128,512]{2,1,0:T(8,128)S(1)}, f32[2,128,512]{2,1,0:T(8,128)S(1)}, u32[]{:S(2)}, u32[]{:S(2)}) collective-permute-start(f32[2,128,512]{2,1,0:T(8,128)S(1)} %shard_map.77), channel_id=1, source_target_pairs={{0,2},{2,0},{4,6},{6,4},{8,10},{10,8},{12,14},{14,12},{16,18},{18,... | collective-permute-start | bytes 1572872 | tf_op jit(solution)/shard_map/ppermute | solution.py:637
  7.4 23.0 %collective-permute-start.3 = (f32[2,512,128]{2,1,0:T(8,128)S(1)}, f32[2,512,128]{2,1,0:T(8,128)S(1)}, u32[]{:S(2)}, u32[]{:S(2)}) collective-permute-start(f32[2,512,128]{2,1,0:T(8,128)S(1)} %get-tuple-element.29), channel_id=1, source_target_pairs={{0,1},{1,0},{2,3},{3,2},{4,5},{5,4},{6,7},{7,6},{8,9},{9,8},{10,11... | collective-permute-start | bytes 1572872 | tf_op jit(solution)/shard_map/ppermute | solution.py:626
  29.8 7.6 %collective-permute-start.2 = (f32[2,2,128,128]{3,2,1,0:T(8,128)S(1)}, f32[2,2,128,128]{3,2,1,0:T(8,128)S(1)}, u32[]{:S(2)}, u32[]{:S(2)}) collective-permute-start(f32[2,2,128,128]{3,2,1,0:T(8,128)S(1)} %shard_map.79), channel_id=1, source_target_pairs={{0,1},{1,0},{2,3},{3,2},{4,5},{5,4},{6,7},{7,6},{8,9},{9,8},{10,11... | collective-permute-start | bytes 786440 | tf_op jit(solution)/shard_map/ppermute | solution.py:626
  42.0 28.6 %copy-start.1 = (f32[2,2,256,256]{3,2,1,0:T(8,128)S(1)}, f32[2,2,256,256]{3,2,1,0:T(8,128)}, u32[]{:S(2)}) copy-start(f32[2,2,256,256]{3,2,1,0:T(8,128)} %refs_2_.1) | copy-start | bytes 3145732
  42.1 2.2 %collective-permute-start.11 = (f32[5,128,256]{2,1,0:T(8,128)S(1)}, f32[5,128,256]{2,1,0:T(8,128)S(1)}, u32[]{:S(2)}, u32[]{:S(2)}) collective-permute-start(f32[5,128,256]{2,1,0:T(8,128)S(1)} %get-tuple-element.45), channel_id=1, source_target_pairs={{0,1},{1,0},{2,3},{3,2},{4,5},{5,4},{6,7},{7,6},{8,9},{9,8},{10,11... | collective-permute-start | bytes 1966088 | tf_op jit(solution)/shard_map/ppermute | solution.py:707
  42.1 39.6 %collective-permute-start.7 = (f32[2,768,128]{2,1,0:T(8,128)S(1)}, f32[2,768,128]{2,1,0:T(8,128)S(1)}, u32[]{:S(2)}, u32[]{:S(2)}) collective-permute-start(f32[2,768,128]{2,1,0:T(8,128)S(1)} %get-tuple-element.40), channel_id=1, source_target_pairs={{0,1},{1,0},{2,3},{3,2},{4,5},{5,4},{6,7},{7,6},{8,9},{9,8},{10,11... | collective-permute-start | bytes 2359304 | tf_op jit(solution)/shard_map/ppermute | solution.py:626
  44.3 16.5 %collective-permute-start.12 = (f32[5,32,256]{2,1,0:T(8,128)S(1)}, f32[5,32,256]{2,1,0:T(8,128)S(1)}, u32[]{:S(2)}, u32[]{:S(2)}) collective-permute-start(f32[5,32,256]{2,1,0:T(8,128)S(1)} %get-tuple-element.47), channel_id=1, source_target_pairs={{0,4},{2,6},{4,0},{6,2},{8,12},{10,14},{12,8},{14,10},{16,20},{18,... | collective-permute-start | bytes 491528 | tf_op jit(solution)/shard_map/ppermute | solution.py:707
  56.4 5.3 %collective-permute-start.13 = (f32[5,32,256]{2,1,0:T(8,128)S(1)}, f32[5,32,256]{2,1,0:T(8,128)S(1)}, u32[]{:S(2)}, u32[]{:S(2)}) collective-permute-start(f32[5,32,256]{2,1,0:T(8,128)S(1)} %get-tuple-element.48), channel_id=1, source_target_pairs={{0,8},{2,10},{4,12},{6,14},{8,0},{10,2},{12,4},{14,6},{16,24},{18,... | collective-permute-start | bytes 491528 | tf_op jit(solution)/shard_map/ppermute | solution.py:707
  56.4 8.9 %collective-permute-start.14 = (f32[5,32,256]{2,1,0:T(8,128)S(1)}, f32[5,32,256]{2,1,0:T(8,128)S(1)}, u32[]{:S(2)}, u32[]{:S(2)}) collective-permute-start(f32[5,32,256]{2,1,0:T(8,128)S(1)} %get-tuple-element.49), channel_id=1, source_target_pairs={{0,12},{2,14},{4,8},{6,10},{8,4},{10,6},{12,0},{14,2},{16,28},{18,... | collective-permute-start | bytes 491528 | tf_op jit(solution)/shard_map/ppermute | solution.py:707
  65.3 3.8 %collective-permute-start.15 = (f32[5,8,256]{2,1,0:T(8,128)S(1)}, f32[5,8,256]{2,1,0:T(8,128)S(1)}, u32[]{:S(2)}, u32[]{:S(2)}) collective-permute-start(f32[5,8,256]{2,1,0:T(8,128)S(1)} %get-tuple-element.51), channel_id=1, source_target_pairs={{0,16},{2,18},{4,20},{6,22},{8,24},{10,26},{12,28},{14,30},{16,0},... | collective-permute-start | bytes 122888 | tf_op jit(solution)/shard_map/ppermute | solution.py:707
  65.4 3.8 %collective-permute-start.16 = (f32[5,8,256]{2,1,0:T(8,128)S(1)}, f32[5,8,256]{2,1,0:T(8,128)S(1)}, u32[]{:S(2)}, u32[]{:S(2)}) collective-permute-start(f32[5,8,256]{2,1,0:T(8,128)S(1)} %get-tuple-element.52), channel_id=1, source_target_pairs={{0,2},{2,0},{4,6},{6,4},{8,10},{10,8},{12,14},{14,12},{16,18},{18,... | collective-permute-start | bytes 122888 | tf_op jit(solution)/shard_map/ppermute | solution.py:707
  65.5 5.2 %collective-permute-start.17 = (f32[5,8,256]{2,1,0:T(8,128)S(1)}, f32[5,8,256]{2,1,0:T(8,128)S(1)}, u32[]{:S(2)}, u32[]{:S(2)}) collective-permute-start(f32[5,8,256]{2,1,0:T(8,128)S(1)} %get-tuple-element.53), channel_id=1, source_target_pairs={{0,18},{2,16},{4,22},{6,20},{8,26},{10,24},{12,30},{14,28},{16,2},... | collective-permute-start | bytes 122888 | tf_op jit(solution)/shard_map/ppermute | solution.py:707
  70.7 3.7 %collective-permute-start.18 = (f32[4,8,256]{2,1,0:T(8,128)S(1)}, f32[4,8,256]{2,1,0:T(8,128)S(1)}, u32[]{:S(2)}, u32[]{:S(2)}) collective-permute-start(f32[4,8,256]{2,1,0:T(8,128)S(1)} %shard_map.85.refs_0_), channel_id=1, source_target_pairs={{0,16},{2,18},{4,20},{6,22},{8,24},{10,26},{12,28},{14,30},{16,0},... | collective-permute-start | bytes 98312 | tf_op jit(solution)/shard_map/ppermute | solution.py:728
  73.0 2.8 %collective-permute-start.19 = (f32[4,8,256]{2,1,0:T(8,128)S(1)}, f32[4,8,256]{2,1,0:T(8,128)S(1)}, u32[]{:S(2)}, u32[]{:S(2)}) collective-permute-start(f32[4,8,256]{2,1,0:T(8,128)S(1)} %shard_map.85.refs_0_), channel_id=1, source_target_pairs={{0,2},{2,0},{4,6},{6,4},{8,10},{10,8},{12,14},{14,12},{16,18},{18,... | collective-permute-start | bytes 98312 | tf_op jit(solution)/shard_map/ppermute | solution.py:728
  74.4 4.6 %collective-permute-start.20 = (f32[4,8,256]{2,1,0:T(8,128)S(1)}, f32[4,8,256]{2,1,0:T(8,128)S(1)}, u32[]{:S(2)}, u32[]{:S(2)}) collective-permute-start(f32[4,8,256]{2,1,0:T(8,128)S(1)} %shard_map.85.refs_0_), channel_id=1, source_target_pairs={{0,18},{2,16},{4,22},{6,20},{8,26},{10,24},{12,30},{14,28},{16,2},... | collective-permute-start | bytes 98312 | tf_op jit(solution)/shard_map/ppermute | solution.py:728
  79.0 4.0 %collective-permute-start.21 = (f32[4,32,256]{2,1,0:T(8,128)S(1)}, f32[4,32,256]{2,1,0:T(8,128)S(1)}, u32[]{:S(2)}, u32[]{:S(2)}) collective-permute-start(f32[4,32,256]{2,1,0:T(8,128)S(1)} %shard_map.86.refs_0_), channel_id=1, source_target_pairs={{0,4},{2,6},{4,0},{6,2},{8,12},{10,14},{12,8},{14,10},{16,20},{18,... | collective-permute-start | bytes 393224 | tf_op jit(solution)/shard_map/ppermute | solution.py:728
  80.3 3.8 %collective-permute-start.22 = (f32[4,32,256]{2,1,0:T(8,128)S(1)}, f32[4,32,256]{2,1,0:T(8,128)S(1)}, u32[]{:S(2)}, u32[]{:S(2)}) collective-permute-start(f32[4,32,256]{2,1,0:T(8,128)S(1)} %shard_map.86.refs_0_), channel_id=1, source_target_pairs={{0,8},{2,10},{4,12},{6,14},{8,0},{10,2},{12,4},{14,6},{16,24},{18,... | collective-permute-start | bytes 393224 | tf_op jit(solution)/shard_map/ppermute | solution.py:728
  80.3 5.2 %collective-permute-start.23 = (f32[4,32,256]{2,1,0:T(8,128)S(1)}, f32[4,32,256]{2,1,0:T(8,128)S(1)}, u32[]{:S(2)}, u32[]{:S(2)}) collective-permute-start(f32[4,32,256]{2,1,0:T(8,128)S(1)} %shard_map.86.refs_0_), channel_id=1, source_target_pairs={{0,12},{2,14},{4,8},{6,10},{8,4},{10,6},{12,0},{14,2},{16,28},{18,... | collective-permute-start | bytes 393224 | tf_op jit(solution)/shard_map/ppermute | solution.py:728
  81.7 37.0 %copy-start = (f32[2,512,512]{2,1,0:T(8,128)S(1)}, f32[2,512,512]{2,1,0:T(8,128)}, u32[]{:S(2)}) copy-start(f32[2,512,512]{2,1,0:T(8,128)} %tile.7) | copy-start | bytes 6291460
  81.9 36.9 %collective-permute-start.8 = (f32[4,2,128,128]{3,2,1,0:T(8,128)S(1)}, f32[4,2,128,128]{3,2,1,0:T(8,128)S(1)}, u32[]{:S(2)}, u32[]{:S(2)}) collective-permute-start(f32[4,2,128,128]{3,2,1,0:T(8,128)S(1)} %get-tuple-element.41), channel_id=1, source_target_pairs={{0,2},{2,0},{4,6},{6,4},{8,10},{10,8},{12,14},{14,12},{16,18},{18,... | collective-permute-start | bytes 1572872 | tf_op jit(solution)/shard_map/ppermute | solution.py:637
  85.6 34.9 %collective-permute-start.24 = (f32[4,128,256]{2,1,0:T(8,128)S(1)}, f32[4,128,256]{2,1,0:T(8,128)S(1)}, u32[]{:S(2)}, u32[]{:S(2)}) collective-permute-start(f32[4,128,256]{2,1,0:T(8,128)S(1)} %shard_map.87.refs_0_), channel_id=1, source_target_pairs={{0,1},{1,0},{2,3},{3,2},{4,5},{5,4},{6,7},{7,6},{8,9},{9,8},{10,11... | collective-permute-start | bytes 1572872 | tf_op jit(solution)/shard_map/ppermute | solution.py:728
  91.5 27.2 %collective-permute-start.10 = (f32[2,2,128,128]{3,2,1,0:T(8,128)S(1)}, f32[2,2,128,128]{3,2,1,0:T(8,128)S(1)}, u32[]{:S(2)}, u32[]{:S(2)}) collective-permute-start(f32[2,2,128,128]{3,2,1,0:T(8,128)S(1)} %get-tuple-element.43), channel_id=1, source_target_pairs={{2,4},{4,2},{6,8},{8,6},{10,12},{12,10},{14,16},{16,14},{18,20},{2... | collective-permute-start | bytes 786440 | tf_op jit(solution)/shard_map/ppermute | solution.py:637
  94.1 24.6 %collective-permute-start.9 = (f32[2,2,128,128]{3,2,1,0:T(8,128)S(1)}, f32[2,2,128,128]{3,2,1,0:T(8,128)S(1)}, u32[]{:S(2)}, u32[]{:S(2)}) collective-permute-start(f32[2,2,128,128]{3,2,1,0:T(8,128)S(1)} %get-tuple-element.42), channel_id=1, source_target_pairs={{2,4},{4,2},{6,8},{8,6},{10,12},{12,10},{14,16},{16,14},{18,20},{2... | collective-permute-start | bytes 786440 | tf_op jit(solution)/shard_map/ppermute | solution.py:637
  98.6 9.0 %collective-permute-start.4 = (s32[3,6]{1,0:T(4,128)S(1)}, s32[3,6]{1,0:T(4,128)S(1)}, u32[]{:S(2)}, u32[]{:S(2)}) collective-permute-start(s32[3,6]{1,0:T(4,128)S(1)} %get-tuple-element.55.own), channel_id=1, source_target_pairs={{0,2},{2,0},{4,6},{6,4},{8,10},{10,8},{12,14},{14,12},{16,18},{18,... | collective-permute-start | bytes 224 | tf_op jit(solution)/shard_map/ppermute | solution.py:637
  107.6 6.1 %collective-permute-start.5 = (s32[3,6]{1,0:T(4,128)S(1)}, s32[3,6]{1,0:T(4,128)S(1)}, u32[]{:S(2)}, u32[]{:S(2)}) collective-permute-start(s32[3,6]{1,0:T(4,128)S(1)} %get-tuple-element.55.own), channel_id=1, source_target_pairs={{2,4},{4,2},{6,8},{8,6},{10,12},{12,10},{14,16},{16,14},{18,20},{2... | collective-permute-start | bytes 224 | tf_op jit(solution)/shard_map/ppermute | solution.py:637
  113.8 2.9 %collective-permute-start.6 = (s32[3,3,6]{2,1,0:T(4,128)S(1)}, s32[3,3,6]{2,1,0:T(4,128)S(1)}, u32[]{:S(2)}, u32[]{:S(2)}) collective-permute-start(s32[3,3,6]{2,1,0:T(4,128)S(1)} %pad_add_fusion), channel_id=1, source_target_pairs={{0,1},{1,0},{2,3},{3,2},{4,5},{5,4},{6,7},{7,6},{8,9},{9,8},{10,11... | collective-permute-start | bytes 656 | tf_op jit(solution)/shard_map/ppermute | solution.py:626
